TPU v7x, 256 devices: a whole 4x4x8 slice. The times are simulated.
256 devices in a mesh: gx: 4 (over x), gy: 8 (over y, core), gz: 8 (over z).
Axes of the slice: x: 4, y: 4, z: 8, core: 2. Of those that a mesh axis runs over, the one named last changes fastest.
Arguments:
- right_side: float32 [64, 256, 1024], P('gx', 'gy', 'gz'), may hold values from -8 to 8
- diagonal: float32 [64, 256, 1024], P('gx', 'gy', 'gz'), may hold values from 0.16 to 6.1
Outputs:
- solution_field: float32 [64, 256, 1024], P('gx', 'gy', 'gz')
- residual: float32 [64, 256, 1024], P('gx', 'gy', 'gz')
All inputs are finite; a program needn't handle non-finite values.
Results may differ from a plain program's by a relative error of at most 0.0003.
Values sent between devices are 32-bit elements; how exact they have to be, the bound alone decides.
No kernel may reach another device: no remote copies, remote signals or barrier semaphores. Data moves between devices by JAX's collectives and lax.ppermute only.
A program may use at most 128 MiB of HBM per device.

v0:
```python
import jax
import jax.numpy as jnp
from jax import lax
from jax.sharding import Mesh
from jax.sharding import PartitionSpec as P

ITERS = 2
GX_GY_GZ = ("gx", "gy_0", "gy_1", "gz")
GY = ("gy_0", "gy_1")


def extended(cells, sides, width):
    for axis, dim in sides:
        count = lax.axis_size(axis)
        ends = count - 1
        head = lax.slice_in_dim(cells, 0, width, axis=dim)
        tail = lax.slice_in_dim(cells, cells.shape[dim] - width, cells.shape[dim], axis=dim)
        cells = jnp.concatenate(
            [
                lax.ppermute(tail, axis, [(i, (i + 1) % count) for i in range(ends)]),
                cells,
                lax.ppermute(head, axis, [((i + 1) % count, i) for i in range(ends)]),
            ],
            axis=dim,
        )
    return cells


def in_order(tiles, dim):
    tiles = jnp.moveaxis(tiles, 0, dim)
    shape = tiles.shape
    return tiles.reshape(*shape[:dim], shape[dim] * shape[dim + 1], *shape[dim + 2 :])


def one_gather(arrays, axis, dims):
    line = jnp.concatenate([a.reshape(-1) for a in arrays])
    lines, at, outs = (lax.all_gather(line, axis), 0, [])
    for a, dim in zip(arrays, dims):
        tiles = lines[:, at : at + a.size].reshape(-1, *a.shape)
        outs.append(in_order(tiles, dim))
        at += a.size
    return tuple(outs)


def over_axes(array, axes):
    for axis in axes:
        array = lax.psum(array, axis)
    return array


def box_sum(padded):
    total = padded[:-2] + padded[1:-1] + padded[2:]
    total = total[:, :-2] + total[:, 1:-1] + total[:, 2:]
    return total[:, :, :-2] + total[:, :, 1:-1] + total[:, :, 2:]


def operate(field, extra):
    padded = extended(field, (("gx", 0), (GY, 1), ("gz", 2)), 1)
    return (27.0 + extra) * field - box_sum(padded)


def operate_column(field, extra):
    padded = extended(field, (("gx", 0), (GY, 1)), 1)
    padded = jnp.pad(padded, ((0, 0), (0, 0), (1, 1)))
    return (27.0 + extra) * field - box_sum(padded)


def cheb_terms(lower):
    upper = 58.0
    theta = (upper + lower) / 2.0
    delta = (upper - lower) / 2.0
    return (theta, delta, theta / delta)


def smooth(rhs, extra, degree, lower, apply):
    theta, delta, sigma = cheb_terms(lower)
    rho = 1.0 / sigma
    step = rhs / theta
    total = step
    remain = rhs
    for count in range(degree - 1):
        remain = remain - apply(step, extra)
        rho_next = 1.0 / (2.0 * sigma - rho)
        step = rho_next * rho * step + 2.0 * rho_next / delta * remain
        total = total + step
        rho = rho_next
    return total


def blocks(field):
    a, b, c = field.shape
    return field.reshape(a // 2, 2, b // 2, 2, c // 2, 2)


def restrict(field):
    return 0.5 * blocks(field).sum(axis=(1, 3, 5))


def prolong(field):
    a, b, c = field.shape
    wide = jnp.broadcast_to(field[:, None, :, None, :, None], (a, 2, b, 2, c, 2))
    return wide.reshape(2 * a, 2 * b, 2 * c)


def inside_mask(shape):
    places = (lax.axis_index("gx"), lax.axis_index(GY), lax.axis_index("gz"))
    counts = (lax.axis_size("gx"), lax.axis_size(GY), lax.axis_size("gz"))
    result = jnp.ones((1, 1, 1), jnp.float32)
    for dim in range(3):
        count = shape[dim]
        spots = places[dim] * count + jnp.arange(count + 2, dtype=jnp.int32) - 1
        valid = ((spots >= 0) & (spots < counts[dim] * count)).astype(jnp.float32)
        dims_shape = [1, 1, 1]
        dims_shape[dim] = count + 2
        result = result * valid.reshape(dims_shape)
    return result


def deep_pre(r_zero, extra_zero, extra_wide, inside):
    theta, delta, sigma = cheb_terms(7.0)
    rho = 1.0 / sigma
    wide = extended(r_zero, (("gx", 0), (GY, 1), ("gz", 2)), 2)
    step = wide / theta
    middle = step[1:-1, 1:-1, 1:-1]
    extra_mid = extra_wide[1:-1, 1:-1, 1:-1]
    remain = (wide[1:-1, 1:-1, 1:-1] - ((27.0 + extra_mid) * middle - box_sum(step))) * inside
    rho_next = 1.0 / (2.0 * sigma - rho)
    smoothed = middle + (rho_next * rho * middle + 2.0 * rho_next / delta * remain)
    inner = smoothed[1:-1, 1:-1, 1:-1]
    rest = r_zero - ((27.0 + extra_zero) * inner - box_sum(smoothed))
    return (inner, rest)


def coarse_solve(r_two, extra_two):
    whole_r, whole_e = one_gather((r_two, extra_two), "gz", (2, 2))
    solved = smooth(whole_r, whole_e, 3, 1.0, operate_column)
    left = whole_r - operate_column(solved, whole_e)
    shift_line = jnp.sum(left, axis=2, keepdims=True) / jnp.sum(
        1.0 + whole_e, axis=2, keepdims=True
    )
    start = lax.axis_index("gz") * r_two.shape[2]
    return lax.dynamic_slice_in_dim(solved, start, r_two.shape[2], 2) + shift_line


def vcycle(r_zero, extra_zero, extra_one, extra_two, extra_wide, inside):
    z_zero, rest = deep_pre(r_zero, extra_zero, extra_wide, inside)
    r_one = restrict(rest)
    z_one = smooth(r_one, extra_one, 2, 7.0, operate)
    r_two = restrict(r_one - operate(z_one, extra_one))
    z_two = coarse_solve(r_two, extra_two)
    z_one = z_one + prolong(z_two)
    z_one = z_one + smooth(r_one - operate(z_one, extra_one), extra_one, 2, 7.0, operate)
    z_zero = z_zero + prolong(z_one)
    z_zero = z_zero + smooth(r_zero - operate(z_zero, extra_zero), extra_zero, 2, 7.0, operate)
    return z_zero


def local(right_side, diagonal):
    extra_one = blocks(diagonal).mean(axis=(1, 3, 5))
    extra_two = blocks(extra_one).mean(axis=(1, 3, 5))
    extra_wide = None
    inside = None
    extra_wide = extended(diagonal, (("gx", 0), (GY, 1), ("gz", 2)), 2)
    inside = inside_mask(diagonal.shape)
    solution_field = jnp.zeros_like(right_side)
    residual = right_side
    direction = jnp.zeros_like(right_side)
    image = jnp.zeros_like(right_side)
    rz_prev = jnp.float32(1.0)
    curve_prev = jnp.float32(0.0)
    for step in range(ITERS):
        precond = vcycle(residual, diagonal, extra_one, extra_two, extra_wide, inside)
        applied = operate(precond, diagonal)
        rz_now, zw_sum, zq_sum = (
            over_axes(jnp.sum(residual * precond), GX_GY_GZ),
            over_axes(jnp.sum(precond * applied), GX_GY_GZ),
            over_axes(jnp.sum(precond * image), GX_GY_GZ),
        )
        beta = 0.0 if step == 0 else rz_now / rz_prev
        direction = precond + beta * direction
        image = applied + beta * image
        curve = zw_sum + 2.0 * beta * zq_sum + beta * beta * curve_prev
        alpha = rz_now / curve
        solution_field = solution_field + alpha * direction
        residual = residual - alpha * image
        rz_prev = rz_now
        curve_prev = curve
    return (solution_field, residual)


def solution(mesh):
    torus = Mesh(
        mesh.devices.reshape(mesh.shape["gx"], 4, 2, mesh.shape["gz"]), ("gx", "gy_0", "gy_1", "gz")
    )
    in_specs = (P("gx", GY, "gz"), P("gx", GY, "gz"))
    out_specs = (P("gx", GY, "gz"), P("gx", GY, "gz"))
    return jax.shard_map(local, mesh=torus, in_specs=in_specs, out_specs=out_specs, check_vma=False)
```

profile of v0, /device:TPU:1, one launch (start us, length us, event | category | flops | bytes accessed | tf_op | source)
XLA Modules:
  0.0 844.0 jit_solution(9266118594562411616)
XLA Ops:
  2.8 4.6 collective-permute-start
  15.6 5.5 collective-permute-start.2
  34.1 4.2 collective-permute-start.10
  41.8 4.3 collective-permute-done.5
  55.2 18.1 %reshape.156 = f32[8,2,16,2,64,2]{5,4,3,2,1,0:T(8,128)} reshape(f32[16,32,128]{2,1,0:T(8,128)S(1)} %fusion.32) | data formatting | bytes 524288 | tf_op jit(solution)/shard_map/reshape | solution.py:92
  73.4 7.0 reduce_sum.158
  88.8 6.5 collective-permute-start.14
  105.2 18.1 %reshape.157 = f32[8,2,16,2,64,2]{5,4,3,2,1,0:T(8,128)} reshape(f32[16,32,128]{2,1,0:T(8,128)S(1)} %copy-done) | data formatting | bytes 524288 | tf_op jit(solution)/shard_map/reshape | solution.py:92
  123.3 7.0 reduce_sum.159
  146.9 5.4 collective-permute-start.22
  154.2 5.0 collective-permute-done.23
  170.6 19.4 %all-gather = f32[16384]{0:T(1024)S(1)} all-gather(f32[2048]{0:T(1024)S(1)} %pad_maximum_fusion.41), channel_id=2, replica_groups=mesh['gx'=4,'gy_0'=4,'gy_1'=2,'gz'=8] {'gz'}, dimensions={0}, use_global_device_ids=true | all-gather | bytes 73728 | tf_op jit(solution)/shard_map/all_gather | solution.py:37
  197.9 11.6 %collective-permute-start.26 = (f32[6,1,256]{2,1,0:T(1,128)S(1)}, f32[6,1,256]{2,1,0:T(1,128)S(1)}, u32[]{:S(2)}, u32[]{:S(2)}) collective-permute-start(f32[6,1,256]{2,1,0:T(1,128)S(1)} %get-tuple-element.166), channel_id=1, source_target_pairs={{0,8},{8,16},{16,24},{24,32},{32,40},{40,48},{48,56},{1,9},{9,17},... | collective-permute-start | bytes 18440 | tf_op jit(solution)/shard_map/ppermute | solution.py:20
  278.6 5.4 collective-permute-start.44
  298.3 6.6 broadcast_in_dim.11
  304.9 12.6 %reshape.162 = f32[16,32,128]{2,1,0:T(8,128)S(1)} reshape(f32[8,2,16,2,64,2]{5,4,3,2,1,0:T(8,128)} %broadcast_in_dim.11) | data formatting | bytes 524288 | tf_op jit(solution)/shard_map/reshape | solution.py:102
  323.8 4.6 collective-permute-start.50
  338.4 5.6 collective-permute-done.52
  355.1 4.6 collective-permute-start.56
  369.6 5.6 collective-permute-done.58
  386.3 4.7 collective-permute-start.62
  400.9 5.6 collective-permute-done.64
  412.1 6.7 all-reduce.11
  418.8 6.7 all-reduce.9
  425.5 6.3 all-reduce.13
  431.7 12.6 %all-reduce.7 = (f32[]{:T(128)}, f32[]{:T(128)}, f32[]{:T(128)}) all-reduce(f32[]{:T(128)} %get-tuple-element.29, f32[]{:T(128)} %get-tuple-element.30, f32[]{:T(128)} %get-tuple-element.31), channel_id=1, replica_groups=mesh['gx'=4,'gy_0'=4,'gy_1'=2,'gz'=8] {'gz'}, use_global_device_ids=true, to_apply=%region_11.12 | all-reduce | flops 3 | bytes 24 | tf_op jit(solution)/shard_map/psum | solution.py:47
  454.7 8.6 %collective-permute-start.68 = (f32[20,2,128]{2,1,0:T(2,128)S(1)}, f32[20,2,128]{2,1,0:T(2,128)S(1)}, u32[]{:S(2)}, u32[]{:S(2)}) collective-permute-start(f32[20,2,128]{2,1,0:T(2,128)S(1)} %get-tuple-element.64), channel_id=1, source_target_pairs={{0,8},{8,16},{16,24},{24,32},{32,40},{40,48},{48,56},{1,9},{9,17},... | collective-permute-start | bytes 61448 | tf_op jit(solution)/shard_map/ppermute | solution.py:20
  472.1 6.4 collective-permute-done.70
  478.5 4.1 collective-permute-done.71
  486.3 18.1 %reshape.163 = f32[8,2,16,2,64,2]{5,4,3,2,1,0:T(8,128)} reshape(f32[16,32,128]{2,1,0:T(8,128)S(1)} %fusion.21) | data formatting | bytes 524288 | tf_op jit(solution)/shard_map/reshape | solution.py:92
  504.4 7.0 reduce_sum.169
  517.5 4.2 collective-permute-start.74
  531.5 4.8 collective-permute-done.77
  544.4 4.9 collective-permute-start.80
  554.3 5.2 collective-permute-start.82
  571.0 19.0 %all-gather.1 = f32[16384]{0:T(1024)S(1)} all-gather(f32[2048]{0:T(1024)S(1)} %pad_maximum_fusion.40), channel_id=3, replica_groups=mesh['gx'=4,'gy_0'=4,'gy_1'=2,'gz'=8] {'gz'}, dimensions={0}, use_global_device_ids=true | all-gather | bytes 73728 | tf_op jit(solution)/shard_map/all_gather | solution.py:37
  596.4 10.4 %collective-permute-start.86 = (f32[6,1,256]{2,1,0:T(1,128)S(1)}, f32[6,1,256]{2,1,0:T(1,128)S(1)}, u32[]{:S(2)}, u32[]{:S(2)}) collective-permute-start(f32[6,1,256]{2,1,0:T(1,128)S(1)} %get-tuple-element.160), channel_id=1, source_target_pairs={{0,8},{8,16},{16,24},{24,32},{32,40},{40,48},{48,56},{1,9},{9,17},... | collective-permute-start | bytes 18440 | tf_op jit(solution)/shard_map/ppermute | solution.py:20
  676.1 4.6 collective-permute-start.104
  694.9 6.6 broadcast_in_dim.14
  701.5 12.6 %reshape.168 = f32[16,32,128]{2,1,0:T(8,128)S(1)} reshape(f32[8,2,16,2,64,2]{5,4,3,2,1,0:T(8,128)} %broadcast_in_dim.14) | data formatting | bytes 524288 | tf_op jit(solution)/shard_map/reshape | solution.py:102
  735.1 5.6 collective-permute-done.112
  752.3 4.2 collective-permute-start.116
  766.4 5.6 collective-permute-done.118
  796.2 5.6 collective-permute-done.124
  807.4 6.7 all-reduce.10
  814.1 6.6 all-reduce.8
  820.7 6.3 all-reduce.12
  826.9 12.5 %all-reduce.6 = (f32[]{:T(128)}, f32[]{:T(128)}, f32[]{:T(128)}) all-reduce(f32[]{:T(128)} %get-tuple-element.26, f32[]{:T(128)} %get-tuple-element.27, f32[]{:T(128)} %get-tuple-element.28), channel_id=1, replica_groups=mesh['gx'=4,'gy_0'=4,'gy_1'=2,'gz'=8] {'gz'}, use_global_device_ids=true, to_apply=%region_31.32 | all-reduce | flops 3 | bytes 24 | tf_op jit(solution)/shard_map/psum | solution.py:47
  (492 shorter events, 461.0 us)
Async XLA Ops:
  1.5 13.1 %collective-permute-start.1 = (f32[2,32,128]{2,1,0:T(8,128)S(1)}, f32[2,32,128]{2,1,0:T(8,128)S(1)}, u32[]{:S(2)}, u32[]{:S(2)}) collective-permute-start(f32[2,32,128]{2,1,0:T(8,128)S(1)} %get-tuple-element.98), channel_id=1, source_target_pairs={{64,0},{128,64},{192,128},{65,1},{129,65},{193,129},{66,2},{130,66... | collective-permute-start | bytes 98312 | tf_op jit(solution)/shard_map/ppermute | solution.py:22
  2.8 10.8 %collective-permute-start = (f32[2,32,128]{2,1,0:T(8,128)S(1)}, f32[2,32,128]{2,1,0:T(8,128)S(1)}, u32[]{:S(2)}, u32[]{:S(2)}) collective-permute-start(f32[2,32,128]{2,1,0:T(8,128)S(1)} %get-tuple-element.99), channel_id=1, source_target_pairs={{0,64},{64,128},{128,192},{1,65},{65,129},{129,193},{2,66},{66,130... | collective-permute-start | bytes 98312 | tf_op jit(solution)/shard_map/ppermute | solution.py:20
  8.1 14.9 %collective-permute-start.7 = (f32[2,32,128]{2,1,0:T(8,128)S(1)}, f32[2,32,128]{2,1,0:T(8,128)S(1)}, u32[]{:S(2)}, u32[]{:S(2)}) collective-permute-start(f32[2,32,128]{2,1,0:T(8,128)S(1)} %get-tuple-element.96), channel_id=1, source_target_pairs={{64,0},{128,64},{192,128},{65,1},{129,65},{193,129},{66,2},{130,66... | collective-permute-start | bytes 98312 | tf_op jit(solution)/shard_map/ppermute | solution.py:22
  15.6 13.1 %collective-permute-start.2 = (f32[20,2,128]{2,1,0:T(2,128)S(1)}, f32[20,2,128]{2,1,0:T(2,128)S(1)}, u32[]{:S(2)}, u32[]{:S(2)}) collective-permute-start(f32[20,2,128]{2,1,0:T(2,128)S(1)} %get-tuple-element.68), channel_id=1, source_target_pairs={{0,8},{8,16},{16,24},{24,32},{32,40},{40,48},{48,56},{1,9},{9,17},... | collective-permute-start | bytes 61448 | tf_op jit(solution)/shard_map/ppermute | solution.py:20
  21.1 7.6 collective-permute-start.3
  23.1 10.7 %collective-permute-start.8 = (f32[20,2,128]{2,1,0:T(2,128)S(1)}, f32[20,2,128]{2,1,0:T(2,128)S(1)}, u32[]{:S(2)}, u32[]{:S(2)}) collective-permute-start(f32[20,2,128]{2,1,0:T(2,128)S(1)} %get-tuple-element.66), channel_id=1, source_target_pairs={{0,8},{8,16},{16,24},{24,32},{32,40},{40,48},{48,56},{1,9},{9,17},... | collective-permute-start | bytes 61448 | tf_op jit(solution)/shard_map/ppermute | solution.py:20
  26.8 7.1 collective-permute-start.9
  28.9 12.9 %collective-permute-start.4 = (f32[20,36,2]{2,1,0:T(8,128)S(1)}, f32[20,36,2]{2,1,0:T(8,128)S(1)}, u32[]{:S(2)}, u32[]{:S(2)}) collective-permute-start(f32[20,36,2]{2,1,0:T(8,128)S(1)} %get-tuple-element.50), channel_id=1, source_target_pairs={{0,1},{1,2},{2,3},{3,4},{4,5},{5,6},{6,7},{8,9},{9,10},{10,11},{11... | collective-permute-start | bytes 17288 | tf_op jit(solution)/shard_map/ppermute | solution.py:20
  32.5 13.6 %collective-permute-start.5 = (f32[20,36,2]{2,1,0:T(8,128)S(1)}, f32[20,36,2]{2,1,0:T(8,128)S(1)}, u32[]{:S(2)}, u32[]{:S(2)}) collective-permute-start(f32[20,36,2]{2,1,0:T(8,128)S(1)} %get-tuple-element.51), channel_id=1, source_target_pairs={{1,0},{2,1},{3,2},{4,3},{5,4},{6,5},{7,6},{9,8},{10,9},{11,10},{12... | collective-permute-start | bytes 17288 | tf_op jit(solution)/shard_map/ppermute | solution.py:22
  34.1 15.0 %collective-permute-start.10 = (f32[20,36,2]{2,1,0:T(8,128)S(1)}, f32[20,36,2]{2,1,0:T(8,128)S(1)}, u32[]{:S(2)}, u32[]{:S(2)}) collective-permute-start(f32[20,36,2]{2,1,0:T(8,128)S(1)} %get-tuple-element.48), channel_id=1, source_target_pairs={{0,1},{1,2},{2,3},{3,4},{4,5},{5,6},{6,7},{8,9},{9,10},{10,11},{11... | collective-permute-start | bytes 17288 | tf_op jit(solution)/shard_map/ppermute | solution.py:20
  38.3 15.0 %collective-permute-start.11 = (f32[20,36,2]{2,1,0:T(8,128)S(1)}, f32[20,36,2]{2,1,0:T(8,128)S(1)}, u32[]{:S(2)}, u32[]{:S(2)}) collective-permute-start(f32[20,36,2]{2,1,0:T(8,128)S(1)} %get-tuple-element.49), channel_id=1, source_target_pairs={{1,0},{2,1},{3,2},{4,3},{5,4},{6,5},{7,6},{9,8},{10,9},{11,10},{12... | collective-permute-start | bytes 17288 | tf_op jit(solution)/shard_map/ppermute | solution.py:22
  88.8 8.4 collective-permute-start.14
  100.3 30.0 %collective-permute-start.16 = (f32[10,18,1]{2,1,0:T(8,128)S(1)}, f32[10,18,1]{2,1,0:T(8,128)S(1)}, u32[]{:S(2)}, u32[]{:S(2)}) collective-permute-start(f32[10,18,1]{2,1,0:T(8,128)S(1)} %get-tuple-element.114), channel_id=1, source_target_pairs={{0,1},{1,2},{2,3},{3,4},{4,5},{5,6},{6,7},{8,9},{9,10},{10,11},{11... | collective-permute-start | bytes 2168 | tf_op jit(solution)/shard_map/ppermute | solution.py:20
  103.9 26.4 %collective-permute-start.17 = (f32[10,18,1]{2,1,0:T(8,128)S(1)}, f32[10,18,1]{2,1,0:T(8,128)S(1)}, u32[]{:S(2)}, u32[]{:S(2)}) collective-permute-start(f32[10,18,1]{2,1,0:T(8,128)S(1)} %get-tuple-element.115), channel_id=1, source_target_pairs={{1,0},{2,1},{3,2},{4,3},{5,4},{6,5},{7,6},{9,8},{10,9},{11,10},{12... | collective-permute-start | bytes 2168 | tf_op jit(solution)/shard_map/ppermute | solution.py:22
  146.9 7.2 collective-permute-start.22
  152.3 6.8 collective-permute-start.23
  197.9 13.8 %collective-permute-start.26 = (f32[6,1,256]{2,1,0:T(1,128)S(1)}, f32[6,1,256]{2,1,0:T(1,128)S(1)}, u32[]{:S(2)}, u32[]{:S(2)}) collective-permute-start(f32[6,1,256]{2,1,0:T(1,128)S(1)} %get-tuple-element.166), channel_id=1, source_target_pairs={{0,8},{8,16},{16,24},{24,32},{32,40},{40,48},{48,56},{1,9},{9,17},... | collective-permute-start | bytes 18440 | tf_op jit(solution)/shard_map/ppermute | solution.py:20
  262.3 5.9 collective-permute-start.40
  266.4 5.8 collective-permute-start.41
  278.6 7.3 collective-permute-start.44
  292.2 5.8 collective-permute-start.47
  323.8 6.6 collective-permute-start.50
  333.7 10.3 %collective-permute-start.52 = (f32[18,34,1]{2,1,0:T(8,128)S(1)}, f32[18,34,1]{2,1,0:T(8,128)S(1)}, u32[]{:S(2)}, u32[]{:S(2)}) collective-permute-start(f32[18,34,1]{2,1,0:T(8,128)S(1)} %get-tuple-element.62), channel_id=1, source_target_pairs={{0,1},{1,2},{2,3},{3,4},{4,5},{5,6},{6,7},{8,9},{9,10},{10,11},{11... | collective-permute-start | bytes 7352 | tf_op jit(solution)/shard_map/ppermute | solution.py:20
  337.1 11.0 %collective-permute-start.53 = (f32[18,34,1]{2,1,0:T(8,128)S(1)}, f32[18,34,1]{2,1,0:T(8,128)S(1)}, u32[]{:S(2)}, u32[]{:S(2)}) collective-permute-start(f32[18,34,1]{2,1,0:T(8,128)S(1)} %get-tuple-element.63), channel_id=1, source_target_pairs={{1,0},{2,1},{3,2},{4,3},{5,4},{6,5},{7,6},{9,8},{10,9},{11,10},{12... | collective-permute-start | bytes 7352 | tf_op jit(solution)/shard_map/ppermute | solution.py:22
  355.1 7.0 collective-permute-start.56
  365.1 10.1 %collective-permute-start.58 = (f32[18,34,1]{2,1,0:T(8,128)S(1)}, f32[18,34,1]{2,1,0:T(8,128)S(1)}, u32[]{:S(2)}, u32[]{:S(2)}) collective-permute-start(f32[18,34,1]{2,1,0:T(8,128)S(1)} %get-tuple-element.60), channel_id=1, source_target_pairs={{0,1},{1,2},{2,3},{3,4},{4,5},{5,6},{6,7},{8,9},{9,10},{10,11},{11... | collective-permute-start | bytes 7352 | tf_op jit(solution)/shard_map/ppermute | solution.py:20
  368.3 11.0 %collective-permute-start.59 = (f32[18,34,1]{2,1,0:T(8,128)S(1)}, f32[18,34,1]{2,1,0:T(8,128)S(1)}, u32[]{:S(2)}, u32[]{:S(2)}) collective-permute-start(f32[18,34,1]{2,1,0:T(8,128)S(1)} %get-tuple-element.61), channel_id=1, source_target_pairs={{1,0},{2,1},{3,2},{4,3},{5,4},{6,5},{7,6},{9,8},{10,9},{11,10},{12... | collective-permute-start | bytes 7352 | tf_op jit(solution)/shard_map/ppermute | solution.py:22
  386.3 6.6 collective-permute-start.62
  396.2 10.3 %collective-permute-start.64 = (f32[18,34,1]{2,1,0:T(8,128)S(1)}, f32[18,34,1]{2,1,0:T(8,128)S(1)}, u32[]{:S(2)}, u32[]{:S(2)}) collective-permute-start(f32[18,34,1]{2,1,0:T(8,128)S(1)} %get-tuple-element.58), channel_id=1, source_target_pairs={{0,1},{1,2},{2,3},{3,4},{4,5},{5,6},{6,7},{8,9},{9,10},{10,11},{11... | collective-permute-start | bytes 7352 | tf_op jit(solution)/shard_map/ppermute | solution.py:20
  399.6 11.0 %collective-permute-start.65 = (f32[18,34,1]{2,1,0:T(8,128)S(1)}, f32[18,34,1]{2,1,0:T(8,128)S(1)}, u32[]{:S(2)}, u32[]{:S(2)}) collective-permute-start(f32[18,34,1]{2,1,0:T(8,128)S(1)} %get-tuple-element.59), channel_id=1, source_target_pairs={{1,0},{2,1},{3,2},{4,3},{5,4},{6,5},{7,6},{9,8},{10,9},{11,10},{12... | collective-permute-start | bytes 7352 | tf_op jit(solution)/shard_map/ppermute | solution.py:22
  454.7 10.5 %collective-permute-start.68 = (f32[20,2,128]{2,1,0:T(2,128)S(1)}, f32[20,2,128]{2,1,0:T(2,128)S(1)}, u32[]{:S(2)}, u32[]{:S(2)}) collective-permute-start(f32[20,2,128]{2,1,0:T(2,128)S(1)} %get-tuple-element.64), channel_id=1, source_target_pairs={{0,8},{8,16},{16,24},{24,32},{32,40},{40,48},{48,56},{1,9},{9,17},... | collective-permute-start | bytes 61448 | tf_op jit(solution)/shard_map/ppermute | solution.py:20
  468.6 9.9 %collective-permute-start.70 = (f32[20,36,2]{2,1,0:T(8,128)S(1)}, f32[20,36,2]{2,1,0:T(8,128)S(1)}, u32[]{:S(2)}, u32[]{:S(2)}) collective-permute-start(f32[20,36,2]{2,1,0:T(8,128)S(1)} %get-tuple-element.46), channel_id=1, source_target_pairs={{0,1},{1,2},{2,3},{3,4},{4,5},{5,6},{6,7},{8,9},{9,10},{10,11},{11... | collective-permute-start | bytes 17288 | tf_op jit(solution)/shard_map/ppermute | solution.py:20
  470.8 11.8 %collective-permute-start.71 = (f32[20,36,2]{2,1,0:T(8,128)S(1)}, f32[20,36,2]{2,1,0:T(8,128)S(1)}, u32[]{:S(2)}, u32[]{:S(2)}) collective-permute-start(f32[20,36,2]{2,1,0:T(8,128)S(1)} %get-tuple-element.47), channel_id=1, source_target_pairs={{1,0},{2,1},{3,2},{4,3},{5,4},{6,5},{7,6},{9,8},{10,9},{11,10},{12... | collective-permute-start | bytes 17288 | tf_op jit(solution)/shard_map/ppermute | solution.py:22
  517.5 6.1 collective-permute-start.74
  529.7 6.6 collective-permute-start.77
  544.4 6.8 collective-permute-start.80
  554.3 7.0 collective-permute-start.82
  596.4 12.6 %collective-permute-start.86 = (f32[6,1,256]{2,1,0:T(1,128)S(1)}, f32[6,1,256]{2,1,0:T(1,128)S(1)}, u32[]{:S(2)}, u32[]{:S(2)}) collective-permute-start(f32[6,1,256]{2,1,0:T(1,128)S(1)} %get-tuple-element.160), channel_id=1, source_target_pairs={{0,8},{8,16},{16,24},{24,32},{32,40},{40,48},{48,56},{1,9},{9,17},... | collective-permute-start | bytes 18440 | tf_op jit(solution)/shard_map/ppermute | solution.py:20
  676.1 6.6 collective-permute-start.104
  688.7 5.9 collective-permute-start.107
  720.8 6.0 collective-permute-start.110
  730.2 10.6 %collective-permute-start.112 = (f32[18,34,1]{2,1,0:T(8,128)S(1)}, f32[18,34,1]{2,1,0:T(8,128)S(1)}, u32[]{:S(2)}, u32[]{:S(2)}) collective-permute-start(f32[18,34,1]{2,1,0:T(8,128)S(1)} %get-tuple-element.56), channel_id=1, source_target_pairs={{0,1},{1,2},{2,3},{3,4},{4,5},{5,6},{6,7},{8,9},{9,10},{10,11},{11... | collective-permute-start | bytes 7352 | tf_op jit(solution)/shard_map/ppermute | solution.py:20
  733.8 11.0 %collective-permute-start.113 = (f32[18,34,1]{2,1,0:T(8,128)S(1)}, f32[18,34,1]{2,1,0:T(8,128)S(1)}, u32[]{:S(2)}, u32[]{:S(2)}) collective-permute-start(f32[18,34,1]{2,1,0:T(8,128)S(1)} %get-tuple-element.57), channel_id=1, source_target_pairs={{1,0},{2,1},{3,2},{4,3},{5,4},{6,5},{7,6},{9,8},{10,9},{11,10},{12... | collective-permute-start | bytes 7352 | tf_op jit(solution)/shard_map/ppermute | solution.py:22
  752.3 6.2 collective-permute-start.116
  761.7 10.3 %collective-permute-start.118 = (f32[18,34,1]{2,1,0:T(8,128)S(1)}, f32[18,34,1]{2,1,0:T(8,128)S(1)}, u32[]{:S(2)}, u32[]{:S(2)}) collective-permute-start(f32[18,34,1]{2,1,0:T(8,128)S(1)} %get-tuple-element.54), channel_id=1, source_target_pairs={{0,1},{1,2},{2,3},{3,4},{4,5},{5,6},{6,7},{8,9},{9,10},{10,11},{11... | collective-permute-start | bytes 7352 | tf_op jit(solution)/shard_map/ppermute | solution.py:20
  765.1 11.0 %collective-permute-start.119 = (f32[18,34,1]{2,1,0:T(8,128)S(1)}, f32[18,34,1]{2,1,0:T(8,128)S(1)}, u32[]{:S(2)}, u32[]{:S(2)}) collective-permute-start(f32[18,34,1]{2,1,0:T(8,128)S(1)} %get-tuple-element.55), channel_id=1, source_target_pairs={{1,0},{2,1},{3,2},{4,3},{5,4},{6,5},{7,6},{9,8},{10,9},{11,10},{12... | collective-permute-start | bytes 7352 | tf_op jit(solution)/shard_map/ppermute | solution.py:22
  792.0 9.8 %collective-permute-start.124 = (f32[18,34,1]{2,1,0:T(8,128)S(1)}, f32[18,34,1]{2,1,0:T(8,128)S(1)}, u32[]{:S(2)}, u32[]{:S(2)}) collective-permute-start(f32[18,34,1]{2,1,0:T(8,128)S(1)} %get-tuple-element.52), channel_id=1, source_target_pairs={{0,1},{1,2},{2,3},{3,4},{4,5},{5,6},{6,7},{8,9},{9,10},{10,11},{11... | collective-permute-start | bytes 7352 | tf_op jit(solution)/shard_map/ppermute | solution.py:20
  794.9 11.0 %collective-permute-start.125 = (f32[18,34,1]{2,1,0:T(8,128)S(1)}, f32[18,34,1]{2,1,0:T(8,128)S(1)}, u32[]{:S(2)}, u32[]{:S(2)}) collective-permute-start(f32[18,34,1]{2,1,0:T(8,128)S(1)} %get-tuple-element.53), channel_id=1, source_target_pairs={{1,0},{2,1},{3,2},{4,3},{5,4},{6,5},{7,6},{9,8},{10,9},{11,10},{12... | collective-permute-start | bytes 7352 | tf_op jit(solution)/shard_map/ppermute | solution.py:22
  (94 other events, 1449.1 us)
where the time goes:
time: 859 us; the launch traced here: 844 us
  starting transfers between devices  323 us (38%)
  waiting for transfers between devices  245 us (29%)
  local copies, waits for them, and re-layouts  118 us (14%)
  blocking collectives  103 us (12%)
  other arithmetic  47 us (5%)
  between operations  9.07 us (1%)
    ppermute x63, starting transfers between devices, extended(): lax.ppermute(tail, axis, [(i, (i + 1) % count) for i in range(ends)])  226 us
    ppermute x63, waiting for transfers between devices, extended(): lax.ppermute(head, axis, [((i + 1) % count, i) for i in range(ends)])  196 us
    ppermute x63, starting transfers between devices, extended(): lax.ppermute(head, axis, [((i + 1) % count, i) for i in range(ends)])  96.3 us
    psum x8, blocking collectives, over_axes(): array = lax.psum(array, axis)  64.3 us
    reshape x5, local copies, waits for them, and re-layouts, blocks(): return field.reshape(a // 2, 2, b // 2, 2, c // 2, 2)  60.8 us
    ppermute x63, waiting for transfers between devices, extended(): lax.ppermute(tail, axis, [(i, (i + 1) % count) for i in range(ends)])  48.5 us
    all_gather x2, blocking collectives, one_gather(): lines, at, outs = (lax.all_gather(line, axis), 0, [])  38.4 us
    reshape x4, local copies, waits for them, and re-layouts, prolong(): return wide.reshape(2 * a, 2 * b, 2 * c)  30.8 us
  transfers between devices with their start and end apart: 126, of which 74 were waited for; matrix products, arithmetic and copies ran while one was open for 4% of the time, Pallas kernels for 0%

commit v1 on v0

v1 whole, which is shorter than its diff:
```python
import functools

import jax
import jax.numpy as jnp
from jax import lax
from jax.experimental import pallas as pl
from jax.experimental.pallas import tpu as pltpu
from jax.sharding import PartitionSpec as P

GX, GY, GZ = 4, 8, 8
BX, BY, BZ = 16, 32, 128
HX, HY, HZ = 12, 16, 64
EX, EY, EZ = BX + 2 * HX, BY + 2 * HY, BZ + 2 * HZ
MX, MY, MZ = EX // 2, EY // 2, EZ // 2
F32 = jnp.float32
HIGH = lax.Precision.HIGHEST
SPEC = P("gx", "gy", "gz")


def cheb_two(lower, upper=58.0):
    theta, delta = (upper + lower) / 2.0, (upper - lower) / 2.0
    sigma = theta / delta
    rho = 1.0 / sigma
    after = 1.0 / (2.0 * sigma - rho)
    return (1.0 + after * rho) / theta + 2.0 * after / delta, -2.0 * after / (delta * theta)


CR, CA = cheb_two(7.0)


def spread(t):
    t = t + pltpu.roll(t, 1, 0) + pltpu.roll(t, t.shape[0] - 1, 0)
    return t + pltpu.roll(t, 1, 1) + pltpu.roll(t, t.shape[1] - 1, 1)


def inside(first, dim, shape, count):
    spot = first + lax.broadcasted_iota(jnp.int32, shape, dim)
    return jnp.where((spot >= 0) & (spot < count), 1.0, 0.0).astype(F32)


def inside_one(spot, count):
    return jnp.where((spot >= 0) & (spot < count), 1.0, 0.0).astype(F32)


def places():
    return lax.axis_index("gx"), lax.axis_index("gy"), lax.axis_index("gz")


def plane_mask(level, shape, rows):
    _, gy, gz = places()
    size = 1 << level
    lanes = gz * (BZ // size) - HZ // size
    return inside(gy * (BY // size) - rows, 0, shape, GY * BY // size) * inside(
        lanes, 1, shape, GZ * BZ // size
    )


def x_mask(level, plane):
    gx = places()[0]
    size = 1 << level
    return inside_one(gx * (BX // size) - HX // size + plane, GX * BX // size)


def loop(first, last, body, unroll=1):
    def step(i, carry):
        body(i)
        return carry

    lax.fori_loop(first, last, step, 0, unroll=unroll)


def halving(rows, cols, per=2):
    a = lax.broadcasted_iota(jnp.int32, (rows, cols), 0)
    b = lax.broadcasted_iota(jnp.int32, (rows, cols), 1)
    return jnp.where(a // 2 == b, 1.0, 0.0).astype(F32)


def doubling(rows, cols):
    a = lax.broadcasted_iota(jnp.int32, (rows, cols), 0)
    b = lax.broadcasted_iota(jnp.int32, (rows, cols), 1)
    return jnp.where(b // 2 == a, 1.0, 0.0).astype(F32)


def dot(a, b):
    return jnp.dot(a, b, precision=HIGH, preferred_element_type=F32)


def assemble(dst, which, own, xlo, xhi, ylo, yhi, change):
    def part(src, base, count, lo, hi):
        def body(i):
            dst[base + i, lo:hi, :] = change(src[which, i], base + i, lo, hi)

        loop(0, count, body)

    part(own, HX, BX, HY, HY + BY)
    part(xlo, 0, HX, HY, HY + BY)
    part(xhi, HX + BX, HX, HY, HY + BY)
    part(ylo, 0, EX, 0, HY)
    part(yhi, 0, EX, HY + BY, EY)


def halve(scratch, rows_scratch, z_map):
    rows_scratch[...] = dot(scratch[...], z_map)
    count = rows_scratch.shape[0] // 2
    return rows_scratch[pl.ds(0, count, stride=2), :] + rows_scratch[pl.ds(1, count, stride=2), :]


def pre_kernel(first, own, xlo, xhi, ylo, yhi, *refs):
    d0, d1, zs, rs, z1, left1, packed, field, zfull, pairs, rows, r1, small = refs
    gx, gy, gz = places()
    mask = plane_mask(0, (EY, EZ), HY)
    z_map = halving(EZ, MZ)

    assemble(
        field, 0, own, xlo, xhi, ylo, yhi,
        lambda v, p, lo, hi: v * (mask[lo:hi] * x_mask(0, p)),
    )
    if first:
        assemble(d0, 1, own, xlo, xhi, ylo, yhi, lambda v, p, lo, hi: v + 27.0)

        def add_pair(i):
            pairs[pl.ds(pl.multiple_of(i * EY, EY), EY), :] = d0[2 * i] + d0[2 * i + 1]

        loop(0, MX, add_pair)
        d1[...] = (halve(pairs, rows, z_map) * 0.125).reshape(MX, MY, MZ)

    pairs[0:EY, :] = jnp.zeros((EY, EZ), F32)
    pairs[(MX - 1) * EY :, :] = jnp.zeros((EY, EZ), F32)

    def smooth(p):
        r = field[p]
        box = spread(field[p - 1] + r + field[p + 1])
        zfull[p] = (mask * x_mask(0, p)) * (CR * r + CA * (d0[p] * r - box))

    loop(1, EX - 1, smooth)

    def rest(p):
        z = zfull[p]
        return field[p] - d0[p] * z + spread(zfull[p - 1] + z + zfull[p + 1])

    def rest_pair(i):
        a, b = rest(2 * i), rest(2 * i + 1)
        pairs[pl.ds(pl.multiple_of(i * EY, EY), EY), :] = a + b

        @pl.when((i >= 5) & (i < 15))
        def _():
            rs[2 * i - 10] = a[8:56]
            rs[2 * i - 9] = b[8:56]

    loop(1, MX - 1, rest_pair)

    def keep(p):
        zs[p] = zfull[p + 10, 8:56, :]

    loop(0, 20, keep)

    mask1 = plane_mask(1, (MY, MZ), HY // 2)
    r1[...] = (halve(pairs, rows, z_map) * 0.5).reshape(MX, MY, MZ)

    def mask_one(p):
        r1[p] = r1[p] * (mask1 * x_mask(1, p))

    loop(0, MX, mask_one)

    def smooth_one(p):
        r = r1[p]
        box = spread(r1[p - 1] + r + r1[p + 1])
        z1[p] = (mask1 * x_mask(1, p)) * (CR * r + CA * (d1[p] * r - box))

    z1[0] = jnp.zeros((MY, MZ), F32)
    z1[MX - 1] = jnp.zeros((MY, MZ), F32)
    left1[0] = jnp.zeros((MY, MZ), F32)
    left1[MX - 1] = jnp.zeros((MY, MZ), F32)
    loop(1, MX - 1, smooth_one)

    def rest_one(p):
        z = z1[p]
        left1[p] = r1[p] - d1[p] * z + spread(z1[p - 1] + z + z1[p + 1])

    loop(1, MX - 1, rest_one)

    lane = lax.broadcasted_iota(jnp.int32, (MZ, 128), 0)
    col = lax.broadcasted_iota(jnp.int32, (MZ, 128), 1)

    def pack(src, scale):
        total = jnp.zeros((16, 128), F32)
        for k in range(4):
            s = src[6 + 2 * k, 8:24, :] + src[7 + 2 * k, 8:24, :]
            pick = (lane // 2 - 16 + 32 * k == col) & (lane >= 32) & (lane < 96)
            total = total + dot(s, jnp.where(pick, 1.0, 0.0).astype(F32))
        small[...] = total
        return (small[pl.ds(0, 8, stride=2), :] + small[pl.ds(1, 8, stride=2), :]) * scale

    tile = pack(left1, 0.5)
    if first:
        tile = jnp.concatenate([tile, pack(d1, 0.125)], axis=0)

    def copy(i):
        packed[i] = tile

    loop(0, GX * GZ, copy)


def unpack(dst, row, lo, own, hi):
    group = lax.broadcasted_iota(jnp.int32, (8, 128), 1) // 32
    for part, src in enumerate((lo, own, hi)):
        for bx in range(GX):
            for k in range(4):
                halves = []
                for h in range(2):
                    acc = None
                    for j in range(4):
                        block = src[bx * GZ + 4 * h + j, row : row + 8, :]
                        shift = (32 * (j - k)) % 128
                        if shift:
                            block = pltpu.roll(block, shift, 1)
                        acc = block if acc is None else jnp.where(group == j, block, acc)
                    halves.append(acc)
                dst[1 + 4 * bx + k, 8 * part : 8 * part + 8, :] = jnp.concatenate(halves, axis=1)


def coarse(r2, d2, s0, s1, z2, gy):
    shape = (24, 256)
    mask = inside(gy * 8 - 8, 0, shape, 64)
    lane = lax.broadcasted_iota(jnp.int32, shape, 1)

    def box(t):
        t = t + pltpu.roll(t, 1, 0) + pltpu.roll(t, 23, 0)
        return (
            t
            + jnp.where(lane == 0, 0.0, pltpu.roll(t, 1, 1))
            + jnp.where(lane == 255, 0.0, pltpu.roll(t, 255, 1))
        )

    theta, delta = 29.5, 28.5
    sigma = theta / delta
    rho = 1.0 / sigma
    rho1 = 1.0 / (2.0 * sigma - rho)
    rho2 = 1.0 / (2.0 * sigma - rho1)
    zero = jnp.zeros(shape, F32)
    for ref in (r2, s0, s1, z2):
        ref[0] = zero
        ref[17] = zero

    def scale(p):
        r2[p] = r2[p] * mask

    loop(1, 17, scale)

    def one(p):
        r = r2[p]
        step = r * (1.0 / theta)
        remain = mask * (r - d2[p] * step + box(r2[p - 1] + r + r2[p + 1]) * (1.0 / theta))
        s0[p] = remain
        s1[p] = (rho1 * rho) * step + (2.0 * rho1 / delta) * remain

    loop(1, 17, one)

    def two(p):
        step = s1[p]
        remain = mask * (s0[p] - d2[p] * step + box(s1[p - 1] + step + s1[p + 1]))
        last = (rho2 * rho1) * step + (2.0 * rho2 / delta) * remain
        z2[p] = r2[p] * (1.0 / theta) + step + last

    loop(1, 17, two)

    def three(p):
        y = z2[p]
        left = r2[p] - d2[p] * y + box(z2[p - 1] + y + z2[p + 1])
        top = jnp.sum(left, axis=1, keepdims=True)
        low = jnp.sum(d2[p] - 26.0, axis=1, keepdims=True)
        s0[p] = mask * (y + top / low)

    loop(1, 17, three)


def post_kernel(first, *refs):
    if first:
        (lo, own, hi, zs, rs, z1, left1, d0, d1, r_core,
         d2, z_core, q_core, q_ext, dots,
         r2, s0, s1, z2, wide, rows1, u, rem, zf1, rowsv, v, rem0, zf0, acc) = refs
    else:
        (lo, own, hi, zs, rs, z1, left1, d0, d1, d2,
         z_core, q_core,
         r2, s0, s1, z2, wide, rows1, u, rem, zf1, rowsv, v, rem0, zf0) = refs
    gx, gy, gz = places()
    unpack(r2, 0, lo, own, hi)
    if first:
        unpack(d2, 8, lo, own, hi)
    coarse(r2, d2, s0, s1, z2, gy)

    lane2 = lax.broadcasted_iota(jnp.int32, (16, 128), 1) + (32 * gz - 16)
    in2 = jnp.where((lane2 >= 0) & (lane2 < 256), 1.0, 0.0).astype(F32)
    shift = (256 + 16 - 32 * gz) % 256
    for i in range(10):
        p = 4 * gx - 3 + i
        spot = jnp.clip(p + 1, 0, 17)
        plane = pltpu.roll(s0[spot], shift, 1)[4:20, :128]
        wide[16 * i : 16 * i + 16, :] = plane * (in2 * inside_one(p, 16))
    up = dot(wide[...], doubling(128, 128))
    rows1[pl.ds(0, 160, stride=2), :] = up
    rows1[pl.ds(1, 160, stride=2), :] = up
    u[...] = rows1[...].reshape(10, 32, 128)

    mask1 = plane_mask(1, (MY, MZ), HY // 2)

    def remain_one(p):
        c = u[p // 2]
        total = u[(p - 1) // 2] + c + u[(p + 1) // 2]
        rem[p] = (mask1 * x_mask(1, p)) * (left1[p] - d1[p] * c + spread(total))

    loop(3, 17, remain_one)

    def final_one(p):
        r = rem[p]
        box = spread(rem[p - 1] + r + rem[p + 1])
        f = z1[p] + u[p // 2] + (mask1 * x_mask(1, p)) * (CR * r + CA * (d1[p] * r - box))
        zf1[pl.ds(pl.multiple_of((p - 4) * 24, 8), 24), :] = f[4:28]

    loop(4, 16, final_one)

    v_count = 12 * 24
    rowsv[pl.ds(0, v_count, stride=2), :] = zf1[...]
    rowsv[pl.ds(1, v_count, stride=2), :] = zf1[...]
    v[...] = dot(rowsv[...], doubling(128, 256)).reshape(12, 48, 256)

    mask0 = plane_mask(0, (48, EZ), HY - 8)

    def remain(i):
        p = i + 10
        c = v[p // 2 - 4]
        total = v[(p - 1) // 2 - 4] + c + v[(p + 1) // 2 - 4]
        rem0[i] = (mask0 * x_mask(0, p)) * (rs[i] - d0[p, 8:56, :] * c + spread(total))

    loop(0, 20, remain)

    def final(i):
        p = i + 10
        r = rem0[i]
        box = spread(rem0[i - 1] + r + rem0[i + 1])
        zf0[i] = zs[i] + v[p // 2 - 4] + (mask0 * x_mask(0, p)) * (
            CR * r + CA * (d0[p, 8:56, :] * r - box)
        )

    loop(1, 19, final)

    if first:
        acc[...] = jnp.zeros((2, BY, BZ), F32)

    def apply(i):
        c = zf0[i + 2]
        q = d0[i + HX, 8:56, :] * c - spread(zf0[i + 1] + c + zf0[i + 3])
        qc = pltpu.roll(q, EZ - HZ, 1)[8:40, :BZ]
        zc = pltpu.roll(c, EZ - HZ, 1)[8:40, :BZ]
        z_core[i] = zc
        q_core[i] = qc
        if first:
            q_ext[0, i] = q[8:40]
            acc[0] += r_core[i] * zc
            acc[1] += zc * qc

    loop(0, BX, apply)
    if first:
        store_dots(dots, [acc[0], acc[1]])


def store_dots(dots, parts):
    rows = [jnp.sum(part, axis=0, keepdims=True) for part in parts]
    rows.append(jnp.zeros((8 - len(parts), BZ), F32))
    dots[...] = jnp.concatenate(rows, axis=0)


def pick(tile, row):
    return jnp.sum(tile[row : row + 1, :], axis=1, keepdims=True)


def dots_kernel(r, z, q, p, w, sums, dots, acc):
    tile = sums[...]
    alpha = pick(tile, 0) / pick(tile, 1)
    acc[...] = jnp.zeros((3, BY, BZ), F32)

    def body(i):
        qi = q[i]
        z2 = z[i] - alpha * p[i]
        acc[0] += (r[i] - alpha * qi) * z2
        acc[1] += z2 * (qi - alpha * w[i])
        acc[2] += z2 * qi

    loop(0, BX, body)
    store_dots(dots, [acc[0], acc[1], acc[2]])


def end_kernel(r, z, q, p, w, sums, more, solution_field, residual):
    tile, last = sums[...], more[...]
    rz, curve = pick(tile, 0), pick(tile, 1)
    alpha = rz / curve
    rz2 = pick(last, 0)
    beta = rz2 / rz
    alpha2 = rz2 / (pick(last, 1) + 2.0 * beta * pick(last, 2) + beta * beta * curve)

    def body(i):
        zi, qi = z[i], q[i]
        solution_field[i] = alpha * zi + alpha2 * ((zi - alpha * p[i]) + beta * zi)
        residual[i] = (r[i] - alpha * qi) - alpha2 * ((qi - alpha * w[i]) + beta * qi)

    loop(0, BX, body)


def shape(*dims):
    return jax.ShapeDtypeStruct(dims, F32)


def call(kernel, outs, scratch, *args):
    whole = pl.BlockSpec(memory_space=pltpu.VMEM)
    return pl.pallas_call(
        kernel,
        out_shape=outs,
        in_specs=[whole] * len(args),
        out_specs=jax.tree.map(lambda _: whole, outs),
        scratch_shapes=[pltpu.VMEM(s, F32) for s in scratch],
        compiler_params=pltpu.CompilerParams(vmem_limit_bytes=48 * 1024 * 1024),
    )(*args)


def shift(value, axis, count, by):
    return lax.ppermute(value, axis, [(i, (i + by) % count) for i in range(count)])


def exchange_xy(own):
    xlo = shift(own[:, BX - HX :], "gx", GX, 1)
    xhi = shift(own[:, :HX], "gx", GX, -1)
    tall = jnp.concatenate([xlo, own, xhi], axis=1)
    ylo = shift(tall[:, :, BY - HY :], "gy", GY, 1)
    yhi = shift(tall[:, :, :HY], "gy", GY, -1)
    return own, xlo, xhi, ylo, yhi


def all_sum(tile):
    wide = jnp.broadcast_to(tile, (GY * GZ, 8, 128))
    part = lax.all_to_all(wide, ("gy", "gz"), 0, 0).sum(axis=0)
    return part + shift(part, "gx", GX, 1) + shift(part, "gx", GX, 2) + shift(part, "gx", GX, 3)


def spread_coarse(packed):
    own = lax.all_to_all(packed, ("gx", "gz"), 0, 0)
    return shift(own, "gy", GY, 1), own, shift(own, "gy", GY, -1)


def pre_call(pieces, given):
    first = given is None
    kept = (shape(20, 48, EZ), shape(20, 48, EZ), shape(MX, MY, MZ), shape(MX, MY, MZ),
            shape(GX * GZ, 16 if first else 8, 128))
    scratch = [(EX, EY, EZ), (EX, EY, EZ), (MX * EY, EZ), (MX * EY, MZ), (MX, MY, MZ), (16, 128)]
    kernel = functools.partial(pre_kernel, first)
    if first:
        return call(kernel, (shape(EX, EY, EZ), shape(MX, MY, MZ)) + kept, scratch, *pieces)
    return call(kernel, kept, scratch, *pieces, *given)


def post_call(parts, kept, d0, d1, r_core=None, d2=None):
    first = d2 is None
    scratch = [(18, 24, 256)] * 4 + [
        (160, 128), (320, 128), (10, 32, 128), (MX, MY, MZ), (288, 128),
        (576, 128), (12, 48, EZ), (20, 48, EZ), (20, 48, EZ),
    ]
    core = shape(BX, BY, BZ)
    kernel = functools.partial(post_kernel, first)
    if first:
        outs = (shape(18, 24, 256), core, core, shape(1, BX, BY, EZ), shape(8, 128))
        return call(kernel, outs, scratch + [(2, BY, BZ)], *parts, *kept, d0, d1, r_core)
    return call(kernel, (core, core), scratch, *parts, *kept, d0, d1, d2)


def local(right_side, diagonal):
    both = jnp.stack([right_side, diagonal])
    left = shift(both[..., BZ - HZ :], "gz", GZ, 1)
    right = shift(both[..., :HZ], "gz", GZ, -1)
    both = jnp.concatenate([left, both, right], axis=3)
    d0, d1, *kept = pre_call(exchange_xy(both), None)
    d2, z, q, q_ext, dots = post_call(
        spread_coarse(kept[-1]), kept[:-1], d0, d1, r_core=right_side
    )
    sums = all_sum(dots)
    kept = pre_call(exchange_xy(q_ext), (d0, d1))
    p, w = post_call(spread_coarse(kept[-1]), kept[:-1], d0, d1, d2=d2)
    fields = (right_side, z, q, p, w)
    more = call(dots_kernel, shape(8, 128), [(3, BY, BZ)], *fields, sums)
    core = shape(BX, BY, BZ)
    return call(end_kernel, (core, core), [], *fields, sums, all_sum(more))


def solution(mesh):
    return jax.shard_map(
        local, mesh=mesh, in_specs=(SPEC, SPEC), out_specs=(SPEC, SPEC), check_vma=False
    )
```

time: 859 us -> 248 us (0.29); the launches traced: 844 us -> 246 us
  starting transfers between devices: 323 us -> 48 us
  waiting for transfers between devices: 245 us -> 68.7 us
  local copies, waits for them, and re-layouts: 118 us -> 13.2 us
  Pallas kernels: 0 us -> 78.3 us
  blocking collectives: 103 us -> 33.5 us
  other arithmetic: 47 us -> 3.62 us
    ppermute x126 -> x20, starting transfers between devices: 323 us -> 33.1 us  [shift(): lax.ppermute(value, axis, [(i, (i + by) % count) for i in range(count)])]
    ppermute x126 -> x20, waiting for transfers between devices: 245 us -> 64.2 us  [shift(): lax.ppermute(value, axis, [(i, (i + by) % count) for i in range(count)])]
    reshape x13 -> x0, local copies, waits for them, and re-layouts: 92 us -> none  [the longest x5 60.8 us: blocks(): return field.reshape(a // 2, 2, b // 2, 2, c // 2, 2)]
    pallas_call x0 -> x6, Pallas kernels: none -> 78.3 us  [call(): pl.pallas_call(kernel, out_shape=outs, in_specs=[whole] * len(args), out_...]
    psum x8 -> x0, blocking collectives: 64.3 us -> none  [over_axes(): array = lax.psum(array, axis)]
    all_gather x2 -> x0, blocking collectives: 38.4 us -> none  [one_gather(): lines, at, outs = (lax.all_gather(line, axis), 0, [])]
    all_to_all x0 -> x2, blocking collectives: none -> 33.5 us  [the longest x1 18.7 us: all_sum(): part = lax.all_to_all(wide, ('gy', 'gz'), 0, 0).sum(axis=0)]
    reduce_sum x14 -> x2, other arithmetic: 26.7 us -> 1.09 us  [all_sum(): part = lax.all_to_all(wide, ('gy', 'gz'), 0, 0).sum(axis=0)]
  transfers between devices with their start and end apart: 126 -> 22, of which waited for: 74 -> 12; matrix products, arithmetic and copies ran while one was open for 4% -> 1% of each run, Pallas kernels for 0% -> 7%
where the time goes in v1:
time: 248 us; the launch traced here: 246 us
  Pallas kernels  78.3 us (32%)
  waiting for transfers between devices  68.7 us (28%)
  starting transfers between devices  48 us (19%)
  blocking collectives  33.5 us (14%)
  local copies, waits for them, and re-layouts  13.2 us (5%)
  other arithmetic  3.62 us (1%)
    pallas_call x6, Pallas kernels, call(): pl.pallas_call(kernel, out_shape=outs, in_specs=[whole] * len(args), out_...  78.3 us
    ppermute x20, waiting for transfers between devices, shift(): lax.ppermute(value, axis, [(i, (i + by) % count) for i in range(count)])  64.2 us
    ppermute x20, starting transfers between devices, shift(): lax.ppermute(value, axis, [(i, (i + by) % count) for i in range(count)])  33.1 us
    all_to_all x1, blocking collectives, all_sum(): part = lax.all_to_all(wide, ('gy', 'gz'), 0, 0).sum(axis=0)  18.7 us
    all_to_all x1, blocking collectives, spread_coarse(): own = lax.all_to_all(packed, ('gx', 'gz'), 0, 0)  14.8 us
    unnamed x30, local copies, waits for them, and re-layouts  10.7 us
    all_to_all x1, starting transfers between devices, spread_coarse(): own = lax.all_to_all(packed, ('gx', 'gz'), 0, 0)  8 us
    all_to_all x1, starting transfers between devices, all_sum(): part = lax.all_to_all(wide, ('gy', 'gz'), 0, 0).sum(axis=0)  6.94 us
  transfers between devices with their start and end apart: 22, of which 12 were waited for; matrix products, arithmetic and copies ran while one was open for 1% of the time, Pallas kernels for 7%

profile of v1, /device:TPU:1, one launch (start us, length us, event | category | flops | bytes accessed | tf_op | source)
XLA Modules:
  0.0 246.2 jit_solution(15573348339366599315)
XLA Ops:
  0.6 1.5 slice_maximum_fusion
  2.1 2.5 %collective-permute-start = (f32[2,16,32,64]{3,2,1,0:T(8,128)S(1)}, f32[2,16,32,64]{3,2,1,0:T(8,128)S(1)}, u32[]{:S(2)}, u32[]{:S(2)}) collective-permute-start(f32[2,16,32,64]{3,2,1,0:T(8,128)S(1)} %get-tuple-element.48), channel_id=1, source_target_pairs={{0,1},{1,2},{2,3},{3,4},{4,5},{5,6},{6,7},{7,0},{8,9},{9,10},{10,1... | collective-permute-start | bytes 786440 | tf_op jit(solution)/shard_map/ppermute | solution.py:426
  4.6 4.0 %collective-permute-start.1 = (f32[2,16,32,64]{3,2,1,0:T(8,128)S(1)}, f32[2,16,32,64]{3,2,1,0:T(8,128)S(1)}, u32[]{:S(2)}, u32[]{:S(2)}) collective-permute-start(f32[2,16,32,64]{3,2,1,0:T(8,128)S(1)} %get-tuple-element.49), channel_id=1, source_target_pairs={{0,7},{1,0},{2,1},{3,2},{4,3},{5,4},{6,5},{7,6},{8,15},{9,8},{10,9... | collective-permute-start | bytes 786440 | tf_op jit(solution)/shard_map/ppermute | solution.py:426
  8.7 11.6 %collective-permute-done = f32[2,16,32,64]{3,2,1,0:T(8,128)S(1)} collective-permute-done((f32[2,16,32,64]{3,2,1,0:T(8,128)S(1)}, f32[2,16,32,64]{3,2,1,0:T(8,128)S(1)}, u32[]{:S(2)}, u32[]{:S(2)}) %collective-permute-start) | collective-permute-done | bytes 262176 | tf_op jit(solution)/shard_map/ppermute | solution.py:426
  20.9 2.6 %collective-permute-start.3 = (f32[2,12,32,256]{3,2,1,0:T(8,128)S(1)}, f32[2,12,32,256]{3,2,1,0:T(8,128)S(1)}, u32[]{:S(2)}, u32[]{:S(2)}) collective-permute-start(f32[2,12,32,256]{3,2,1,0:T(8,128)S(1)} %get-tuple-element.44), channel_id=1, source_target_pairs={{0,192},{64,0},{128,64},{192,128},{1,193},{65,1},{129,65},{193,129... | collective-permute-start | bytes 2359304 | tf_op jit(solution)/shard_map/ppermute | solution.py:426
  23.5 15.6 %collective-permute-done.3.xhi = f32[2,12,32,256]{3,2,1,0:T(8,128)S(1)} collective-permute-done((f32[2,12,32,256]{3,2,1,0:T(8,128)S(1)}, f32[2,12,32,256]{3,2,1,0:T(8,128)S(1)}, u32[]{:S(2)}, u32[]{:S(2)}) %collective-permute-start.3) | collective-permute-done | bytes 786464 | tf_op jit(solution)/shard_map/ppermute | solution.py:426
  39.1 3.1 %collective-permute-done.2.xlo = f32[2,12,32,256]{3,2,1,0:T(8,128)S(1)} collective-permute-done((f32[2,12,32,256]{3,2,1,0:T(8,128)S(1)}, f32[2,12,32,256]{3,2,1,0:T(8,128)S(1)}, u32[]{:S(2)}, u32[]{:S(2)}) %collective-permute-start.2) | collective-permute-done | bytes 786464 | tf_op jit(solution)/shard_map/ppermute | solution.py:426
  43.1 2.4 collective-permute-start.5
  45.6 1.2 collective-permute-start.4
  46.8 15.6 %collective-permute-done.5.yhi = f32[2,40,16,256]{3,2,1,0:T(8,128)S(1)} collective-permute-done((f32[2,40,16,256]{3,2,1,0:T(8,128)S(1)}, f32[2,40,16,256]{3,2,1,0:T(8,128)S(1)}, u32[]{:S(2)}, u32[]{:S(2)}) %collective-permute-start.5) | collective-permute-done | bytes 1310752 | tf_op jit(solution)/shard_map/ppermute | solution.py:426
  62.4 1.1 copy-done.12
  63.5 1.1 copy-done.13
  64.5 21.4 %shard_map.41 = (f32[40,64,256]{2,1,0:T(8,128)}, f32[20,32,128]{2,1,0:T(8,128)S(1)}, f32[20,48,256]{2,1,0:T(8,128)S(1)}, f32[20,48,256]{2,1,0:T(8,128)S(1)}, f32...) custom-call(f32[2,16,32,256]{3,2,1,0:T(8,128)S(1)} %pad_maximum_fusion.1.own, ...), custom_call_target="tpu_custom_call" | custom-call | tf_op jit(solution)/shard_map/pallas_call | solution.py:415
  86.0 14.8 %all_to_all.20.refs_1_ = f32[32,16,128]{2,1,0:T(8,128)S(1)} all-to-all(f32[32,16,128]{2,1,0:T(8,128)S(1)} %get-tuple-element.21), channel_id=1, replica_groups=mesh['gx'=4,'gy'=8,'gz'=8] {'gx','gz'}, dimensions={0} | all-to-all | bytes 524288 | tf_op jit(solution)/shard_map/all_to_all | solution.py:445
  100.8 3.7 %collective-permute-start.7 = (f32[32,16,128]{2,1,0:T(8,128)S(1)}, f32[32,16,128]{2,1,0:T(8,128)S(1)}, u32[]{:S(2)}, u32[]{:S(2)}) collective-permute-start(f32[32,16,128]{2,1,0:T(8,128)S(1)} %all_to_all.20.refs_1_), channel_id=1, source_target_pairs={{0,56},{8,0},{16,8},{24,16},{32,24},{40,32},{48,40},{56,48},{1,57}... | collective-permute-start | bytes 786440 | tf_op jit(solution)/shard_map/ppermute | solution.py:426
  104.5 4.3 %collective-permute-done.7.refs_2_ = f32[32,16,128]{2,1,0:T(8,128)S(1)} collective-permute-done((f32[32,16,128]{2,1,0:T(8,128)S(1)}, f32[32,16,128]{2,1,0:T(8,128)S(1)}, u32[]{:S(2)}, u32[]{:S(2)}) %collective-permute-start.7) | collective-permute-done | bytes 262176 | tf_op jit(solution)/shard_map/ppermute | solution.py:426
  108.8 19.1 %shard_map.42 = (f32[18,24,256]{2,1,0:T(8,128)S(1)}, f32[16,32,128]{2,1,0:T(8,128)S(1)}, f32[16,32,128]{2,1,0:T(8,128)S(1)}, f32[1,16,32,256]{3,2,1,0:T(8,128)S(1)}, f32[8,128]{1,0:T(8,128)S(1)}) custom-call(f32[32,16,128]{2,1,0:T(8,128)S(1)} %collective-permute-done.6.refs_0_, f32[32,16,128]{2,1,0:T(8,128)S(1)} %all_to_all.20.refs_1_, ...), custom_call_target="tpu_custom_call" | custom-call | tf_op jit(solution)/shard_map/pallas_call | solution.py:415
  128.5 2.4 collective-permute-start.9
  130.9 6.5 %collective-permute-done.8.xlo = f32[1,12,32,256]{3,2,1,0:T(8,128)S(1)} collective-permute-done((f32[1,12,32,256]{3,2,1,0:T(8,128)S(1)}, f32[1,12,32,256]{3,2,1,0:T(8,128)S(1)}, u32[]{:S(2)}, u32[]{:S(2)}) %collective-permute-start.8) | collective-permute-done | bytes 393248 | tf_op jit(solution)/shard_map/ppermute | solution.py:426
  137.5 1.2 fusion.1
  138.7 3.6 %collective-permute-start.11 = (f32[1,40,16,256]{3,2,1,0:T(8,128)}, f32[1,40,16,256]{3,2,1,0:T(8,128)S(1)}, u32[]{:S(2)}, u32[]{:S(2)}) collective-permute-start(f32[1,40,16,256]{3,2,1,0:T(8,128)} %get-tuple-element.42), channel_id=1, source_target_pairs={{0,56},{8,0},{16,8},{24,16},{32,24},{40,32},{48,40},{56,48},{1,57}... | collective-permute-start | bytes 1966088 | tf_op jit(solution)/shard_map/ppermute | solution.py:426
  142.3 1.1 collective-permute-start.10
  143.3 0.7 broadcast_in_dim.6
  144.1 6.9 %all-to-all-start.2 = ((f32[64,8,128]{2,1,0:T(8,128)}), f32[64,8,128]{2,1,0:T(8,128)}, u32[]{:S(2)}, u32[]{:S(2)}) async-start(f32[64,8,128]{2,1,0:T(8,128)} %broadcast_in_dim.6), calls=%async_computation.2 | async-start | bytes 524288 | tf_op jit(solution)/shard_map/all_to_all | solution.py:440
  151.0 1.2 collective-permute-done.11.yhi
  152.2 0.8 copy-done.3
  153.1 1.1 copy-done.4
  154.2 16.7 %shard_map.43 = (f32[20,48,256]{2,1,0:T(8,128)S(1)}, f32[20,48,256]{2,1,0:T(8,128)S(1)}, f32[20,32,128]{2,1,0:T(8,128)S(1)}, f32[20,32,128]{2,1,0:T(8,128)S(1)}, f32[32,8,128]{2,1,0:T(8,128)}) custom-call(f32[1,16,32,256]{3,2,1,0:T(8,128)S(1)} %get-tuple-element.30.own, f32[1,12,32,256]{3,2,1,0:T(8,128)S(1)} %collective-permute-done.8.xlo, ...), custom_call_target="tpu_custom_call" | custom-call | tf_op jit(solution)/shard_map/pallas_call | solution.py:415
  170.8 1.0 copy-done.1
  173.2 8.0 %all-to-all-start.1 = ((f32[32,8,128]{2,1,0:T(8,128)}), f32[32,8,128]{2,1,0:T(8,128)S(1)}, u32[]{:S(2)}, u32[]{:S(2)}) async-start(f32[32,8,128]{2,1,0:T(8,128)} %get-tuple-element.31), calls=%async_computation.1 | async-start | bytes 262144 | tf_op jit(solution)/shard_map/all_to_all | solution.py:445
  181.2 1.0 reduce_sum.18
  182.2 2.6 %collective-permute-start.16 = (f32[8,128]{1,0:T(8,128)S(1)}, f32[8,128]{1,0:T(8,128)S(1)}, u32[]{:S(2)}, u32[]{:S(2)}) collective-permute-start(f32[8,128]{1,0:T(8,128)S(1)} %reduce_sum.18), channel_id=1, source_target_pairs={{0,192},{64,0},{128,64},{192,128},{1,193},{65,1},{129,65},{193,129... | collective-permute-start | bytes 12296 | tf_op jit(solution)/shard_map/ppermute | solution.py:426
  185.9 4.5 %all-to-all-done.1.refs_1_ = f32[32,8,128]{2,1,0:T(8,128)S(1)} async-done(((f32[32,8,128]{2,1,0:T(8,128)}), f32[32,8,128]{2,1,0:T(8,128)S(1)}, u32[]{:S(2)}, u32[]{:S(2)}) %all-to-all-start.1) | async-done | bytes 131104 | tf_op jit(solution)/shard_map/all_to_all | solution.py:445
  190.4 2.1 collective-permute-start.13
  192.5 1.1 collective-permute-start.12
  193.6 2.6 %collective-permute-done.13.refs_2_ = f32[32,8,128]{2,1,0:T(8,128)S(1)} collective-permute-done((f32[32,8,128]{2,1,0:T(8,128)S(1)}, f32[32,8,128]{2,1,0:T(8,128)S(1)}, u32[]{:S(2)}, u32[]{:S(2)}) %collective-permute-start.13) | collective-permute-done | bytes 131104 | tf_op jit(solution)/shard_map/ppermute | solution.py:426
  196.2 1.2 copy-done.2
  197.4 1.0 copy-done.6
  198.5 1.0 copy-done.8
  199.4 1.0 copy-done.10
  200.4 18.7 %shard_map.44 = (f32[16,32,128]{2,1,0:T(8,128)S(1)}, f32[16,32,128]{2,1,0:T(8,128)S(1)}) custom-call(f32[32,8,128]{2,1,0:T(8,128)S(1)} %collective-permute-done.12.refs_0_, f32[32,8,128]{2,1,0:T(8,128)S(1)} %all-to-all-done.1.refs_1_, f32[32,8,128]{2,1,0:T(8,128)S(1)} %collective-permute-done.13.refs_2_, f32[20,48,256]{2,1,0:T(8,128)S(1)} %get-tuple-element.32.refs_3_, ...), custom_call_target="tpu_custom_call" | custom-call | tf_op jit(solution)/shard_map/pallas_call | solution.py:415
  219.1 0.8 shard_map.45
  220.0 18.7 %all_to_all.21 = f32[64,8,128]{2,1,0:T(8,128)S(1)} all-to-all(f32[64,8,128]{2,1,0:T(8,128)S(1)} %broadcast_in_dim.7), channel_id=1, replica_groups=mesh['gx'=4,'gy'=8,'gz'=8] {'gy','gz'}, dimensions={0} | all-to-all | bytes 524288 | tf_op jit(solution)/shard_map/all_to_all | solution.py:440
  238.7 1.0 collective-permute-start.19
  239.7 1.2 collective-permute-start.18
  241.3 2.4 collective-permute-done.18
  243.7 0.9 collective-permute-done.17
  244.6 1.6 shard_map.46
  (48 shorter events, 5.4 us)
Async XLA Ops:
  0.6 19.6 %copy-start = (f32[16,32,128]{2,1,0:T(8,128)S(1)}, f32[16,32,128]{2,1,0:T(8,128)}, u32[]{:S(2)}) copy-start(f32[16,32,128]{2,1,0:T(8,128)} %r.3) | copy-start | bytes 786436
  0.6 19.6 %copy-start.11 = (f32[16,32,128]{2,1,0:T(8,128)S(1)}, f32[16,32,128]{2,1,0:T(8,128)}, u32[]{:S(2)}) copy-start(f32[16,32,128]{2,1,0:T(8,128)} %param.3) | copy-start | bytes 786436
  2.1 18.1 %collective-permute-start = (f32[2,16,32,64]{3,2,1,0:T(8,128)S(1)}, f32[2,16,32,64]{3,2,1,0:T(8,128)S(1)}, u32[]{:S(2)}, u32[]{:S(2)}) collective-permute-start(f32[2,16,32,64]{3,2,1,0:T(8,128)S(1)} %get-tuple-element.48), channel_id=1, source_target_pairs={{0,1},{1,2},{2,3},{3,4},{4,5},{5,6},{6,7},{7,0},{8,9},{9,10},{10,1... | collective-permute-start | bytes 786440 | tf_op jit(solution)/shard_map/ppermute | solution.py:426
  4.6 15.6 %collective-permute-start.1 = (f32[2,16,32,64]{3,2,1,0:T(8,128)S(1)}, f32[2,16,32,64]{3,2,1,0:T(8,128)S(1)}, u32[]{:S(2)}, u32[]{:S(2)}) collective-permute-start(f32[2,16,32,64]{3,2,1,0:T(8,128)S(1)} %get-tuple-element.49), channel_id=1, source_target_pairs={{0,7},{1,0},{2,1},{3,2},{4,3},{5,4},{6,5},{7,6},{8,15},{9,8},{10,9... | collective-permute-start | bytes 786440 | tf_op jit(solution)/shard_map/ppermute | solution.py:426
  20.9 18.2 %collective-permute-start.3 = (f32[2,12,32,256]{3,2,1,0:T(8,128)S(1)}, f32[2,12,32,256]{3,2,1,0:T(8,128)S(1)}, u32[]{:S(2)}, u32[]{:S(2)}) collective-permute-start(f32[2,12,32,256]{3,2,1,0:T(8,128)S(1)} %get-tuple-element.44), channel_id=1, source_target_pairs={{0,192},{64,0},{128,64},{192,128},{1,193},{65,1},{129,65},{193,129... | collective-permute-start | bytes 2359304 | tf_op jit(solution)/shard_map/ppermute | solution.py:426
  23.5 18.7 %collective-permute-start.2 = (f32[2,12,32,256]{3,2,1,0:T(8,128)S(1)}, f32[2,12,32,256]{3,2,1,0:T(8,128)S(1)}, u32[]{:S(2)}, u32[]{:S(2)}) collective-permute-start(f32[2,12,32,256]{3,2,1,0:T(8,128)S(1)} %get-tuple-element.45), channel_id=1, source_target_pairs={{0,64},{64,128},{128,192},{192,0},{1,65},{65,129},{129,193},{193,1... | collective-permute-start | bytes 2359304 | tf_op jit(solution)/shard_map/ppermute | solution.py:426
  43.1 19.2 %collective-permute-start.5 = (f32[2,40,16,256]{3,2,1,0:T(8,128)S(1)}, f32[2,40,16,256]{3,2,1,0:T(8,128)S(1)}, u32[]{:S(2)}, u32[]{:S(2)}) collective-permute-start(f32[2,40,16,256]{3,2,1,0:T(8,128)S(1)} %get-tuple-element.40), channel_id=1, source_target_pairs={{0,56},{8,0},{16,8},{24,16},{32,24},{40,32},{48,40},{56,48},{1,57}... | collective-permute-start | bytes 3932168 | tf_op jit(solution)/shard_map/ppermute | solution.py:426
  45.6 16.8 %collective-permute-start.4 = (f32[2,40,16,256]{3,2,1,0:T(8,128)S(1)}, f32[2,40,16,256]{3,2,1,0:T(8,128)S(1)}, u32[]{:S(2)}, u32[]{:S(2)}) collective-permute-start(f32[2,40,16,256]{3,2,1,0:T(8,128)S(1)} %get-tuple-element.41), channel_id=1, source_target_pairs={{0,8},{8,16},{16,24},{24,32},{32,40},{40,48},{48,56},{56,0},{1,9},... | collective-permute-start | bytes 3932168 | tf_op jit(solution)/shard_map/ppermute | solution.py:426
  62.4 1.1 copy-start.12
  63.5 1.1 copy-start.13
  100.8 8.0 %collective-permute-start.7 = (f32[32,16,128]{2,1,0:T(8,128)S(1)}, f32[32,16,128]{2,1,0:T(8,128)S(1)}, u32[]{:S(2)}, u32[]{:S(2)}) collective-permute-start(f32[32,16,128]{2,1,0:T(8,128)S(1)} %all_to_all.20.refs_1_), channel_id=1, source_target_pairs={{0,56},{8,0},{16,8},{24,16},{32,24},{40,32},{48,40},{56,48},{1,57}... | collective-permute-start | bytes 786440 | tf_op jit(solution)/shard_map/ppermute | solution.py:426
  104.5 4.4 %collective-permute-start.6 = (f32[32,16,128]{2,1,0:T(8,128)S(1)}, f32[32,16,128]{2,1,0:T(8,128)S(1)}, u32[]{:S(2)}, u32[]{:S(2)}) collective-permute-start(f32[32,16,128]{2,1,0:T(8,128)S(1)} %all_to_all.20.refs_1_), channel_id=1, source_target_pairs={{0,8},{8,16},{16,24},{24,32},{32,40},{40,48},{48,56},{56,0},{1,9},... | collective-permute-start | bytes 786440 | tf_op jit(solution)/shard_map/ppermute | solution.py:426
  127.9 9.6 %copy-start.5 = (f32[18,24,256]{2,1,0:T(8,128)}, f32[18,24,256]{2,1,0:T(8,128)S(1)}, u32[]{:S(2)}) copy-start(f32[18,24,256]{2,1,0:T(8,128)S(1)} %get-tuple-element.36.refs_9_) | copy-start | bytes 1327108
  128.0 9.4 %collective-permute-start.8 = (f32[1,12,32,256]{3,2,1,0:T(8,128)S(1)}, f32[1,12,32,256]{3,2,1,0:T(8,128)S(1)}, u32[]{:S(2)}, u32[]{:S(2)}) collective-permute-start(f32[1,12,32,256]{3,2,1,0:T(8,128)S(1)} %get-tuple-element.47), channel_id=1, source_target_pairs={{0,64},{64,128},{128,192},{192,0},{1,65},{65,129},{129,193},{193,1... | collective-permute-start | bytes 1179656 | tf_op jit(solution)/shard_map/ppermute | solution.py:426
  128.5 8.9 %collective-permute-start.9 = (f32[1,12,32,256]{3,2,1,0:T(8,128)S(1)}, f32[1,12,32,256]{3,2,1,0:T(8,128)S(1)}, u32[]{:S(2)}, u32[]{:S(2)}) collective-permute-start(f32[1,12,32,256]{3,2,1,0:T(8,128)S(1)} %get-tuple-element.46), channel_id=1, source_target_pairs={{0,192},{64,0},{128,64},{192,128},{1,193},{65,1},{129,65},{193,129... | collective-permute-start | bytes 1179656 | tf_op jit(solution)/shard_map/ppermute | solution.py:426
  138.7 13.5 %collective-permute-start.11 = (f32[1,40,16,256]{3,2,1,0:T(8,128)}, f32[1,40,16,256]{3,2,1,0:T(8,128)S(1)}, u32[]{:S(2)}, u32[]{:S(2)}) collective-permute-start(f32[1,40,16,256]{3,2,1,0:T(8,128)} %get-tuple-element.42), channel_id=1, source_target_pairs={{0,56},{8,0},{16,8},{24,16},{32,24},{40,32},{48,40},{56,48},{1,57}... | collective-permute-start | bytes 1966088 | tf_op jit(solution)/shard_map/ppermute | solution.py:426
  142.3 10.8 %collective-permute-start.10 = (f32[1,40,16,256]{3,2,1,0:T(8,128)}, f32[1,40,16,256]{3,2,1,0:T(8,128)}, u32[]{:S(2)}, u32[]{:S(2)}) collective-permute-start(f32[1,40,16,256]{3,2,1,0:T(8,128)} %get-tuple-element.43), channel_id=1, source_target_pairs={{0,8},{8,16},{16,24},{24,32},{32,40},{40,48},{48,56},{56,0},{1,9},... | collective-permute-start | bytes 1966088 | tf_op jit(solution)/shard_map/ppermute | solution.py:426
  144.1 29.2 %all-to-all-start.2 = ((f32[64,8,128]{2,1,0:T(8,128)}), f32[64,8,128]{2,1,0:T(8,128)}, u32[]{:S(2)}, u32[]{:S(2)}) async-start(f32[64,8,128]{2,1,0:T(8,128)} %broadcast_in_dim.6), calls=%async_computation.2 | async-start | bytes 524288 | tf_op jit(solution)/shard_map/all_to_all | solution.py:440
  152.2 0.8 copy-start.3
  153.1 1.1 copy-start.4
  170.8 1.0 copy-start.1
  171.8 0.7 copy-start.7
  172.5 0.7 copy-start.9
  173.2 17.2 %all-to-all-start.1 = ((f32[32,8,128]{2,1,0:T(8,128)}), f32[32,8,128]{2,1,0:T(8,128)S(1)}, u32[]{:S(2)}, u32[]{:S(2)}) async-start(f32[32,8,128]{2,1,0:T(8,128)} %get-tuple-element.31), calls=%async_computation.1 | async-start | bytes 262144 | tf_op jit(solution)/shard_map/all_to_all | solution.py:445
  182.2 11.3 %collective-permute-start.16 = (f32[8,128]{1,0:T(8,128)S(1)}, f32[8,128]{1,0:T(8,128)S(1)}, u32[]{:S(2)}, u32[]{:S(2)}) collective-permute-start(f32[8,128]{1,0:T(8,128)S(1)} %reduce_sum.18), channel_id=1, source_target_pairs={{0,192},{64,0},{128,64},{192,128},{1,193},{65,1},{129,65},{193,129... | collective-permute-start | bytes 12296 | tf_op jit(solution)/shard_map/ppermute | solution.py:426
  184.8 8.8 %collective-permute-start.15 = (f32[8,128]{1,0:T(8,128)S(1)}, f32[8,128]{1,0:T(8,128)S(1)}, u32[]{:S(2)}, u32[]{:S(2)}) collective-permute-start(f32[8,128]{1,0:T(8,128)S(1)} %reduce_sum.18), channel_id=1, source_target_pairs={{0,128},{64,192},{128,0},{192,64},{1,129},{65,193},{129,1},{193,65... | collective-permute-start | bytes 12296 | tf_op jit(solution)/shard_map/ppermute | solution.py:426
  185.3 8.3 %collective-permute-start.14 = (f32[8,128]{1,0:T(8,128)S(1)}, f32[8,128]{1,0:T(8,128)S(1)}, u32[]{:S(2)}, u32[]{:S(2)}) collective-permute-start(f32[8,128]{1,0:T(8,128)S(1)} %reduce_sum.18), channel_id=1, source_target_pairs={{0,64},{64,128},{128,192},{192,0},{1,65},{65,129},{129,193},{193,1... | collective-permute-start | bytes 12296 | tf_op jit(solution)/shard_map/ppermute | solution.py:426
  190.4 5.9 %collective-permute-start.13 = (f32[32,8,128]{2,1,0:T(8,128)S(1)}, f32[32,8,128]{2,1,0:T(8,128)S(1)}, u32[]{:S(2)}, u32[]{:S(2)}) collective-permute-start(f32[32,8,128]{2,1,0:T(8,128)S(1)} %all-to-all-done.1.refs_1_), channel_id=1, source_target_pairs={{0,56},{8,0},{16,8},{24,16},{32,24},{40,32},{48,40},{56,48},{1,57}... | collective-permute-start | bytes 393224 | tf_op jit(solution)/shard_map/ppermute | solution.py:426
  192.5 3.8 %collective-permute-start.12 = (f32[32,8,128]{2,1,0:T(8,128)S(1)}, f32[32,8,128]{2,1,0:T(8,128)S(1)}, u32[]{:S(2)}, u32[]{:S(2)}) collective-permute-start(f32[32,8,128]{2,1,0:T(8,128)S(1)} %all-to-all-done.1.refs_1_), channel_id=1, source_target_pairs={{0,8},{8,16},{16,24},{24,32},{32,40},{40,48},{48,56},{56,0},{1,9},... | collective-permute-start | bytes 393224 | tf_op jit(solution)/shard_map/ppermute | solution.py:426
  196.2 1.2 copy-start.2
  197.4 1.0 copy-start.6
  198.5 1.0 copy-start.8
  199.4 1.0 copy-start.10
  238.7 2.5 %collective-permute-start.19 = (f32[8,128]{1,0:T(8,128)S(1)}, f32[8,128]{1,0:T(8,128)S(1)}, u32[]{:S(2)}, u32[]{:S(2)}) collective-permute-start(f32[8,128]{1,0:T(8,128)S(1)} %reduce_sum.19), channel_id=1, source_target_pairs={{0,192},{64,0},{128,64},{192,128},{1,193},{65,1},{129,65},{193,129... | collective-permute-start | bytes 12296 | tf_op jit(solution)/shard_map/ppermute | solution.py:426
  239.7 4.0 %collective-permute-start.18 = (f32[8,128]{1,0:T(8,128)S(1)}, f32[8,128]{1,0:T(8,128)S(1)}, u32[]{:S(2)}, u32[]{:S(2)}) collective-permute-start(f32[8,128]{1,0:T(8,128)S(1)} %reduce_sum.19), channel_id=1, source_target_pairs={{0,128},{64,192},{128,0},{192,64},{1,129},{65,193},{129,1},{193,65... | collective-permute-start | bytes 12296 | tf_op jit(solution)/shard_map/ppermute | solution.py:426
  240.9 3.7 %collective-permute-start.17 = (f32[8,128]{1,0:T(8,128)S(1)}, f32[8,128]{1,0:T(8,128)S(1)}, u32[]{:S(2)}, u32[]{:S(2)}) collective-permute-start(f32[8,128]{1,0:T(8,128)S(1)} %reduce_sum.19), channel_id=1, source_target_pairs={{0,64},{64,128},{128,192},{192,0},{1,65},{65,129},{129,193},{193,1... | collective-permute-start | bytes 12296 | tf_op jit(solution)/shard_map/ppermute | solution.py:426

commit v2 on v1

--- a/solution.py
+++ b/solution.py
@@ -13,7 +13,6 @@
 EX, EY, EZ = BX + 2 * HX, BY + 2 * HY, BZ + 2 * HZ
 MX, MY, MZ = EX // 2, EY // 2, EZ // 2
 F32 = jnp.float32
-HIGH = lax.Precision.HIGHEST
 SPEC = P("gx", "gy", "gz")
 
 
@@ -61,12 +60,9 @@
     return inside_one(gx * (BX // size) - HX // size + plane, GX * BX // size)
 
 
-def loop(first, last, body, unroll=1):
-    def step(i, carry):
+def loop(first, last, body):
+    for i in range(first, last):
         body(i)
-        return carry
-
-    lax.fori_loop(first, last, step, 0, unroll=unroll)
 
 
 def halving(rows, cols, per=2):
@@ -82,21 +78,160 @@
 
 
 def dot(a, b):
-    return jnp.dot(a, b, precision=HIGH, preferred_element_type=F32)
-
-
-def assemble(dst, which, own, xlo, xhi, ylo, yhi, change):
-    def part(src, base, count, lo, hi):
-        def body(i):
-            dst[base + i, lo:hi, :] = change(src[which, i], base + i, lo, hi)
-
-        loop(0, count, body)
-
-    part(own, HX, BX, HY, HY + BY)
-    part(xlo, 0, HX, HY, HY + BY)
-    part(xhi, HX + BX, HX, HY, HY + BY)
-    part(ylo, 0, EX, 0, HY)
-    part(yhi, 0, EX, HY + BY, EY)
+    b = b.astype(jnp.bfloat16)
+    hi = a.astype(jnp.bfloat16)
+    a = a - hi.astype(F32)
+    mid = a.astype(jnp.bfloat16)
+    lo = (a - mid.astype(F32)).astype(jnp.bfloat16)
+    one = functools.partial(jnp.dot, preferred_element_type=F32)
+    return one(hi, b) + one(mid, b) + one(lo, b)
+
+
+def join(center, left, right, first, last):
+    lane = lax.broadcasted_iota(jnp.int32, center.shape, 1)
+    turned = pltpu.roll(center, HZ, 1)
+    low = jnp.where(lane >= HZ, turned, jnp.where(lane >= first, left, 0.0))
+    high = jnp.where(lane < HZ, turned, jnp.where(lane < last, right, 0.0))
+    return low, high
+
+
+def half_tile(src, base, plane, upper):
+    tile = src[base + plane // 2]
+    return tile if plane % 2 == upper else pltpu.roll(tile, 4, 0)
+
+
+def assemble(dst, parts, change):
+    for p in range(EX):
+        for lo, hi, (center, left, right, first, last) in parts(p):
+            low, high = join(center, left, right, first, last)
+            dst[p, lo:hi, 0:128] = change(low, p, lo, hi, 0)
+            dst[p, lo:hi, 128:256] = change(high, p, lo, hi, 128)
+
+
+def turn(tile, by):
+    by = by % 128
+    return pltpu.roll(tile, by, 1) if by else tile
+
+
+def x_plane(own, xlo, xhi, p):
+    if p < HX:
+        return xlo(p)
+    return own(p - HX) if p < HX + BX else xhi(p - HX - BX)
+
+
+def first_parts(a, own, xlo, xhi, zl, zr, ylo, yhi):
+    base = a * 90
+
+    def parts(p):
+        g, k = p // 4, p % 4
+        sides = lambda l, r: (turn(l, 32 - 32 * k), turn(r, 64 - 32 * k), 32, 96)
+        center = x_plane(
+            lambda i: own[i], lambda i: xlo[a, i], lambda i: xhi[a, i], p
+        )
+        whole = lambda y: (y[base + p], *sides(y[base + 40 + g], y[base + 50 + g]))
+        half = lambda y, upper: (
+            half_tile(y, base + 60, p, upper),
+            *sides(
+                half_tile(y, base + 60, 40 + g, upper), half_tile(y, base + 60, 50 + g, upper)
+            ),
+        )
+        return [
+            (0, 8, half(ylo, 1)),
+            (8, 16, whole(ylo)),
+            (16, 48, (center, *sides(zl[a, g], zr[a, g]))),
+            (48, 56, whole(yhi)),
+            (56, 64, half(yhi, 0)),
+        ]
+
+    return parts
+
+
+def later_parts(own, halo, xlo, xhi, ylo, yhi):
+    def parts(p):
+        g, k = p // 4, p % 4
+        sides = lambda h: (turn(h, 48 - 32 * k),) * 2 + (48, 80)
+        center = x_plane(lambda i: own[i], lambda i: xlo[i], lambda i: xhi[i], p)
+        side = x_plane(
+            lambda i: halo[i // 4], lambda i: xlo[12 + i // 4], lambda i: xhi[12 + i // 4], p
+        )
+        whole = lambda y: (y[p], *sides(y[40 + g]))
+        half = lambda y, upper: (
+            half_tile(y, 50, p, upper), *sides(half_tile(y, 50, 40 + g, upper))
+        )
+        return [
+            (0, 8, half(ylo, 1)),
+            (8, 16, whole(ylo)),
+            (16, 48, (center, *sides(side))),
+            (48, 56, whole(yhi)),
+            (56, 64, half(yhi, 0)),
+        ]
+
+    return parts
+
+
+def z_pack_kernel(right_side, diagonal, xlo, xhi, down, up):
+    group = lax.broadcasted_iota(jnp.int32, (BY, BZ), 1) // 32
+    for a, own in enumerate((right_side, diagonal)):
+        for g in range(EX // 4):
+            low = high = None
+            for k in range(4):
+                src = x_plane(
+                    lambda i: own[i], lambda i: xlo[a, i], lambda i: xhi[a, i], 4 * g + k
+                )
+                first, last = turn(src, 32 * k), turn(src, 32 * k - 96)
+                low = first if k == 0 else jnp.where(group == k, first, low)
+                high = last if k == 0 else jnp.where(group == k, last, high)
+            down[a, g] = low
+            up[a, g] = high
+
+
+def y_rows(planes, base, down, up):
+    count = len(planes)
+    for m, plane in enumerate(planes):
+        down[base + m] = plane(0, 8)
+        up[base + m] = plane(24, 32)
+    for m in range(0, count, 2):
+        one, two = planes[m], planes[m + 1]
+        at = base + count + m // 2
+        down[at] = jnp.concatenate([one(8, 12), two(8, 12)], axis=0)
+        up[at] = jnp.concatenate([one(20, 24), two(20, 24)], axis=0)
+
+
+def y_pack_kernel(right_side, diagonal, xlo, xhi, zl, zr, down, up):
+    def rows(ref, *index):
+        return lambda lo, hi: ref[(*index, slice(lo, hi))]
+
+    for a, own in enumerate((right_side, diagonal)):
+        planes = [
+            x_plane(
+                lambda i: rows(own, i), lambda i: rows(xlo, a, i), lambda i: rows(xhi, a, i), p
+            )
+            for p in range(EX)
+        ]
+        planes += [rows(zl, a, g) for g in range(10)] + [rows(zr, a, g) for g in range(10)]
+        y_rows(planes, 90 * a, down, up)
+
+
+def y_pack_later_kernel(own, halo, xlo, xhi, dots, down, up):
+    def rows(ref, index):
+        return lambda lo, hi: ref[index, lo:hi]
+
+    planes = [
+        x_plane(lambda i: rows(own, i), lambda i: rows(xlo, i), lambda i: rows(xhi, i), p)
+        for p in range(EX)
+    ]
+    planes += [
+        x_plane(
+            lambda i: rows(halo, i // 4),
+            lambda i: rows(xlo, 12 + i // 4),
+            lambda i: rows(xhi, 12 + i // 4),
+            4 * g,
+        )
+        for g in range(10)
+    ]
+    y_rows(planes, 0, down, up)
+    down[75] = dots[...]
+    up[75] = dots[...]
 
 
 def halve(scratch, rows_scratch, z_map):
@@ -105,21 +240,29 @@
     return rows_scratch[pl.ds(0, count, stride=2), :] + rows_scratch[pl.ds(1, count, stride=2), :]
 
 
-def pre_kernel(first, own, xlo, xhi, ylo, yhi, *refs):
+def pre_kernel(first, *refs):
+    if first:
+        right_side, diagonal, xlo, xhi, zl, zr, ylo, yhi = refs[:8]
+        refs = refs[8:]
+        r_parts = first_parts(0, right_side, xlo, xhi, zl, zr, ylo, yhi)
+        d_parts = first_parts(1, diagonal, xlo, xhi, zl, zr, ylo, yhi)
+    else:
+        own, halo, xlo, xhi, ylo, yhi, dots = refs[:7]
+        refs = refs[7:]
+        r_parts = later_parts(own, halo, xlo, xhi, ylo, yhi)
     d0, d1, zs, rs, z1, left1, packed, field, zfull, pairs, rows, r1, small = refs
-    gx, gy, gz = places()
     mask = plane_mask(0, (EY, EZ), HY)
     z_map = halving(EZ, MZ)
 
     assemble(
-        field, 0, own, xlo, xhi, ylo, yhi,
-        lambda v, p, lo, hi: v * (mask[lo:hi] * x_mask(0, p)),
+        field, r_parts,
+        lambda v, p, lo, hi, at: v * (mask[lo:hi, at : at + 128] * x_mask(0, p)),
     )
     if first:
-        assemble(d0, 1, own, xlo, xhi, ylo, yhi, lambda v, p, lo, hi: v + 27.0)
+        assemble(d0, d_parts, lambda v, p, lo, hi, at: v + 27.0)
 
         def add_pair(i):
-            pairs[pl.ds(pl.multiple_of(i * EY, EY), EY), :] = d0[2 * i] + d0[2 * i + 1]
+            pairs[i * EY : (i + 1) * EY, :] = d0[2 * i] + d0[2 * i + 1]
 
         loop(0, MX, add_pair)
         d1[...] = (halve(pairs, rows, z_map) * 0.125).reshape(MX, MY, MZ)
@@ -140,10 +283,9 @@
 
     def rest_pair(i):
         a, b = rest(2 * i), rest(2 * i + 1)
-        pairs[pl.ds(pl.multiple_of(i * EY, EY), EY), :] = a + b
-
-        @pl.when((i >= 5) & (i < 15))
-        def _():
+        pairs[i * EY : (i + 1) * EY, :] = a + b
+
+        if 5 <= i < 15:
             rs[2 * i - 10] = a[8:56]
             rs[2 * i - 9] = b[8:56]
 
@@ -193,7 +335,11 @@
 
     tile = pack(left1, 0.5)
     if first:
-        tile = jnp.concatenate([tile, pack(d1, 0.125)], axis=0)
+        other = pack(d1, 0.125)
+    else:
+        three = ylo[75] + dots[...] + yhi[75]
+        other = three + pltpu.roll(dots[...] + yhi[75], 2, 0)
+    tile = jnp.concatenate([tile, other], axis=0)
 
     def copy(i):
         packed[i] = tile
@@ -277,7 +423,7 @@
 def post_kernel(first, *refs):
     if first:
         (lo, own, hi, zs, rs, z1, left1, d0, d1, r_core,
-         d2, z_core, q_core, q_ext, dots,
+         d2, z_core, q_core, q_down, q_up, q_halo, dots,
          r2, s0, s1, z2, wide, rows1, u, rem, zf1, rowsv, v, rem0, zf0, acc) = refs
     else:
         (lo, own, hi, zs, rs, z1, left1, d0, d1, d2,
@@ -315,7 +461,7 @@
         r = rem[p]
         box = spread(rem[p - 1] + r + rem[p + 1])
         f = z1[p] + u[p // 2] + (mask1 * x_mask(1, p)) * (CR * r + CA * (d1[p] * r - box))
-        zf1[pl.ds(pl.multiple_of((p - 4) * 24, 8), 24), :] = f[4:28]
+        zf1[(p - 4) * 24 : (p - 3) * 24, :] = f[4:28]
 
     loop(4, 16, final_one)
 
@@ -346,6 +492,8 @@
 
     if first:
         acc[...] = jnp.zeros((2, BY, BZ), F32)
+
+    lane = lax.broadcasted_iota(jnp.int32, (BY, BZ), 1)
 
     def apply(i):
         c = zf0[i + 2]
@@ -355,7 +503,18 @@
         z_core[i] = zc
         q_core[i] = qc
         if first:
-            q_ext[0, i] = q[8:40]
+            if i < 12:
+                q_down[i] = qc
+            if i >= 4:
+                q_up[i - 4] = qc
+            edge = jnp.where(lane < HZ, q[8:40, :128], q[8:40, 128:])
+            edge = turn(edge, 32 * (i % 4) - 48)
+            halo = edge if i % 4 == 0 else jnp.where(lane // 32 == i % 4, edge, q_halo[i // 4])
+            q_halo[i // 4] = halo
+            if i % 4 == 3 and i < 12:
+                q_down[12 + i // 4] = halo
+            if i % 4 == 3 and i >= 4:
+                q_up[11 + i // 4] = halo
             acc[0] += r_core[i] * zc
             acc[1] += zc * qc
 
@@ -374,9 +533,14 @@
     return jnp.sum(tile[row : row + 1, :], axis=1, keepdims=True)
 
 
-def dots_kernel(r, z, q, p, w, sums, dots, acc):
-    tile = sums[...]
-    alpha = pick(tile, 0) / pick(tile, 1)
+def first_sums(here, after, before):
+    h, a, b = here[...], after[...], before[...]
+    return pick(h, 0) + pick(a, 0) + pick(b, 2), pick(h, 1) + pick(a, 1) + pick(b, 3)
+
+
+def dots_kernel(r, z, q, p, w, here, after, before, dots, acc):
+    rz, curve = first_sums(here, after, before)
+    alpha = rz / curve
     acc[...] = jnp.zeros((3, BY, BZ), F32)
 
     def body(i):
@@ -387,16 +551,23 @@
         acc[2] += z2 * qi
 
     loop(0, BX, body)
-    store_dots(dots, [acc[0], acc[1], acc[2]])
-
-
-def end_kernel(r, z, q, p, w, sums, more, solution_field, residual):
-    tile, last = sums[...], more[...]
-    rz, curve = pick(tile, 0), pick(tile, 1)
+    lane = lax.broadcasted_iota(jnp.int32, (1, 128), 1)
+    row = jnp.zeros((1, 128), F32)
+    for i in range(3):
+        total = jnp.sum(jnp.sum(acc[i], axis=0, keepdims=True), axis=1, keepdims=True)
+        row = jnp.where(lane == i, total, row)
+    dots[...] = jnp.broadcast_to(row[None], (GY * GZ, 1, 128))
+
+
+def end_kernel(r, z, q, p, w, here, after, before, m0, m1, m2, m3, solution_field, residual):
+    rz, curve = first_sums(here, after, before)
     alpha = rz / curve
-    rz2 = pick(last, 0)
+    last = jnp.sum(m0[...] + m1[...] + m2[...] + m3[...], axis=0)
+    lane = lax.broadcasted_iota(jnp.int32, (1, 128), 1)
+    at = lambda i: jnp.sum(jnp.where(lane == i, last, 0.0), axis=1, keepdims=True)
+    rz2 = at(0)
     beta = rz2 / rz
-    alpha2 = rz2 / (pick(last, 1) + 2.0 * beta * pick(last, 2) + beta * beta * curve)
+    alpha2 = rz2 / (at(1) + 2.0 * beta * at(2) + beta * beta * curve)
 
     def body(i):
         zi, qi = z[i], q[i]
@@ -418,27 +589,12 @@
         in_specs=[whole] * len(args),
         out_specs=jax.tree.map(lambda _: whole, outs),
         scratch_shapes=[pltpu.VMEM(s, F32) for s in scratch],
-        compiler_params=pltpu.CompilerParams(vmem_limit_bytes=48 * 1024 * 1024),
+        compiler_params=pltpu.CompilerParams(vmem_limit_bytes=24 * 1024 * 1024),
     )(*args)
 
 
 def shift(value, axis, count, by):
     return lax.ppermute(value, axis, [(i, (i + by) % count) for i in range(count)])
-
-
-def exchange_xy(own):
-    xlo = shift(own[:, BX - HX :], "gx", GX, 1)
-    xhi = shift(own[:, :HX], "gx", GX, -1)
-    tall = jnp.concatenate([xlo, own, xhi], axis=1)
-    ylo = shift(tall[:, :, BY - HY :], "gy", GY, 1)
-    yhi = shift(tall[:, :, :HY], "gy", GY, -1)
-    return own, xlo, xhi, ylo, yhi
-
-
-def all_sum(tile):
-    wide = jnp.broadcast_to(tile, (GY * GZ, 8, 128))
-    part = lax.all_to_all(wide, ("gy", "gz"), 0, 0).sum(axis=0)
-    return part + shift(part, "gx", GX, 1) + shift(part, "gx", GX, 2) + shift(part, "gx", GX, 3)
 
 
 def spread_coarse(packed):
@@ -446,15 +602,14 @@
     return shift(own, "gy", GY, 1), own, shift(own, "gy", GY, -1)
 
 
-def pre_call(pieces, given):
-    first = given is None
+def pre_call(first, *args):
     kept = (shape(20, 48, EZ), shape(20, 48, EZ), shape(MX, MY, MZ), shape(MX, MY, MZ),
-            shape(GX * GZ, 16 if first else 8, 128))
+            shape(GX * GZ, 16, 128))
     scratch = [(EX, EY, EZ), (EX, EY, EZ), (MX * EY, EZ), (MX * EY, MZ), (MX, MY, MZ), (16, 128)]
     kernel = functools.partial(pre_kernel, first)
     if first:
-        return call(kernel, (shape(EX, EY, EZ), shape(MX, MY, MZ)) + kept, scratch, *pieces)
-    return call(kernel, kept, scratch, *pieces, *given)
+        kept = (shape(EX, EY, EZ), shape(MX, MY, MZ)) + kept
+    return call(kernel, kept, scratch, *args)
 
 
 def post_call(parts, kept, d0, d1, r_core=None, d2=None):
@@ -466,27 +621,52 @@
     core = shape(BX, BY, BZ)
     kernel = functools.partial(post_kernel, first)
     if first:
-        outs = (shape(18, 24, 256), core, core, shape(1, BX, BY, EZ), shape(8, 128))
+        slab = shape(15, BY, BZ)
+        outs = (shape(18, 24, 256), core, core, slab, slab, shape(4, BY, BZ), shape(8, 128))
         return call(kernel, outs, scratch + [(2, BY, BZ)], *parts, *kept, d0, d1, r_core)
     return call(kernel, (core, core), scratch, *parts, *kept, d0, d1, d2)
 
 
+def first_exchange(right_side, diagonal):
+    def slab(lo, hi):
+        return jnp.stack([right_side[lo:hi], diagonal[lo:hi]])
+
+    xlo = shift(slab(BX - HX, BX), "gx", GX, 1)
+    xhi = shift(slab(0, HX), "gx", GX, -1)
+    edge = shape(2, EX // 4, BY, BZ)
+    down, up = call(z_pack_kernel, (edge, edge), [], right_side, diagonal, xlo, xhi)
+    zl = shift(up, "gz", GZ, 1)
+    zr = shift(down, "gz", GZ, -1)
+    edge = shape(180, 8, BZ)
+    pieces = (right_side, diagonal, xlo, xhi, zl, zr)
+    down, up = call(y_pack_kernel, (edge, edge), [], *pieces)
+    return *pieces, shift(up, "gy", GY, 1), shift(down, "gy", GY, -1)
+
+
+def later_exchange(q, q_down, q_up, q_halo, dots):
+    xlo = shift(q_up, "gx", GX, 1)
+    xhi = shift(q_down, "gx", GX, -1)
+    edge = shape(76, 8, BZ)
+    down, up = call(y_pack_later_kernel, (edge, edge), [], q, q_halo, xlo, xhi, dots)
+    return q, q_halo, xlo, xhi, shift(up, "gy", GY, 1), shift(down, "gy", GY, -1), dots
+
+
 def local(right_side, diagonal):
-    both = jnp.stack([right_side, diagonal])
-    left = shift(both[..., BZ - HZ :], "gz", GZ, 1)
-    right = shift(both[..., :HZ], "gz", GZ, -1)
-    both = jnp.concatenate([left, both, right], axis=3)
-    d0, d1, *kept = pre_call(exchange_xy(both), None)
-    d2, z, q, q_ext, dots = post_call(
+    d0, d1, *kept = pre_call(True, *first_exchange(right_side, diagonal))
+    d2, z, q, *edges = post_call(
         spread_coarse(kept[-1]), kept[:-1], d0, d1, r_core=right_side
     )
-    sums = all_sum(dots)
-    kept = pre_call(exchange_xy(q_ext), (d0, d1))
-    p, w = post_call(spread_coarse(kept[-1]), kept[:-1], d0, d1, d2=d2)
+    kept = pre_call(False, *later_exchange(q, *edges), d0, d1)
+    parts = spread_coarse(kept[-1])
+    here = jnp.sum(parts[1][:, 8:], axis=0)
+    sums = (here, shift(here, "gy", GY, -3), shift(here, "gy", GY, 3))
+    p, w = post_call(parts, kept[:-1], d0, d1, d2=d2)
     fields = (right_side, z, q, p, w)
-    more = call(dots_kernel, shape(8, 128), [(3, BY, BZ)], *fields, sums)
+    more = call(dots_kernel, shape(GY * GZ, 1, 128), [(3, BY, BZ)], *fields, *sums)
+    more = lax.all_to_all(more, ("gy", "gz"), 0, 0)
+    others = [shift(more, "gx", GX, i) for i in (1, 2, 3)]
     core = shape(BX, BY, BZ)
-    return call(end_kernel, (core, core), [], *fields, sums, all_sum(more))
+    return call(end_kernel, (core, core), [], *fields, *sums, more, *others)
 
 
 def solution(mesh):

time: 248 us -> 159 us (0.64)
  Pallas kernels: 78.3 us -> 26.4 us
  waiting for transfers between devices: 68.7 us -> 41.9 us
  blocking collectives: 33.5 us -> 53.4 us
  starting transfers between devices: 48 us -> 34.4 us
  local copies, waits for them, and re-layouts: 13.2 us -> 1.33 us
  other arithmetic: 3.62 us -> 0.09 us
    pallas_call x6 -> x9, Pallas kernels: 78.3 us -> 26.4 us  [call(): pl.pallas_call(kernel, out_shape=outs, in_specs=[whole] * len(args), out_...]
    ppermute x20 -> x19, waiting for transfers between devices: 64.2 us -> 41.9 us  [shift(): lax.ppermute(value, axis, [(i, (i + by) % count) for i in range(count)])]
    all_to_all x1 -> x2, blocking collectives: 14.8 us -> 34.5 us  [spread_coarse(): own = lax.all_to_all(packed, ('gx', 'gz'), 0, 0)]
    all_to_all x2 -> x0, starting transfers between devices: 14.9 us -> none  [the longest x1 8 us: spread_coarse(): own = lax.all_to_all(packed, ('gx', 'gz'), 0, 0)]
    unnamed x30 -> x4, local copies, waits for them, and re-layouts: 10.7 us -> 0.01 us
    all_to_all x2 -> x0, waiting for transfers between devices: 4.46 us -> none  [the longest x1 4.46 us: spread_coarse(): own = lax.all_to_all(packed, ('gx', 'gz'), 0, 0)]
    ppermute x20 -> x19, starting transfers between devices: 33.1 us -> 34.4 us  [shift(): lax.ppermute(value, axis, [(i, (i + by) % count) for i in range(count)])]
  transfers between devices with their start and end apart: 22 -> 19, of which waited for: 12 -> 13; matrix products, arithmetic and copies ran while one was open for 1% -> 0% of each run, Pallas kernels for 7% -> 4%
where the time goes in v2:
time: 159 us; the launch traced here: 158 us
  blocking collectives  53.4 us (34%)
  waiting for transfers between devices  41.9 us (26%)
  starting transfers between devices  34.4 us (22%)
  Pallas kernels  26.4 us (17%)
    ppermute x19, waiting for transfers between devices, shift(): lax.ppermute(value, axis, [(i, (i + by) % count) for i in range(count)])  41.9 us
    all_to_all x2, blocking collectives, spread_coarse(): own = lax.all_to_all(packed, ('gx', 'gz'), 0, 0)  34.5 us
    ppermute x19, starting transfers between devices, shift(): lax.ppermute(value, axis, [(i, (i + by) % count) for i in range(count)])  34.4 us
    pallas_call x9, Pallas kernels, call(): pl.pallas_call(kernel, out_shape=outs, in_specs=[whole] * len(args), out_...  26.4 us
    all_to_all x1, blocking collectives, local(): more = lax.all_to_all(more, ('gy', 'gz'), 0, 0)  18.9 us
  transfers between devices with their start and end apart: 19, of which 13 were waited for; matrix products, arithmetic and copies ran while one was open for 0% of the time, Pallas kernels for 4%

profile of v2, /device:TPU:1, one launch (start us, length us, event | category | flops | bytes accessed | tf_op | source)
XLA Modules:
  0.0 158.3 jit_solution(13893621635091686000)
XLA Ops:
  0.6 1.3 slice_bitcast_fusion
  2.0 2.1 %collective-permute-start = (f32[2,12,32,128]{3,2,1,0:T(8,128)S(1)}, f32[2,12,32,128]{3,2,1,0:T(8,128)S(1)}, u32[]{:S(2)}, u32[]{:S(2)}) collective-permute-start(f32[2,12,32,128]{3,2,1,0:T(8,128)S(1)} %pad_maximum_fusion), channel_id=1, source_target_pairs={{0,64},{64,128},{128,192},{192,0},{1,65},{65,129},{129,193},{193,1... | collective-permute-start | bytes 1179656 | tf_op jit(solution)/shard_map/ppermute | solution.py:597
  4.2 1.4 collective-permute-start.1
  5.5 6.4 %collective-permute-done.xlo.refs_2_ = f32[2,12,32,128]{3,2,1,0:T(8,128)S(1)} collective-permute-done((f32[2,12,32,128]{3,2,1,0:T(8,128)S(1)}, f32[2,12,32,128]{3,2,1,0:T(8,128)S(1)}, u32[]{:S(2)}, u32[]{:S(2)}) %collective-permute-start) | collective-permute-done | bytes 393248 | tf_op jit(solution)/shard_map/ppermute | solution.py:597
  11.9 1.7 %collective-permute-done.1.xhi.refs_3_ = f32[2,12,32,128]{3,2,1,0:T(8,128)S(1)} collective-permute-done((f32[2,12,32,128]{3,2,1,0:T(8,128)S(1)}, f32[2,12,32,128]{3,2,1,0:T(8,128)S(1)}, u32[]{:S(2)}, u32[]{:S(2)}) %collective-permute-start.1) | collective-permute-done | bytes 393248 | tf_op jit(solution)/shard_map/ppermute | solution.py:597
  13.6 0.6 shard_map.41
  14.2 2.2 %collective-permute-start.2 = (f32[2,10,32,128]{3,2,1,0:T(8,128)S(1)}, f32[2,10,32,128]{3,2,1,0:T(8,128)S(1)}, u32[]{:S(2)}, u32[]{:S(2)}) collective-permute-start(f32[2,10,32,128]{3,2,1,0:T(8,128)S(1)} %get-tuple-element.29), channel_id=1, source_target_pairs={{0,1},{1,2},{2,3},{3,4},{4,5},{5,6},{6,7},{7,0},{8,9},{9,10},{10,1... | collective-permute-start | bytes 983048 | tf_op jit(solution)/shard_map/ppermute | solution.py:597
  16.4 4.0 %collective-permute-start.3 = (f32[2,10,32,128]{3,2,1,0:T(8,128)S(1)}, f32[2,10,32,128]{3,2,1,0:T(8,128)S(1)}, u32[]{:S(2)}, u32[]{:S(2)}) collective-permute-start(f32[2,10,32,128]{3,2,1,0:T(8,128)S(1)} %get-tuple-element.30), channel_id=1, source_target_pairs={{0,7},{1,0},{2,1},{3,2},{4,3},{5,4},{6,5},{7,6},{8,15},{9,8},{10,9... | collective-permute-start | bytes 983048 | tf_op jit(solution)/shard_map/ppermute | solution.py:597
  20.4 6.3 %collective-permute-done.2.zl.refs_4_ = f32[2,10,32,128]{3,2,1,0:T(8,128)S(1)} collective-permute-done((f32[2,10,32,128]{3,2,1,0:T(8,128)S(1)}, f32[2,10,32,128]{3,2,1,0:T(8,128)S(1)}, u32[]{:S(2)}, u32[]{:S(2)}) %collective-permute-start.2) | collective-permute-done | bytes 327712 | tf_op jit(solution)/shard_map/ppermute | solution.py:597
  26.7 0.0 collective-permute-done.3.zr.refs_5_
  26.7 0.1 shard_map.42
  26.9 3.5 %collective-permute-start.4 = (f32[180,8,128]{2,1,0:T(8,128)S(1)}, f32[180,8,128]{2,1,0:T(8,128)S(1)}, u32[]{:S(2)}, u32[]{:S(2)}) collective-permute-start(f32[180,8,128]{2,1,0:T(8,128)S(1)} %get-tuple-element.31), channel_id=1, source_target_pairs={{0,8},{8,16},{16,24},{24,32},{32,40},{40,48},{48,56},{56,0},{1,9},... | collective-permute-start | bytes 2211848 | tf_op jit(solution)/shard_map/ppermute | solution.py:597
  30.3 0.0 collective-permute-start.5
  30.3 8.4 %collective-permute-done.4.refs_6_ = f32[180,8,128]{2,1,0:T(8,128)S(1)} collective-permute-done((f32[180,8,128]{2,1,0:T(8,128)S(1)}, f32[180,8,128]{2,1,0:T(8,128)S(1)}, u32[]{:S(2)}, u32[]{:S(2)}) %collective-permute-start.4) | collective-permute-done | bytes 737312 | tf_op jit(solution)/shard_map/ppermute | solution.py:597
  38.8 2.5 %collective-permute-done.5.refs_7_ = f32[180,8,128]{2,1,0:T(8,128)S(1)} collective-permute-done((f32[180,8,128]{2,1,0:T(8,128)S(1)}, f32[180,8,128]{2,1,0:T(8,128)S(1)}, u32[]{:S(2)}, u32[]{:S(2)}) %collective-permute-start.5) | collective-permute-done | bytes 737312 | tf_op jit(solution)/shard_map/ppermute | solution.py:597
  41.2 6.8 %shard_map.43 = (f32[40,64,256]{2,1,0:T(8,128)S(1)}, f32[20,32,128]{2,1,0:T(8,128)S(1)}, f32[20,48,256]{2,1,0:T(8,128)S(1)}, f32[20,48,256]{2,1,0:T(8,128)S(1)},...) custom-call(f32[16,32,128]{2,1,0:T(8,128)S(1)} %copy-done, ...), custom_call_target="tpu_custom_call" | custom-call | tf_op jit(solution)/shard_map/pallas_call | solution.py:586
  48.0 18.2 %all_to_all.15.refs_1_ = f32[32,16,128]{2,1,0:T(8,128)S(1)} all-to-all(f32[32,16,128]{2,1,0:T(8,128)S(1)} %get-tuple-element.33), channel_id=1, replica_groups=mesh['gx'=4,'gy'=8,'gz'=8] {'gx','gz'}, dimensions={0} | all-to-all | bytes 524288 | tf_op jit(solution)/shard_map/all_to_all | solution.py:601
  66.3 2.4 %collective-permute-start.7 = (f32[32,16,128]{2,1,0:T(8,128)S(1)}, f32[32,16,128]{2,1,0:T(8,128)S(1)}, u32[]{:S(2)}, u32[]{:S(2)}) collective-permute-start(f32[32,16,128]{2,1,0:T(8,128)S(1)} %all_to_all.15.refs_1_), channel_id=1, source_target_pairs={{0,56},{8,0},{16,8},{24,16},{32,24},{40,32},{48,40},{56,48},{1,57}... | collective-permute-start | bytes 786440 | tf_op jit(solution)/shard_map/ppermute | solution.py:597
  68.7 0.0 collective-permute-start.6
  68.7 3.4 %collective-permute-done.7.refs_2_ = f32[32,16,128]{2,1,0:T(8,128)S(1)} collective-permute-done((f32[32,16,128]{2,1,0:T(8,128)S(1)}, f32[32,16,128]{2,1,0:T(8,128)S(1)}, u32[]{:S(2)}, u32[]{:S(2)}) %collective-permute-start.7) | collective-permute-done | bytes 262176 | tf_op jit(solution)/shard_map/ppermute | solution.py:597
  72.1 0.0 collective-permute-done.6.refs_0_
  72.1 6.4 %shard_map.44 = (f32[18,24,256]{2,1,0:T(8,128)S(1)}, f32[16,32,128]{2,1,0:T(8,128)S(1)}, f32[16,32,128]{2,1,0:T(8,128)S(1)}, f32[15,32,128]{2,1,0:T(8,128)S(1)},...) custom-call(f32[32,16,128]{2,1,0:T(8,128)S(1)} %collective-permute-done.6.refs_0_, ...), custom_call_target="tpu_custom_call" | custom-call | tf_op jit(solution)/shard_map/pallas_call | solution.py:586
  78.5 0.8 collective-permute-start.8
  79.3 2.0 %collective-permute-start.9 = (f32[15,32,128]{2,1,0:T(8,128)S(1)}, f32[15,32,128]{2,1,0:T(8,128)S(1)}, u32[]{:S(2)}, u32[]{:S(2)}) collective-permute-start(f32[15,32,128]{2,1,0:T(8,128)S(1)} %get-tuple-element.44), channel_id=1, source_target_pairs={{0,192},{64,0},{128,64},{192,128},{1,193},{65,1},{129,65},{193,129... | collective-permute-start | bytes 737288 | tf_op jit(solution)/shard_map/ppermute | solution.py:597
  81.2 3.6 %collective-permute-done.8.xlo.refs_2_ = f32[15,32,128]{2,1,0:T(8,128)S(1)} collective-permute-done((f32[15,32,128]{2,1,0:T(8,128)S(1)}, f32[15,32,128]{2,1,0:T(8,128)S(1)}, u32[]{:S(2)}, u32[]{:S(2)}) %collective-permute-start.8) | collective-permute-done | bytes 245792 | tf_op jit(solution)/shard_map/ppermute | solution.py:597
  84.8 0.1 shard_map.45
  84.9 5.5 %collective-permute-start.10 = (f32[76,8,128]{2,1,0:T(8,128)S(1)}, f32[76,8,128]{2,1,0:T(8,128)S(1)}, u32[]{:S(2)}, u32[]{:S(2)}) collective-permute-start(f32[76,8,128]{2,1,0:T(8,128)S(1)} %get-tuple-element.46), channel_id=1, source_target_pairs={{0,8},{8,16},{16,24},{24,32},{32,40},{40,48},{48,56},{56,0},{1,9},... | collective-permute-start | bytes 933896 | tf_op jit(solution)/shard_map/ppermute | solution.py:597
  90.4 1.1 collective-permute-start.11
  91.5 2.8 %collective-permute-done.10.refs_4_ = f32[76,8,128]{2,1,0:T(8,128)S(1)} collective-permute-done((f32[76,8,128]{2,1,0:T(8,128)S(1)}, f32[76,8,128]{2,1,0:T(8,128)S(1)}, u32[]{:S(2)}, u32[]{:S(2)}) %collective-permute-start.10) | collective-permute-done | bytes 311328 | tf_op jit(solution)/shard_map/ppermute | solution.py:597
  94.2 2.8 %collective-permute-done.11.refs_5_ = f32[76,8,128]{2,1,0:T(8,128)S(1)} collective-permute-done((f32[76,8,128]{2,1,0:T(8,128)S(1)}, f32[76,8,128]{2,1,0:T(8,128)S(1)}, u32[]{:S(2)}, u32[]{:S(2)}) %collective-permute-start.11) | collective-permute-done | bytes 311328 | tf_op jit(solution)/shard_map/ppermute | solution.py:597
  97.0 4.9 %shard_map.46 = (f32[20,48,256]{2,1,0:T(8,128)S(1)}, f32[20,48,256]{2,1,0:T(8,128)S(1)}, f32[20,32,128]{2,1,0:T(8,128)S(1)}, f32[20,32,128]{2,1,0:T(8,128)S(1)}, f32[32,16,128]{2,1,0:T(8,128)S(1)}) custom-call(f32[16,32,128]{2,1,0:T(8,128)S(1)} %get-tuple-element.41.own.refs_0_.q, f32[4,32,128]{2,1,0:T(8,128)S(1)} %get-tuple-element.42.halo.refs_1_, ...), custom_call_target="tpu_custom_call" | custom-call | tf_op jit(solution)/shard_map/pallas_call | solution.py:586
  101.9 16.3 %all_to_all.16.refs_1_ = f32[32,16,128]{2,1,0:T(8,128)S(1)} all-to-all(f32[32,16,128]{2,1,0:T(8,128)S(1)} %get-tuple-element.48), channel_id=1, replica_groups=mesh['gx'=4,'gy'=8,'gz'=8] {'gx','gz'}, dimensions={0} | all-to-all | bytes 524288 | tf_op jit(solution)/shard_map/all_to_all | solution.py:601
  118.2 4.0 %collective-permute-start.13 = (f32[32,16,128]{2,1,0:T(8,128)S(1)}, f32[32,16,128]{2,1,0:T(8,128)S(1)}, u32[]{:S(2)}, u32[]{:S(2)}) collective-permute-start(f32[32,16,128]{2,1,0:T(8,128)S(1)} %all_to_all.16.refs_1_), channel_id=1, source_target_pairs={{0,56},{8,0},{16,8},{24,16},{32,24},{40,32},{48,40},{56,48},{1,57}... | collective-permute-start | bytes 786440 | tf_op jit(solution)/shard_map/ppermute | solution.py:597
  122.2 0.0 collective-permute-start.12
  122.3 2.0 %collective-permute-start.15 = (f32[8,128]{1,0:T(8,128)S(1)}, f32[8,128]{1,0:T(8,128)S(1)}, u32[]{:S(2)}, u32[]{:S(2)}) collective-permute-start(f32[8,128]{1,0:T(8,128)S(1)} %slice_reduce_fusion.here), channel_id=1, source_target_pairs={{0,24},{8,32},{16,40},{24,48},{32,56},{40,0},{48,8},{56,16},{1,25}... | collective-permute-start | bytes 12296 | tf_op jit(solution)/shard_map/ppermute | solution.py:597
  124.2 1.3 collective-permute-start.14
  125.5 0.0 collective-permute-done.13.refs_2_
  125.5 0.2 collective-permute-done.12.refs_0_
  125.7 6.0 %shard_map.47 = (f32[16,32,128]{2,1,0:T(8,128)S(1)}, f32[16,32,128]{2,1,0:T(8,128)S(1)}) custom-call(f32[32,16,128]{2,1,0:T(8,128)S(1)} %collective-permute-done.12.refs_0_, f32[32,16,128]{2,1,0:T(8,128)S(1)} %all_to_all.16.refs_1_, f32[32,16,128]{2,1,0:T(8,128)S(1)} %collective-permute-done.13.refs_2_, f32[20,48,256]{2,1,0:T(8,128)S(1)} %get-tuple-element.49.refs_3_, ...), custom_call_target="tpu_custom_call" | custom-call | tf_op jit(solution)/shard_map/pallas_call | solution.py:586
  131.8 0.3 shard_map.48
  132.1 18.9 %all_to_all.17.m0 = f32[64,1,128]{2,1,0:T(1,128)S(1)} all-to-all(f32[64,1,128]{2,1,0:T(1,128)S(1)} %shard_map.48), channel_id=1, replica_groups=mesh['gx'=4,'gy'=8,'gz'=8] {'gy','gz'}, dimensions={0} | all-to-all | bytes 65536 | tf_op jit(solution)/shard_map/all_to_all | solution.py:666
  151.0 0.9 collective-permute-start.18
  151.9 1.2 collective-permute-start.17
  153.2 0.0 collective-permute-start.16
  153.2 0.6 collective-permute-done.18.m3
  153.8 2.4 %collective-permute-done.17.m2 = f32[64,1,128]{2,1,0:T(1,128)S(1)} collective-permute-done((f32[64,1,128]{2,1,0:T(1,128)S(1)}, f32[64,1,128]{2,1,0:T(1,128)S(1)}, u32[]{:S(2)}, u32[]{:S(2)}) %collective-permute-start.17) | collective-permute-done | bytes 32800 | tf_op jit(solution)/shard_map/ppermute | solution.py:597
  156.2 0.9 collective-permute-done.16.m1
  157.1 1.2 shard_map.49
  (10 shorter events, 0.1 us)
Async XLA Ops:
  0.6 13.0 %copy-start = (f32[16,32,128]{2,1,0:T(8,128)S(1)}, f32[16,32,128]{2,1,0:T(8,128)}, u32[]{:S(2)}) copy-start(f32[16,32,128]{2,1,0:T(8,128)} %r.3) | copy-start | bytes 786436
  0.6 13.0 %copy-start.1 = (f32[16,32,128]{2,1,0:T(8,128)S(1)}, f32[16,32,128]{2,1,0:T(8,128)}, u32[]{:S(2)}) copy-start(f32[16,32,128]{2,1,0:T(8,128)} %refs_1_.1) | copy-start | bytes 786436
  2.0 9.9 %collective-permute-start = (f32[2,12,32,128]{3,2,1,0:T(8,128)S(1)}, f32[2,12,32,128]{3,2,1,0:T(8,128)S(1)}, u32[]{:S(2)}, u32[]{:S(2)}) collective-permute-start(f32[2,12,32,128]{3,2,1,0:T(8,128)S(1)} %pad_maximum_fusion), channel_id=1, source_target_pairs={{0,64},{64,128},{128,192},{192,0},{1,65},{65,129},{129,193},{193,1... | collective-permute-start | bytes 1179656 | tf_op jit(solution)/shard_map/ppermute | solution.py:597
  4.2 9.5 %collective-permute-start.1 = (f32[2,12,32,128]{3,2,1,0:T(8,128)S(1)}, f32[2,12,32,128]{3,2,1,0:T(8,128)S(1)}, u32[]{:S(2)}, u32[]{:S(2)}) collective-permute-start(f32[2,12,32,128]{3,2,1,0:T(8,128)S(1)} %pad_maximum_fusion.1), channel_id=1, source_target_pairs={{0,192},{64,0},{128,64},{192,128},{1,193},{65,1},{129,65},{193,129... | collective-permute-start | bytes 1179656 | tf_op jit(solution)/shard_map/ppermute | solution.py:597
  14.2 12.5 %collective-permute-start.2 = (f32[2,10,32,128]{3,2,1,0:T(8,128)S(1)}, f32[2,10,32,128]{3,2,1,0:T(8,128)S(1)}, u32[]{:S(2)}, u32[]{:S(2)}) collective-permute-start(f32[2,10,32,128]{3,2,1,0:T(8,128)S(1)} %get-tuple-element.29), channel_id=1, source_target_pairs={{0,1},{1,2},{2,3},{3,4},{4,5},{5,6},{6,7},{7,0},{8,9},{9,10},{10,1... | collective-permute-start | bytes 983048 | tf_op jit(solution)/shard_map/ppermute | solution.py:597
  16.4 10.3 %collective-permute-start.3 = (f32[2,10,32,128]{3,2,1,0:T(8,128)S(1)}, f32[2,10,32,128]{3,2,1,0:T(8,128)S(1)}, u32[]{:S(2)}, u32[]{:S(2)}) collective-permute-start(f32[2,10,32,128]{3,2,1,0:T(8,128)S(1)} %get-tuple-element.30), channel_id=1, source_target_pairs={{0,7},{1,0},{2,1},{3,2},{4,3},{5,4},{6,5},{7,6},{8,15},{9,8},{10,9... | collective-permute-start | bytes 983048 | tf_op jit(solution)/shard_map/ppermute | solution.py:597
  26.9 11.9 %collective-permute-start.4 = (f32[180,8,128]{2,1,0:T(8,128)S(1)}, f32[180,8,128]{2,1,0:T(8,128)S(1)}, u32[]{:S(2)}, u32[]{:S(2)}) collective-permute-start(f32[180,8,128]{2,1,0:T(8,128)S(1)} %get-tuple-element.31), channel_id=1, source_target_pairs={{0,8},{8,16},{16,24},{24,32},{32,40},{40,48},{48,56},{56,0},{1,9},... | collective-permute-start | bytes 2211848 | tf_op jit(solution)/shard_map/ppermute | solution.py:597
  30.3 10.9 %collective-permute-start.5 = (f32[180,8,128]{2,1,0:T(8,128)S(1)}, f32[180,8,128]{2,1,0:T(8,128)S(1)}, u32[]{:S(2)}, u32[]{:S(2)}) collective-permute-start(f32[180,8,128]{2,1,0:T(8,128)S(1)} %get-tuple-element.32), channel_id=1, source_target_pairs={{0,56},{8,0},{16,8},{24,16},{32,24},{40,32},{48,40},{56,48},{1,57}... | collective-permute-start | bytes 2211848 | tf_op jit(solution)/shard_map/ppermute | solution.py:597
  66.3 5.8 %collective-permute-start.7 = (f32[32,16,128]{2,1,0:T(8,128)S(1)}, f32[32,16,128]{2,1,0:T(8,128)S(1)}, u32[]{:S(2)}, u32[]{:S(2)}) collective-permute-start(f32[32,16,128]{2,1,0:T(8,128)S(1)} %all_to_all.15.refs_1_), channel_id=1, source_target_pairs={{0,56},{8,0},{16,8},{24,16},{32,24},{40,32},{48,40},{56,48},{1,57}... | collective-permute-start | bytes 786440 | tf_op jit(solution)/shard_map/ppermute | solution.py:597
  68.7 3.4 %collective-permute-start.6 = (f32[32,16,128]{2,1,0:T(8,128)S(1)}, f32[32,16,128]{2,1,0:T(8,128)S(1)}, u32[]{:S(2)}, u32[]{:S(2)}) collective-permute-start(f32[32,16,128]{2,1,0:T(8,128)S(1)} %all_to_all.15.refs_1_), channel_id=1, source_target_pairs={{0,8},{8,16},{16,24},{24,32},{32,40},{40,48},{48,56},{56,0},{1,9},... | collective-permute-start | bytes 786440 | tf_op jit(solution)/shard_map/ppermute | solution.py:597
  78.5 6.3 %collective-permute-start.8 = (f32[15,32,128]{2,1,0:T(8,128)S(1)}, f32[15,32,128]{2,1,0:T(8,128)S(1)}, u32[]{:S(2)}, u32[]{:S(2)}) collective-permute-start(f32[15,32,128]{2,1,0:T(8,128)S(1)} %get-tuple-element.43), channel_id=1, source_target_pairs={{0,64},{64,128},{128,192},{192,0},{1,65},{65,129},{129,193},{193,1... | collective-permute-start | bytes 737288 | tf_op jit(solution)/shard_map/ppermute | solution.py:597
  79.3 5.5 %collective-permute-start.9 = (f32[15,32,128]{2,1,0:T(8,128)S(1)}, f32[15,32,128]{2,1,0:T(8,128)S(1)}, u32[]{:S(2)}, u32[]{:S(2)}) collective-permute-start(f32[15,32,128]{2,1,0:T(8,128)S(1)} %get-tuple-element.44), channel_id=1, source_target_pairs={{0,192},{64,0},{128,64},{192,128},{1,193},{65,1},{129,65},{193,129... | collective-permute-start | bytes 737288 | tf_op jit(solution)/shard_map/ppermute | solution.py:597
  84.9 9.4 %collective-permute-start.10 = (f32[76,8,128]{2,1,0:T(8,128)S(1)}, f32[76,8,128]{2,1,0:T(8,128)S(1)}, u32[]{:S(2)}, u32[]{:S(2)}) collective-permute-start(f32[76,8,128]{2,1,0:T(8,128)S(1)} %get-tuple-element.46), channel_id=1, source_target_pairs={{0,8},{8,16},{16,24},{24,32},{32,40},{40,48},{48,56},{56,0},{1,9},... | collective-permute-start | bytes 933896 | tf_op jit(solution)/shard_map/ppermute | solution.py:597
  90.4 6.6 %collective-permute-start.11 = (f32[76,8,128]{2,1,0:T(8,128)S(1)}, f32[76,8,128]{2,1,0:T(8,128)S(1)}, u32[]{:S(2)}, u32[]{:S(2)}) collective-permute-start(f32[76,8,128]{2,1,0:T(8,128)S(1)} %get-tuple-element.47), channel_id=1, source_target_pairs={{0,56},{8,0},{16,8},{24,16},{32,24},{40,32},{48,40},{56,48},{1,57}... | collective-permute-start | bytes 933896 | tf_op jit(solution)/shard_map/ppermute | solution.py:597
  118.2 7.3 %collective-permute-start.13 = (f32[32,16,128]{2,1,0:T(8,128)S(1)}, f32[32,16,128]{2,1,0:T(8,128)S(1)}, u32[]{:S(2)}, u32[]{:S(2)}) collective-permute-start(f32[32,16,128]{2,1,0:T(8,128)S(1)} %all_to_all.16.refs_1_), channel_id=1, source_target_pairs={{0,56},{8,0},{16,8},{24,16},{32,24},{40,32},{48,40},{56,48},{1,57}... | collective-permute-start | bytes 786440 | tf_op jit(solution)/shard_map/ppermute | solution.py:597
  122.2 3.5 %collective-permute-start.12 = (f32[32,16,128]{2,1,0:T(8,128)S(1)}, f32[32,16,128]{2,1,0:T(8,128)S(1)}, u32[]{:S(2)}, u32[]{:S(2)}) collective-permute-start(f32[32,16,128]{2,1,0:T(8,128)S(1)} %all_to_all.16.refs_1_), channel_id=1, source_target_pairs={{0,8},{8,16},{16,24},{24,32},{32,40},{40,48},{48,56},{56,0},{1,9},... | collective-permute-start | bytes 786440 | tf_op jit(solution)/shard_map/ppermute | solution.py:597
  122.3 9.5 %collective-permute-start.15 = (f32[8,128]{1,0:T(8,128)S(1)}, f32[8,128]{1,0:T(8,128)S(1)}, u32[]{:S(2)}, u32[]{:S(2)}) collective-permute-start(f32[8,128]{1,0:T(8,128)S(1)} %slice_reduce_fusion.here), channel_id=1, source_target_pairs={{0,24},{8,32},{16,40},{24,48},{32,56},{40,0},{48,8},{56,16},{1,25}... | collective-permute-start | bytes 12296 | tf_op jit(solution)/shard_map/ppermute | solution.py:597
  124.2 7.6 %collective-permute-start.14 = (f32[8,128]{1,0:T(8,128)S(1)}, f32[8,128]{1,0:T(8,128)S(1)}, u32[]{:S(2)}, u32[]{:S(2)}) collective-permute-start(f32[8,128]{1,0:T(8,128)S(1)} %slice_reduce_fusion.here), channel_id=1, source_target_pairs={{0,40},{8,48},{16,56},{24,0},{32,8},{40,16},{48,24},{56,32},{1,41}... | collective-permute-start | bytes 12296 | tf_op jit(solution)/shard_map/ppermute | solution.py:597
  151.0 2.8 %collective-permute-start.18 = (f32[64,1,128]{2,1,0:T(1,128)S(1)}, f32[64,1,128]{2,1,0:T(1,128)S(1)}, u32[]{:S(2)}, u32[]{:S(2)}) collective-permute-start(f32[64,1,128]{2,1,0:T(1,128)S(1)} %all_to_all.17.m0), channel_id=1, source_target_pairs={{0,192},{64,0},{128,64},{192,128},{1,193},{65,1},{129,65},{193,129... | collective-permute-start | bytes 98312 | tf_op jit(solution)/shard_map/ppermute | solution.py:597
  151.9 4.3 %collective-permute-start.17 = (f32[64,1,128]{2,1,0:T(1,128)S(1)}, f32[64,1,128]{2,1,0:T(1,128)S(1)}, u32[]{:S(2)}, u32[]{:S(2)}) collective-permute-start(f32[64,1,128]{2,1,0:T(1,128)S(1)} %all_to_all.17.m0), channel_id=1, source_target_pairs={{0,128},{64,192},{128,0},{192,64},{1,129},{65,193},{129,1},{193,65... | collective-permute-start | bytes 98312 | tf_op jit(solution)/shard_map/ppermute | solution.py:597
  153.2 4.0 %collective-permute-start.16 = (f32[64,1,128]{2,1,0:T(1,128)S(1)}, f32[64,1,128]{2,1,0:T(1,128)S(1)}, u32[]{:S(2)}, u32[]{:S(2)}) collective-permute-start(f32[64,1,128]{2,1,0:T(1,128)S(1)} %all_to_all.17.m0), channel_id=1, source_target_pairs={{0,64},{64,128},{128,192},{192,0},{1,65},{65,129},{129,193},{193,1... | collective-permute-start | bytes 98312 | tf_op jit(solution)/shard_map/ppermute | solution.py:597

commit v3 on v2

v3 whole, which is shorter than its diff:
```python
import functools

import jax
import jax.numpy as jnp
from jax import lax
from jax.experimental import pallas as pl
from jax.experimental.pallas import tpu as pltpu
from jax.sharding import PartitionSpec as P

GX, GY, GZ = 4, 8, 8
BX, BY, BZ = 16, 32, 128
HX, HY = 12, 12
EX, EY, EZ = BX + 2 * HX, BY + 2 * HY, 2 * BZ
MX, MR, MY, MZ = EX // 2, EY // 2, 32, BZ
PY = BY + 8
F32 = jnp.float32
SPEC = P("gx", "gy", "gz")


def cheb_two(lower, upper=58.0):
    theta, delta = (upper + lower) / 2.0, (upper - lower) / 2.0
    sigma = theta / delta
    rho = 1.0 / sigma
    after = 1.0 / (2.0 * sigma - rho)
    return (1.0 + after * rho) / theta + 2.0 * after / delta, -2.0 * after / (delta * theta)


CR, CA = cheb_two(7.0)


def spread(t):
    t = t + pltpu.roll(t, 1, 0) + pltpu.roll(t, t.shape[0] - 1, 0)
    return t + pltpu.roll(t, 1, 1) + pltpu.roll(t, t.shape[1] - 1, 1)


def flag(condition):
    return jnp.where(condition, 1.0, 0.0).astype(F32)


def places():
    return lax.axis_index("gx"), lax.axis_index("gy"), lax.axis_index("gz")


def plane_mask(level, shape, row):
    _, gy, gz = places()
    size = 1 << level
    y = lax.broadcasted_iota(jnp.int32, shape, 0) + (gy * (BY // size) + row)
    lane = lax.broadcasted_iota(jnp.int32, shape, 1)
    z = jnp.where(lane < 3 * shape[1] // 4, lane, lane - shape[1]) + gz * (BZ // size)
    return flag((y >= 0) & (y < GY * BY // size) & (z >= 0) & (z < GZ * BZ // size))


def x_masks(mask, level, scale=1.0):
    gx = places()[0]
    first, last = HX >> level, (HX + BX) >> level
    low, high = flag(gx > 0) * scale, flag(gx < GX - 1) * scale
    low, mid, high = mask * low, mask * scale, mask * high
    return lambda p: low if p < first else mid if p < last else high


def loop(first, last, body):
    for i in range(first, last):
        body(i)


def halving(rows, cols):
    a = lax.broadcasted_iota(jnp.int32, (rows, cols), 0)
    b = lax.broadcasted_iota(jnp.int32, (rows, cols), 1)
    return flag(a // 2 == b)


def doubling(rows, cols):
    a = lax.broadcasted_iota(jnp.int32, (rows, cols), 0)
    b = lax.broadcasted_iota(jnp.int32, (rows, cols), 1)
    return flag(b // 2 == a)


def dot(a, b):
    b = b.astype(jnp.bfloat16)
    hi = a.astype(jnp.bfloat16)
    a = a - hi.astype(F32)
    mid = a.astype(jnp.bfloat16)
    lo = (a - mid.astype(F32)).astype(jnp.bfloat16)
    one = functools.partial(jnp.dot, preferred_element_type=F32)
    return one(hi, b) + one(mid, b) + one(lo, b)


def turn(tile, by):
    by = by % 128
    return pltpu.roll(tile, by, 1) if by else tile


def x_plane(own, xlo, xhi, p):
    if p < HX:
        return xlo(p)
    return own(p - HX) if p < HX + BX else xhi(p - HX - BX)


def half_tile(src, base, plane):
    at = 4 * (plane % 2)
    return src[base + plane // 2, at : at + 4]


def first_parts(a, own, xlo, xhi, zl, zr, ylo, yhi):
    base = a * 84

    def parts(p):
        g, k = p // 5, p % 5

        def pair(center, left, right):
            lane = lax.broadcasted_iota(jnp.int32, left.shape, 1)
            return center, jnp.where(lane < 64, turn(right, -24 * k), turn(left, 104 - 24 * k))

        whole = lambda y: pair(y[base + p], y[base + 40 + g], y[base + 48 + g])
        half = lambda y: pair(*(half_tile(y, base + 56, m) for m in (p, 40 + g, 48 + g)))
        center = x_plane(lambda i: own[i], lambda i: xlo[a, i], lambda i: xhi[a, i], p)
        middle = pair(center, zl[a, g], zr[a, g])
        return whole(ylo), half(ylo), middle, half(yhi), whole(yhi)

    return parts


def later_parts(own, halo, xlo, xhi, ylo, yhi):
    def parts(p):
        g, k = p // 4, p % 4
        pair = lambda center, side: (center, turn(side, 112 - 32 * k))
        whole = lambda y: pair(y[p], y[40 + g])
        half = lambda y: pair(half_tile(y, 50, p), half_tile(y, 50, 40 + g))
        center = x_plane(lambda i: own[i], lambda i: xlo[i], lambda i: xhi[i], p)
        side = x_plane(
            lambda i: halo[i // 4], lambda i: xlo[12 + i // 4], lambda i: xhi[12 + i // 4], p
        )
        return whole(ylo), half(ylo), pair(center, side), half(yhi), whole(yhi)

    return parts


ROWS = ((0, 8), (8, 12), (12, 44), (44, 48), (48, 56))


def assemble_field(dst, parts):
    gx, gy, gz = places()
    lane = lax.broadcasted_iota(jnp.int32, (1, BZ), 1)
    side = jnp.where(lane < 64, flag(gz < GZ - 1), flag(gz > 0))
    x_low, x_high = flag(gx > 0), flag(gx < GX - 1)
    y_low, y_high = flag(gy > 0), flag(gy < GY - 1)
    for p in range(EX):
        x = x_low if p < HX else None if p < HX + BX else x_high
        for (lo, hi), y, (center, halo) in zip(
            ROWS, (y_low, y_low, None, y_high, y_high), parts(p)
        ):
            scale = x if y is None else y if x is None else x * y
            dst[p, lo:hi, :BZ] = center if scale is None else center * scale
            dst[p, lo:hi, BZ:] = halo * (side if scale is None else side * scale)


def assemble_diagonal(dst, parts):
    for p in range(EX):
        for (lo, hi), (center, halo) in zip(ROWS, parts(p)):
            dst[p, lo:hi, :BZ] = center + 27.0
            dst[p, lo:hi, BZ:] = halo + 27.0


def z_pack_kernel(right_side, diagonal, xlo, xhi, down, up):
    group = lax.broadcasted_iota(jnp.int32, (BY, BZ), 1) // 24
    for a, own in enumerate((right_side, diagonal)):
        for g in range(EX // 5):
            low = high = None
            for k in range(5):
                src = x_plane(
                    lambda i: own[i], lambda i: xlo[a, i], lambda i: xhi[a, i], 5 * g + k
                )
                first, last = turn(src, 24 * k), turn(src, 24 * k - 104)
                low = first if k == 0 else jnp.where(group == k, first, low)
                high = last if k == 0 else jnp.where(group == k, last, high)
            down[a, g] = low
            up[a, g] = high


def y_rows(planes, base, down, up):
    count = len(planes)
    for m, plane in enumerate(planes):
        down[base + m] = plane(4, 12)
        up[base + m] = plane(20, 28)
        at = base + count + m // 2
        row = 4 * (m % 2)
        down[at, row : row + 4] = plane(0, 4)
        up[at, row : row + 4] = plane(28, 32)


def y_pack_kernel(right_side, diagonal, xlo, xhi, zl, zr, down, up):
    def rows(ref, *index):
        return lambda lo, hi: ref[(*index, slice(lo, hi))]

    for a, own in enumerate((right_side, diagonal)):
        planes = [
            x_plane(
                lambda i: rows(own, i), lambda i: rows(xlo, a, i), lambda i: rows(xhi, a, i), p
            )
            for p in range(EX)
        ]
        planes += [rows(zl, a, g) for g in range(8)] + [rows(zr, a, g) for g in range(8)]
        y_rows(planes, 84 * a, down, up)


def y_pack_later_kernel(own, halo, xlo, xhi, down, up):
    def rows(ref, index):
        return lambda lo, hi: ref[index, lo:hi]

    planes = [
        x_plane(lambda i: rows(own, i), lambda i: rows(xlo, i), lambda i: rows(xhi, i), p)
        for p in range(EX)
    ]
    planes += [
        x_plane(
            lambda i: rows(halo, i // 4),
            lambda i: rows(xlo, 12 + i // 4),
            lambda i: rows(xhi, 12 + i // 4),
            4 * g,
        )
        for g in range(10)
    ]
    y_rows(planes, 0, down, up)


def halve(pairs, rows, z_map, dst, scale):
    rows[...] = dot(pairs[...], z_map)
    for p in range(MX):
        at = p * EY
        total = rows[pl.ds(at, MR, stride=2), :] + rows[pl.ds(at + 1, MR, stride=2), :]
        dst[p, :MR] = total * scale
        dst[p, MR:] = jnp.zeros((MY - MR, MZ), F32)


def pre_kernel(first, *refs):
    if first:
        right_side, diagonal, xlo, xhi, zl, zr, ylo, yhi = refs[:8]
        refs = refs[8:]
        assemble_field(refs[7], first_parts(0, right_side, xlo, xhi, zl, zr, ylo, yhi))
    else:
        own, halo, xlo, xhi, ylo, yhi = refs[:6]
        refs = refs[6:]
        assemble_field(refs[7], later_parts(own, halo, xlo, xhi, ylo, yhi))
    d0, d1, zs, rs, z1, left1, packed, field, zfull, pairs, rows, r1, small = refs
    z_map = halving(EZ, MZ)
    if first:
        assemble_diagonal(d0, first_parts(1, diagonal, xlo, xhi, zl, zr, ylo, yhi))
        for i in range(MX):
            pairs[i * EY : (i + 1) * EY, :] = d0[2 * i] + d0[2 * i + 1]
        halve(pairs, rows, z_map, d1, 0.125)
    pairs[0:EY, :] = jnp.zeros((EY, EZ), F32)
    pairs[(MX - 1) * EY :, :] = jnp.zeros((EY, EZ), F32)
    mask = x_masks(plane_mask(0, (EY, EZ), -HY), 0, CA)

    def smooth(p):
        r = field[p]
        box = spread(field[p - 1] + r + field[p + 1])
        z = (CR + CA * d0[p]) * r - mask(p) * box
        zfull[p] = z
        if 10 <= p < 30:
            zs[p - 10] = z[8:48]

    def rest(p):
        z = zfull[p]
        left = field[p] - d0[p] * z + spread(zfull[p - 1] + z + zfull[p + 1])
        if 10 <= p < 30:
            rs[p - 10] = left[8:48]
        return left

    def rest_pair(i):
        pairs[i * EY : (i + 1) * EY, :] = rest(2 * i) + rest(2 * i + 1)

    loop(1, EX - 1, smooth)
    loop(1, MX - 1, rest_pair)
    halve(pairs, rows, z_map, r1, 0.5)
    mask1 = plane_mask(1, (MY, MZ), -HY // 2)
    keep1, mask1 = x_masks(mask1, 1), x_masks(mask1, 1, CA)

    def mask_one(p):
        r1[p] = r1[p] * keep1(p)

    loop(0, MX, mask_one)

    def smooth_one(p):
        r = r1[p]
        box = spread(r1[p - 1] + r + r1[p + 1])
        z1[p] = (CR + CA * d1[p]) * r - mask1(p) * box

    zero = jnp.zeros((MY, MZ), F32)
    for ref in (z1, left1):
        ref[0] = zero
        ref[MX - 1] = zero
    loop(1, MX - 1, smooth_one)

    def rest_one(p):
        z = z1[p]
        left1[p] = r1[p] - d1[p] * z + spread(z1[p - 1] + z + z1[p + 1])

    loop(1, MX - 1, rest_one)

    lane = lax.broadcasted_iota(jnp.int32, (MZ, 128), 0)
    col = lax.broadcasted_iota(jnp.int32, (MZ, 128), 1)

    def pack(src, scale):
        total = jnp.zeros((16, 128), F32)
        for k in range(4):
            s = src[6 + 2 * k, 6:22, :] + src[7 + 2 * k, 6:22, :]
            total = total + dot(s, flag((lane // 2 + 32 * k == col) & (lane < 64)))
        small[...] = total
        return (small[pl.ds(0, 8, stride=2), :] + small[pl.ds(1, 8, stride=2), :]) * scale

    tile = pack(left1, 0.5)
    if first:
        tile = jnp.concatenate([tile, pack(d1, 0.125)], axis=0)
    for i in range(GX * GZ):
        packed[i] = tile


def unpack(dst, row, lo, own, hi):
    group = lax.broadcasted_iota(jnp.int32, (8, 128), 1) // 32
    for part, src in enumerate((lo, own, hi)):
        for bx in range(GX):
            for k in range(4):
                halves = []
                for h in range(2):
                    acc = None
                    for j in range(4):
                        block = src[bx * GZ + 4 * h + j, row : row + 8, :]
                        shift = (32 * (j - k)) % 128
                        if shift:
                            block = pltpu.roll(block, shift, 1)
                        acc = block if acc is None else jnp.where(group == j, block, acc)
                    halves.append(acc)
                dst[1 + 4 * bx + k, 8 * part : 8 * part + 8, :] = jnp.concatenate(halves, axis=1)


def coarse(r2, d2, s0, s1, z2, gy):
    shape = (24, 256)
    row = lax.broadcasted_iota(jnp.int32, shape, 0) + (gy * 8 - 8)
    mask = flag((row >= 0) & (row < 64))
    lane = lax.broadcasted_iota(jnp.int32, shape, 1)

    def box(t):
        t = t + pltpu.roll(t, 1, 0) + pltpu.roll(t, 23, 0)
        return (
            t
            + jnp.where(lane == 0, 0.0, pltpu.roll(t, 1, 1))
            + jnp.where(lane == 255, 0.0, pltpu.roll(t, 255, 1))
        )

    theta, delta = 29.5, 28.5
    sigma = theta / delta
    rho = 1.0 / sigma
    rho1 = 1.0 / (2.0 * sigma - rho)
    rho2 = 1.0 / (2.0 * sigma - rho1)
    zero = jnp.zeros(shape, F32)
    for ref in (r2, s0, s1, z2):
        ref[0] = zero
        ref[17] = zero

    def scale(p):
        r2[p] = r2[p] * mask

    loop(1, 17, scale)

    def one(p):
        r = r2[p]
        step = r * (1.0 / theta)
        remain = mask * (r - d2[p] * step + box(r2[p - 1] + r + r2[p + 1]) * (1.0 / theta))
        s0[p] = remain
        s1[p] = (rho1 * rho) * step + (2.0 * rho1 / delta) * remain

    loop(1, 17, one)

    def two(p):
        step = s1[p]
        remain = mask * (s0[p] - d2[p] * step + box(s1[p - 1] + step + s1[p + 1]))
        last = (rho2 * rho1) * step + (2.0 * rho2 / delta) * remain
        z2[p] = r2[p] * (1.0 / theta) + step + last

    loop(1, 17, two)

    def three(p):
        y = z2[p]
        left = r2[p] - d2[p] * y + box(z2[p - 1] + y + z2[p + 1])
        top = jnp.sum(left, axis=1, keepdims=True)
        low = jnp.sum(d2[p] - 26.0, axis=1, keepdims=True)
        s0[p] = mask * (y + top / low)

    loop(1, 17, three)


def post_kernel(first, *refs):
    if first:
        (lo, own, hi, zs, rs, z1, left1, d0, d1,
         d2, z_core, q_core, q_down, q_up, q_halo,
         r2, s0, s1, z2, wide, rows1, u, rem, zf1, rowsv, v, sv, rem0, zf0) = refs
    else:
        (lo, own, hi, zs, rs, z1, left1, d0, d1, d2,
         z_core, q_core,
         r2, s0, s1, z2, wide, rows1, u, rem, zf1, rowsv, v, sv, rem0, zf0) = refs
    gx, gy, gz = places()
    unpack(r2, 0, lo, own, hi)
    if first:
        unpack(d2, 8, lo, own, hi)
    coarse(r2, d2, s0, s1, z2, gy)

    lane = lax.broadcasted_iota(jnp.int32, (16, 128), 1)
    z = jnp.where(lane < 48, lane, lane - 64) + 32 * gz
    in2 = flag((z >= 0) & (z < 256) & (lane < 64))
    turned = (256 - 32 * gz) % 256
    for i in range(10):
        p = 4 * gx - 3 + i
        plane = pltpu.roll(s0[jnp.clip(p + 1, 0, 17)], turned, 1)[5:21]
        plane = jnp.where(lane < 48, plane[:, :128], turn(plane[:, 128:], 64))
        wide[16 * i : 16 * i + 16, :] = plane * (in2 * flag((p >= 0) & (p < 16)))
    up = dot(wide[...], doubling(128, 128))
    rows1[pl.ds(0, 160, stride=2), :] = up
    rows1[pl.ds(1, 160, stride=2), :] = up
    u[...] = rows1[...].reshape(10, 32, 128)

    mask1 = plane_mask(1, (MY, MZ), -HY // 2)
    keep1, mask1 = x_masks(mask1, 1), x_masks(mask1, 1, CA)

    def remain_one(p):
        c = u[p // 2]
        total = u[(p - 1) // 2] + c + u[(p + 1) // 2]
        rem[p] = keep1(p) * (left1[p] - d1[p] * c + spread(total))

    loop(3, 17, remain_one)

    def final_one(p):
        r = rem[p]
        box = spread(rem[p - 1] + r + rem[p + 1])
        f = z1[p] + u[p // 2] + ((CR + CA * d1[p]) * r - mask1(p) * box)
        zf1[(p - 4) * 20 : (p - 3) * 20, :] = f[4:24]

    loop(4, 16, final_one)

    rowsv[pl.ds(0, 240, stride=2), :] = zf1[...]
    rowsv[pl.ds(1, 240, stride=2), :] = zf1[...]
    v[...] = dot(rowsv[...], doubling(128, 256)).reshape(12, PY, EZ)
    for i in range(12):
        sv[i] = spread(v[i])

    mask0 = plane_mask(0, (PY, EZ), -4)
    keep0, mask0 = x_masks(mask0, 0), x_masks(mask0, 0, CA)

    def remain(i):
        p = i + 10
        at = p // 2 - 4
        other = (p - 1) // 2 - 4 if p % 2 == 0 else (p + 1) // 2 - 4
        rem0[i] = keep0(p) * (rs[i] - d0[p, 8:48, :] * v[at] + (2.0 * sv[at] + sv[other]))

    loop(0, 20, remain)

    def final(i):
        p = i + 10
        r = rem0[i]
        box = spread(rem0[i - 1] + r + rem0[i + 1])
        zf0[i] = zs[i] + v[p // 2 - 4] + ((CR + CA * d0[p, 8:48, :]) * r - mask0(p) * box)

    loop(1, 19, final)

    group = lax.broadcasted_iota(jnp.int32, (BY, BZ), 1) // 32

    def apply(i):
        c = zf0[i + 2]
        q = d0[i + HX, 8:48, :] * c - spread(zf0[i + 1] + c + zf0[i + 3])
        q_own = q[4:36, :BZ]
        z_core[i] = c[4:36, :BZ]
        q_core[i] = q_own
        if first:
            if i < 12:
                q_down[i] = q_own
            if i >= 4:
                q_up[i - 4] = q_own
            g, k = i // 4, i % 4
            halo = turn(q[4:36, BZ:], 32 * k - 112)
            if k:
                halo = jnp.where(group == k, halo, q_halo[g])
            q_halo[g] = halo
            if k == 3 and g < 3:
                q_down[12 + g] = halo
            if k == 3 and g > 0:
                q_up[11 + g] = halo

    loop(0, BX, apply)


def dots_kernel(r, z, q, p, w, dots):
    acc = [None] * 9
    for i in range(BX):
        ri, zi, qi, pi, wi = r[i], z[i], q[i], p[i], w[i]
        r1, z1, w1 = ri - qi, zi - pi, qi - wi
        terms = (
            ri * zi, zi * qi, r1 * z1, r1 * pi + qi * z1, qi * pi,
            z1 * w1, z1 * wi + pi * w1, pi * wi, z1 * qi,
        )
        for k, term in enumerate(terms):
            acc[k] = term if i == 0 else acc[k] + term
    lane = lax.broadcasted_iota(jnp.int32, (1, 128), 1)
    row = jnp.zeros((1, 128), F32)
    for k, part in enumerate(acc):
        total = jnp.sum(jnp.sum(part, axis=0, keepdims=True), axis=1, keepdims=True)
        row = jnp.where(lane == k, total, row)
    dots[...] = jnp.broadcast_to(row[None], (GY * GZ, 1, 128))


def end_kernel(r, z, q, p, w, m0, m1, m2, m3, solution_field, residual):
    last = jnp.sum(m0[...] + m1[...] + m2[...] + m3[...], axis=0)
    lane = lax.broadcasted_iota(jnp.int32, (1, 128), 1)
    at = lambda i: jnp.sum(jnp.where(lane == i, last, 0.0), axis=1, keepdims=True)
    rz, curve = at(0), at(1)
    alpha = rz / curve
    t = alpha - 1.0
    rz2 = at(2) - t * at(3) + t * t * at(4)
    zw = at(5) - t * at(6) + t * t * at(7)
    zq = at(8) - t * at(4)
    beta = rz2 / rz
    alpha2 = rz2 / (zw + 2.0 * beta * zq + beta * beta * curve)

    def body(i):
        zi, qi = z[i], q[i]
        solution_field[i] = alpha * zi + alpha2 * ((zi - alpha * p[i]) + beta * zi)
        residual[i] = (r[i] - alpha * qi) - alpha2 * ((qi - alpha * w[i]) + beta * qi)

    loop(0, BX, body)


def shape(*dims):
    return jax.ShapeDtypeStruct(dims, F32)


def call(kernel, outs, scratch, *args):
    whole = pl.BlockSpec(memory_space=pltpu.VMEM)
    return pl.pallas_call(
        kernel,
        out_shape=outs,
        in_specs=[whole] * len(args),
        out_specs=jax.tree.map(lambda _: whole, outs),
        scratch_shapes=[pltpu.VMEM(s, F32) for s in scratch],
        compiler_params=pltpu.CompilerParams(vmem_limit_bytes=24 * 1024 * 1024),
    )(*args)


def shift(value, axis, count, by):
    return lax.ppermute(value, axis, [(i, (i + by) % count) for i in range(count)])


def spread_coarse(packed):
    own = lax.all_to_all(packed, ("gx", "gz"), 0, 0)
    return shift(own, "gy", GY, 1), own, shift(own, "gy", GY, -1)


def pre_call(first, *args):
    kept = (shape(20, PY, EZ), shape(20, PY, EZ), shape(MX, MY, MZ), shape(MX, MY, MZ),
            shape(GX * GZ, 16 if first else 8, 128))
    scratch = [(EX, EY, EZ), (EX, EY, EZ), (MX * EY, EZ), (MX * EY, MZ), (MX, MY, MZ), (16, 128)]
    kernel = functools.partial(pre_kernel, first)
    if first:
        kept = (shape(EX, EY, EZ), shape(MX, MY, MZ)) + kept
    return call(kernel, kept, scratch, *args)


def post_call(parts, kept, d0, d1, d2=None):
    first = d2 is None
    scratch = [(18, 24, 256)] * 4 + [
        (160, 128), (320, 128), (10, 32, 128), (MX, MY, MZ), (240, 128),
        (480, 128), (12, PY, EZ), (12, PY, EZ), (20, PY, EZ), (20, PY, EZ),
    ]
    core = shape(BX, BY, BZ)
    kernel = functools.partial(post_kernel, first)
    if first:
        slab = shape(15, BY, BZ)
        outs = (shape(18, 24, 256), core, core, slab, slab, shape(4, BY, BZ))
        return call(kernel, outs, scratch, *parts, *kept, d0, d1)
    return call(kernel, (core, core), scratch, *parts, *kept, d0, d1, d2)


def first_exchange(right_side, diagonal):
    def slab(lo, hi):
        return jnp.stack([right_side[lo:hi], diagonal[lo:hi]])

    xlo = shift(slab(BX - HX, BX), "gx", GX, 1)
    xhi = shift(slab(0, HX), "gx", GX, -1)
    edge = shape(2, EX // 5, BY, BZ)
    down, up = call(z_pack_kernel, (edge, edge), [], right_side, diagonal, xlo, xhi)
    zl = shift(up, "gz", GZ, 1)
    zr = shift(down, "gz", GZ, -1)
    edge = shape(168, 8, BZ)
    pieces = (right_side, diagonal, xlo, xhi, zl, zr)
    down, up = call(y_pack_kernel, (edge, edge), [], *pieces)
    return *pieces, shift(up, "gy", GY, 1), shift(down, "gy", GY, -1)


def later_exchange(q, q_down, q_up, q_halo):
    xlo = shift(q_up, "gx", GX, 1)
    xhi = shift(q_down, "gx", GX, -1)
    edge = shape(75, 8, BZ)
    down, up = call(y_pack_later_kernel, (edge, edge), [], q, q_halo, xlo, xhi)
    return q, q_halo, xlo, xhi, shift(up, "gy", GY, 1), shift(down, "gy", GY, -1)


def local(right_side, diagonal):
    d0, d1, *kept = pre_call(True, *first_exchange(right_side, diagonal))
    d2, z, q, *edges = post_call(spread_coarse(kept[-1]), kept[:-1], d0, d1)
    kept = pre_call(False, *later_exchange(q, *edges), d0, d1)
    p, w = post_call(spread_coarse(kept[-1]), kept[:-1], d0, d1, d2=d2)
    fields = (right_side, z, q, p, w)
    more = call(dots_kernel, shape(GY * GZ, 1, 128), [], *fields)
    more = lax.all_to_all(more, ("gy", "gz"), 0, 0)
    others = [shift(more, "gx", GX, i) for i in (1, 2, 3)]
    core = shape(BX, BY, BZ)
    return call(end_kernel, (core, core), [], *fields, more, *others)


def solution(mesh):
    return jax.shard_map(
        local, mesh=mesh, in_specs=(SPEC, SPEC), out_specs=(SPEC, SPEC), check_vma=False
    )
```

time: 159 us -> 150 us (0.943)
  starting transfers between devices: 34.4 us -> 30.7 us
  Pallas kernels: 26.4 us -> 23.4 us
  blocking collectives: 53.4 us -> 51.4 us
    ppermute x19 -> x17, starting transfers between devices: 34.4 us -> 30.7 us  [shift(): lax.ppermute(value, axis, [(i, (i + by) % count) for i in range(count)])]
    pallas_call x9, Pallas kernels: 26.4 us -> 23.4 us  [call(): pl.pallas_call(kernel, out_shape=outs, in_specs=[whole] * len(args), out_...]
    ppermute x19 -> x17, waiting for transfers between devices: 41.9 us -> 42 us  [shift(): lax.ppermute(value, axis, [(i, (i + by) % count) for i in range(count)])]
  transfers between devices with their start and end apart: 19 -> 17, of which waited for: 13 -> 14; matrix products, arithmetic and copies ran while one was open for 0% -> 0% of each run, Pallas kernels for 4% -> 0%
where the time goes in v3:
time: 150 us; the launch traced here: 149 us
  blocking collectives  51.4 us (34%)
  waiting for transfers between devices  42 us (28%)
  starting transfers between devices  30.7 us (20%)
  Pallas kernels  23.4 us (16%)
    ppermute x17, waiting for transfers between devices, shift(): lax.ppermute(value, axis, [(i, (i + by) % count) for i in range(count)])  42 us
    all_to_all x2, blocking collectives, spread_coarse(): own = lax.all_to_all(packed, ('gx', 'gz'), 0, 0)  34 us
    ppermute x17, starting transfers between devices, shift(): lax.ppermute(value, axis, [(i, (i + by) % count) for i in range(count)])  30.7 us
    pallas_call x9, Pallas kernels, call(): pl.pallas_call(kernel, out_shape=outs, in_specs=[whole] * len(args), out_...  23.4 us
    all_to_all x1, blocking collectives, local(): more = lax.all_to_all(more, ('gy', 'gz'), 0, 0)  17.3 us
  transfers between devices with their start and end apart: 17, of which 14 were waited for; matrix products, arithmetic and copies ran while one was open for 0% of the time, Pallas kernels for 0%

profile of v3, /device:TPU:1, one launch (start us, length us, event | category | flops | bytes accessed | tf_op | source)
XLA Modules:
  0.0 149.5 jit_solution(7364324877799480772)
XLA Ops:
  0.6 0.0 copy-start
  0.6 1.3 slice_bitcast_fusion
  2.0 2.1 %collective-permute-start = (f32[2,12,32,128]{3,2,1,0:T(8,128)S(1)}, f32[2,12,32,128]{3,2,1,0:T(8,128)S(1)}, u32[]{:S(2)}, u32[]{:S(2)}) collective-permute-start(f32[2,12,32,128]{3,2,1,0:T(8,128)S(1)} %pad_maximum_fusion), channel_id=1, source_target_pairs={{0,64},{64,128},{128,192},{192,0},{1,65},{65,129},{129,193},{193,1... | collective-permute-start | bytes 1179656 | tf_op jit(solution)/shard_map/ppermute | solution.py:548
  4.2 1.4 collective-permute-start.1
  5.5 6.4 %collective-permute-done.xlo.refs_2_ = f32[2,12,32,128]{3,2,1,0:T(8,128)S(1)} collective-permute-done((f32[2,12,32,128]{3,2,1,0:T(8,128)S(1)}, f32[2,12,32,128]{3,2,1,0:T(8,128)S(1)}, u32[]{:S(2)}, u32[]{:S(2)}) %collective-permute-start) | collective-permute-done | bytes 393248 | tf_op jit(solution)/shard_map/ppermute | solution.py:548
  11.9 1.7 %collective-permute-done.1.xhi.refs_3_ = f32[2,12,32,128]{3,2,1,0:T(8,128)S(1)} collective-permute-done((f32[2,12,32,128]{3,2,1,0:T(8,128)S(1)}, f32[2,12,32,128]{3,2,1,0:T(8,128)S(1)}, u32[]{:S(2)}, u32[]{:S(2)}) %collective-permute-start.1) | collective-permute-done | bytes 393248 | tf_op jit(solution)/shard_map/ppermute | solution.py:548
  13.6 0.7 shard_map.41
  14.3 2.2 %collective-permute-start.2 = (f32[2,8,32,128]{3,2,1,0:T(8,128)S(1)}, f32[2,8,32,128]{3,2,1,0:T(8,128)S(1)}, u32[]{:S(2)}, u32[]{:S(2)}) collective-permute-start(f32[2,8,32,128]{3,2,1,0:T(8,128)S(1)} %get-tuple-element.28), channel_id=1, source_target_pairs={{0,1},{1,2},{2,3},{3,4},{4,5},{5,6},{6,7},{7,0},{8,9},{9,10},{10,1... | collective-permute-start | bytes 786440 | tf_op jit(solution)/shard_map/ppermute | solution.py:548
  16.5 4.0 %collective-permute-start.3 = (f32[2,8,32,128]{3,2,1,0:T(8,128)S(1)}, f32[2,8,32,128]{3,2,1,0:T(8,128)S(1)}, u32[]{:S(2)}, u32[]{:S(2)}) collective-permute-start(f32[2,8,32,128]{3,2,1,0:T(8,128)S(1)} %get-tuple-element.29), channel_id=1, source_target_pairs={{0,7},{1,0},{2,1},{3,2},{4,3},{5,4},{6,5},{7,6},{8,15},{9,8},{10,9... | collective-permute-start | bytes 786440 | tf_op jit(solution)/shard_map/ppermute | solution.py:548
  20.5 4.9 %collective-permute-done.2.zl.refs_4_ = f32[2,8,32,128]{3,2,1,0:T(8,128)S(1)} collective-permute-done((f32[2,8,32,128]{3,2,1,0:T(8,128)S(1)}, f32[2,8,32,128]{3,2,1,0:T(8,128)S(1)}, u32[]{:S(2)}, u32[]{:S(2)}) %collective-permute-start.2) | collective-permute-done | bytes 262176 | tf_op jit(solution)/shard_map/ppermute | solution.py:548
  25.4 0.0 collective-permute-done.3.zr.refs_5_
  25.4 0.1 shard_map.42
  25.5 3.5 %collective-permute-start.4 = (f32[168,8,128]{2,1,0:T(8,128)S(1)}, f32[168,8,128]{2,1,0:T(8,128)S(1)}, u32[]{:S(2)}, u32[]{:S(2)}) collective-permute-start(f32[168,8,128]{2,1,0:T(8,128)S(1)} %get-tuple-element.30), channel_id=1, source_target_pairs={{0,8},{8,16},{16,24},{24,32},{32,40},{40,48},{48,56},{56,0},{1,9},... | collective-permute-start | bytes 2064392 | tf_op jit(solution)/shard_map/ppermute | solution.py:548
  29.0 0.0 collective-permute-start.5
  29.0 7.9 %collective-permute-done.4.refs_6_ = f32[168,8,128]{2,1,0:T(8,128)S(1)} collective-permute-done((f32[168,8,128]{2,1,0:T(8,128)S(1)}, f32[168,8,128]{2,1,0:T(8,128)S(1)}, u32[]{:S(2)}, u32[]{:S(2)}) %collective-permute-start.4) | collective-permute-done | bytes 688160 | tf_op jit(solution)/shard_map/ppermute | solution.py:548
  36.9 2.5 %collective-permute-done.5.refs_7_ = f32[168,8,128]{2,1,0:T(8,128)S(1)} collective-permute-done((f32[168,8,128]{2,1,0:T(8,128)S(1)}, f32[168,8,128]{2,1,0:T(8,128)S(1)}, u32[]{:S(2)}, u32[]{:S(2)}) %collective-permute-start.5) | collective-permute-done | bytes 688160 | tf_op jit(solution)/shard_map/ppermute | solution.py:548
  39.4 5.4 %shard_map.43 = (f32[40,56,256]{2,1,0:T(8,128)S(1)}, f32[20,32,128]{2,1,0:T(8,128)S(1)}, f32[20,40,256]{2,1,0:T(8,128)S(1)}, f32[20,40,256]{2,1,0:T(8,128)S(1)},...) custom-call(f32[16,32,128]{2,1,0:T(8,128)S(1)} %copy-done, ...), custom_call_target="tpu_custom_call" | custom-call | tf_op jit(solution)/shard_map/pallas_call | solution.py:537
  44.8 18.2 %all_to_all.15.refs_1_ = f32[32,16,128]{2,1,0:T(8,128)S(1)} all-to-all(f32[32,16,128]{2,1,0:T(8,128)S(1)} %get-tuple-element.32), channel_id=1, replica_groups=mesh['gx'=4,'gy'=8,'gz'=8] {'gx','gz'}, dimensions={0} | all-to-all | bytes 524288 | tf_op jit(solution)/shard_map/all_to_all | solution.py:552
  63.0 2.4 %collective-permute-start.7 = (f32[32,16,128]{2,1,0:T(8,128)S(1)}, f32[32,16,128]{2,1,0:T(8,128)S(1)}, u32[]{:S(2)}, u32[]{:S(2)}) collective-permute-start(f32[32,16,128]{2,1,0:T(8,128)S(1)} %all_to_all.15.refs_1_), channel_id=1, source_target_pairs={{0,56},{8,0},{16,8},{24,16},{32,24},{40,32},{48,40},{56,48},{1,57}... | collective-permute-start | bytes 786440 | tf_op jit(solution)/shard_map/ppermute | solution.py:548
  65.4 0.0 collective-permute-start.6
  65.4 3.4 %collective-permute-done.7.refs_2_ = f32[32,16,128]{2,1,0:T(8,128)S(1)} collective-permute-done((f32[32,16,128]{2,1,0:T(8,128)S(1)}, f32[32,16,128]{2,1,0:T(8,128)S(1)}, u32[]{:S(2)}, u32[]{:S(2)}) %collective-permute-start.7) | collective-permute-done | bytes 262176 | tf_op jit(solution)/shard_map/ppermute | solution.py:548
  68.8 0.0 collective-permute-done.6.refs_0_
  68.8 6.4 %shard_map.44 = (f32[18,24,256]{2,1,0:T(8,128)S(1)}, f32[16,32,128]{2,1,0:T(8,128)S(1)}, f32[16,32,128]{2,1,0:T(8,128)S(1)}, f32[15,32,128]{2,1,0:T(8,128)S(1)},...) custom-call(f32[32,16,128]{2,1,0:T(8,128)S(1)} %collective-permute-done.6.refs_0_, ...), custom_call_target="tpu_custom_call" | custom-call | tf_op jit(solution)/shard_map/pallas_call | solution.py:537
  75.2 0.8 collective-permute-start.8
  75.9 2.0 %collective-permute-start.9 = (f32[15,32,128]{2,1,0:T(8,128)S(1)}, f32[15,32,128]{2,1,0:T(8,128)S(1)}, u32[]{:S(2)}, u32[]{:S(2)}) collective-permute-start(f32[15,32,128]{2,1,0:T(8,128)S(1)} %get-tuple-element.43), channel_id=1, source_target_pairs={{0,192},{64,0},{128,64},{192,128},{1,193},{65,1},{129,65},{193,129... | collective-permute-start | bytes 737288 | tf_op jit(solution)/shard_map/ppermute | solution.py:548
  77.9 3.6 %collective-permute-done.8.xlo.refs_2_ = f32[15,32,128]{2,1,0:T(8,128)S(1)} collective-permute-done((f32[15,32,128]{2,1,0:T(8,128)S(1)}, f32[15,32,128]{2,1,0:T(8,128)S(1)}, u32[]{:S(2)}, u32[]{:S(2)}) %collective-permute-start.8) | collective-permute-done | bytes 245792 | tf_op jit(solution)/shard_map/ppermute | solution.py:548
  81.5 0.0 collective-permute-done.9.xhi.refs_3_
  81.5 0.1 shard_map.45
  81.5 5.5 %collective-permute-start.10 = (f32[75,8,128]{2,1,0:T(8,128)S(1)}, f32[75,8,128]{2,1,0:T(8,128)S(1)}, u32[]{:S(2)}, u32[]{:S(2)}) collective-permute-start(f32[75,8,128]{2,1,0:T(8,128)S(1)} %get-tuple-element.44), channel_id=1, source_target_pairs={{0,8},{8,16},{16,24},{24,32},{32,40},{40,48},{48,56},{56,0},{1,9},... | collective-permute-start | bytes 921608 | tf_op jit(solution)/shard_map/ppermute | solution.py:548
  87.0 1.1 collective-permute-start.11
  88.1 2.7 %collective-permute-done.10.refs_4_ = f32[75,8,128]{2,1,0:T(8,128)S(1)} collective-permute-done((f32[75,8,128]{2,1,0:T(8,128)S(1)}, f32[75,8,128]{2,1,0:T(8,128)S(1)}, u32[]{:S(2)}, u32[]{:S(2)}) %collective-permute-start.10) | collective-permute-done | bytes 307232 | tf_op jit(solution)/shard_map/ppermute | solution.py:548
  90.8 2.8 %collective-permute-done.11.refs_5_ = f32[75,8,128]{2,1,0:T(8,128)S(1)} collective-permute-done((f32[75,8,128]{2,1,0:T(8,128)S(1)}, f32[75,8,128]{2,1,0:T(8,128)S(1)}, u32[]{:S(2)}, u32[]{:S(2)}) %collective-permute-start.11) | collective-permute-done | bytes 307232 | tf_op jit(solution)/shard_map/ppermute | solution.py:548
  93.6 4.2 %shard_map.46 = (f32[20,40,256]{2,1,0:T(8,128)S(1)}, f32[20,40,256]{2,1,0:T(8,128)S(1)}, f32[20,32,128]{2,1,0:T(8,128)S(1)}, f32[20,32,128]{2,1,0:T(8,128)S(1)}, f32[32,8,128]{2,1,0:T(8,128)S(1)}) custom-call(f32[16,32,128]{2,1,0:T(8,128)S(1)} %get-tuple-element.40.own.refs_0_.q, f32[4,32,128]{2,1,0:T(8,128)S(1)} %get-tuple-element.41.halo.refs_1_, ...), custom_call_target="tpu_custom_call" | custom-call | tf_op jit(solution)/shard_map/pallas_call | solution.py:537
  97.8 15.8 %all_to_all.16.refs_1_ = f32[32,8,128]{2,1,0:T(8,128)S(1)} all-to-all(f32[32,8,128]{2,1,0:T(8,128)S(1)} %get-tuple-element.46), channel_id=1, replica_groups=mesh['gx'=4,'gy'=8,'gz'=8] {'gx','gz'}, dimensions={0} | all-to-all | bytes 262144 | tf_op jit(solution)/shard_map/all_to_all | solution.py:552
  113.6 3.6 %collective-permute-start.13 = (f32[32,8,128]{2,1,0:T(8,128)S(1)}, f32[32,8,128]{2,1,0:T(8,128)S(1)}, u32[]{:S(2)}, u32[]{:S(2)}) collective-permute-start(f32[32,8,128]{2,1,0:T(8,128)S(1)} %all_to_all.16.refs_1_), channel_id=1, source_target_pairs={{0,56},{8,0},{16,8},{24,16},{32,24},{40,32},{48,40},{56,48},{1,57}... | collective-permute-start | bytes 393224 | tf_op jit(solution)/shard_map/ppermute | solution.py:548
  117.2 0.0 collective-permute-start.12
  117.2 1.0 collective-permute-done.13.refs_2_
  118.2 1.2 collective-permute-done.12.refs_0_
  119.4 5.2 %shard_map.47 = (f32[16,32,128]{2,1,0:T(8,128)S(1)}, f32[16,32,128]{2,1,0:T(8,128)S(1)}) custom-call(f32[32,8,128]{2,1,0:T(8,128)S(1)} %collective-permute-done.12.refs_0_, f32[32,8,128]{2,1,0:T(8,128)S(1)} %all_to_all.16.refs_1_, f32[32,8,128]{2,1,0:T(8,128)S(1)} %collective-permute-done.13.refs_2_, f32[20,40,256]{2,1,0:T(8,128)S(1)} %get-tuple-element.47.refs_3_, ...), custom_call_target="tpu_custom_call" | custom-call | tf_op jit(solution)/shard_map/pallas_call | solution.py:537
  124.6 0.4 shard_map.48
  125.0 17.3 %all_to_all.17.m0 = f32[64,1,128]{2,1,0:T(1,128)S(1)} all-to-all(f32[64,1,128]{2,1,0:T(1,128)S(1)} %shard_map.48), channel_id=1, replica_groups=mesh['gx'=4,'gy'=8,'gz'=8] {'gy','gz'}, dimensions={0} | all-to-all | bytes 65536 | tf_op jit(solution)/shard_map/all_to_all | solution.py:612
  142.3 0.9 collective-permute-start.16
  143.2 1.2 collective-permute-start.15
  144.4 0.0 collective-permute-start.14
  144.4 0.6 collective-permute-done.16.m3
  145.1 2.4 %collective-permute-done.15.m2 = f32[64,1,128]{2,1,0:T(1,128)S(1)} collective-permute-done((f32[64,1,128]{2,1,0:T(1,128)S(1)}, f32[64,1,128]{2,1,0:T(1,128)S(1)}, u32[]{:S(2)}, u32[]{:S(2)}) %collective-permute-start.15) | collective-permute-done | bytes 32800 | tf_op jit(solution)/shard_map/ppermute | solution.py:548
  147.5 0.9 collective-permute-done.14.m1
  148.4 1.1 shard_map.49
  (5 shorter events, 0.1 us)
Async XLA Ops:
  0.6 13.0 %copy-start = (f32[16,32,128]{2,1,0:T(8,128)S(1)}, f32[16,32,128]{2,1,0:T(8,128)}, u32[]{:S(2)}) copy-start(f32[16,32,128]{2,1,0:T(8,128)} %r.3) | copy-start | bytes 786436
  0.6 13.0 %copy-start.1 = (f32[16,32,128]{2,1,0:T(8,128)S(1)}, f32[16,32,128]{2,1,0:T(8,128)}, u32[]{:S(2)}) copy-start(f32[16,32,128]{2,1,0:T(8,128)} %refs_1_.1) | copy-start | bytes 786436
  2.0 9.9 %collective-permute-start = (f32[2,12,32,128]{3,2,1,0:T(8,128)S(1)}, f32[2,12,32,128]{3,2,1,0:T(8,128)S(1)}, u32[]{:S(2)}, u32[]{:S(2)}) collective-permute-start(f32[2,12,32,128]{3,2,1,0:T(8,128)S(1)} %pad_maximum_fusion), channel_id=1, source_target_pairs={{0,64},{64,128},{128,192},{192,0},{1,65},{65,129},{129,193},{193,1... | collective-permute-start | bytes 1179656 | tf_op jit(solution)/shard_map/ppermute | solution.py:548
  4.2 9.5 %collective-permute-start.1 = (f32[2,12,32,128]{3,2,1,0:T(8,128)S(1)}, f32[2,12,32,128]{3,2,1,0:T(8,128)S(1)}, u32[]{:S(2)}, u32[]{:S(2)}) collective-permute-start(f32[2,12,32,128]{3,2,1,0:T(8,128)S(1)} %pad_maximum_fusion.1), channel_id=1, source_target_pairs={{0,192},{64,0},{128,64},{192,128},{1,193},{65,1},{129,65},{193,129... | collective-permute-start | bytes 1179656 | tf_op jit(solution)/shard_map/ppermute | solution.py:548
  14.3 11.1 %collective-permute-start.2 = (f32[2,8,32,128]{3,2,1,0:T(8,128)S(1)}, f32[2,8,32,128]{3,2,1,0:T(8,128)S(1)}, u32[]{:S(2)}, u32[]{:S(2)}) collective-permute-start(f32[2,8,32,128]{3,2,1,0:T(8,128)S(1)} %get-tuple-element.28), channel_id=1, source_target_pairs={{0,1},{1,2},{2,3},{3,4},{4,5},{5,6},{6,7},{7,0},{8,9},{9,10},{10,1... | collective-permute-start | bytes 786440 | tf_op jit(solution)/shard_map/ppermute | solution.py:548
  16.5 8.9 %collective-permute-start.3 = (f32[2,8,32,128]{3,2,1,0:T(8,128)S(1)}, f32[2,8,32,128]{3,2,1,0:T(8,128)S(1)}, u32[]{:S(2)}, u32[]{:S(2)}) collective-permute-start(f32[2,8,32,128]{3,2,1,0:T(8,128)S(1)} %get-tuple-element.29), channel_id=1, source_target_pairs={{0,7},{1,0},{2,1},{3,2},{4,3},{5,4},{6,5},{7,6},{8,15},{9,8},{10,9... | collective-permute-start | bytes 786440 | tf_op jit(solution)/shard_map/ppermute | solution.py:548
  25.5 11.4 %collective-permute-start.4 = (f32[168,8,128]{2,1,0:T(8,128)S(1)}, f32[168,8,128]{2,1,0:T(8,128)S(1)}, u32[]{:S(2)}, u32[]{:S(2)}) collective-permute-start(f32[168,8,128]{2,1,0:T(8,128)S(1)} %get-tuple-element.30), channel_id=1, source_target_pairs={{0,8},{8,16},{16,24},{24,32},{32,40},{40,48},{48,56},{56,0},{1,9},... | collective-permute-start | bytes 2064392 | tf_op jit(solution)/shard_map/ppermute | solution.py:548
  29.0 10.4 %collective-permute-start.5 = (f32[168,8,128]{2,1,0:T(8,128)S(1)}, f32[168,8,128]{2,1,0:T(8,128)S(1)}, u32[]{:S(2)}, u32[]{:S(2)}) collective-permute-start(f32[168,8,128]{2,1,0:T(8,128)S(1)} %get-tuple-element.31), channel_id=1, source_target_pairs={{0,56},{8,0},{16,8},{24,16},{32,24},{40,32},{48,40},{56,48},{1,57}... | collective-permute-start | bytes 2064392 | tf_op jit(solution)/shard_map/ppermute | solution.py:548
  63.0 5.8 %collective-permute-start.7 = (f32[32,16,128]{2,1,0:T(8,128)S(1)}, f32[32,16,128]{2,1,0:T(8,128)S(1)}, u32[]{:S(2)}, u32[]{:S(2)}) collective-permute-start(f32[32,16,128]{2,1,0:T(8,128)S(1)} %all_to_all.15.refs_1_), channel_id=1, source_target_pairs={{0,56},{8,0},{16,8},{24,16},{32,24},{40,32},{48,40},{56,48},{1,57}... | collective-permute-start | bytes 786440 | tf_op jit(solution)/shard_map/ppermute | solution.py:548
  65.4 3.4 %collective-permute-start.6 = (f32[32,16,128]{2,1,0:T(8,128)S(1)}, f32[32,16,128]{2,1,0:T(8,128)S(1)}, u32[]{:S(2)}, u32[]{:S(2)}) collective-permute-start(f32[32,16,128]{2,1,0:T(8,128)S(1)} %all_to_all.15.refs_1_), channel_id=1, source_target_pairs={{0,8},{8,16},{16,24},{24,32},{32,40},{40,48},{48,56},{56,0},{1,9},... | collective-permute-start | bytes 786440 | tf_op jit(solution)/shard_map/ppermute | solution.py:548
  75.2 6.3 %collective-permute-start.8 = (f32[15,32,128]{2,1,0:T(8,128)S(1)}, f32[15,32,128]{2,1,0:T(8,128)S(1)}, u32[]{:S(2)}, u32[]{:S(2)}) collective-permute-start(f32[15,32,128]{2,1,0:T(8,128)S(1)} %get-tuple-element.42), channel_id=1, source_target_pairs={{0,64},{64,128},{128,192},{192,0},{1,65},{65,129},{129,193},{193,1... | collective-permute-start | bytes 737288 | tf_op jit(solution)/shard_map/ppermute | solution.py:548
  75.9 5.5 %collective-permute-start.9 = (f32[15,32,128]{2,1,0:T(8,128)S(1)}, f32[15,32,128]{2,1,0:T(8,128)S(1)}, u32[]{:S(2)}, u32[]{:S(2)}) collective-permute-start(f32[15,32,128]{2,1,0:T(8,128)S(1)} %get-tuple-element.43), channel_id=1, source_target_pairs={{0,192},{64,0},{128,64},{192,128},{1,193},{65,1},{129,65},{193,129... | collective-permute-start | bytes 737288 | tf_op jit(solution)/shard_map/ppermute | solution.py:548
  81.5 9.3 %collective-permute-start.10 = (f32[75,8,128]{2,1,0:T(8,128)S(1)}, f32[75,8,128]{2,1,0:T(8,128)S(1)}, u32[]{:S(2)}, u32[]{:S(2)}) collective-permute-start(f32[75,8,128]{2,1,0:T(8,128)S(1)} %get-tuple-element.44), channel_id=1, source_target_pairs={{0,8},{8,16},{16,24},{24,32},{32,40},{40,48},{48,56},{56,0},{1,9},... | collective-permute-start | bytes 921608 | tf_op jit(solution)/shard_map/ppermute | solution.py:548
  87.0 6.6 %collective-permute-start.11 = (f32[75,8,128]{2,1,0:T(8,128)S(1)}, f32[75,8,128]{2,1,0:T(8,128)S(1)}, u32[]{:S(2)}, u32[]{:S(2)}) collective-permute-start(f32[75,8,128]{2,1,0:T(8,128)S(1)} %get-tuple-element.45), channel_id=1, source_target_pairs={{0,56},{8,0},{16,8},{24,16},{32,24},{40,32},{48,40},{56,48},{1,57}... | collective-permute-start | bytes 921608 | tf_op jit(solution)/shard_map/ppermute | solution.py:548
  113.6 4.6 %collective-permute-start.13 = (f32[32,8,128]{2,1,0:T(8,128)S(1)}, f32[32,8,128]{2,1,0:T(8,128)S(1)}, u32[]{:S(2)}, u32[]{:S(2)}) collective-permute-start(f32[32,8,128]{2,1,0:T(8,128)S(1)} %all_to_all.16.refs_1_), channel_id=1, source_target_pairs={{0,56},{8,0},{16,8},{24,16},{32,24},{40,32},{48,40},{56,48},{1,57}... | collective-permute-start | bytes 393224 | tf_op jit(solution)/shard_map/ppermute | solution.py:548
  117.2 2.2 %collective-permute-start.12 = (f32[32,8,128]{2,1,0:T(8,128)S(1)}, f32[32,8,128]{2,1,0:T(8,128)S(1)}, u32[]{:S(2)}, u32[]{:S(2)}) collective-permute-start(f32[32,8,128]{2,1,0:T(8,128)S(1)} %all_to_all.16.refs_1_), channel_id=1, source_target_pairs={{0,8},{8,16},{16,24},{24,32},{32,40},{40,48},{48,56},{56,0},{1,9},... | collective-permute-start | bytes 393224 | tf_op jit(solution)/shard_map/ppermute | solution.py:548
  142.3 2.8 %collective-permute-start.16 = (f32[64,1,128]{2,1,0:T(1,128)S(1)}, f32[64,1,128]{2,1,0:T(1,128)S(1)}, u32[]{:S(2)}, u32[]{:S(2)}) collective-permute-start(f32[64,1,128]{2,1,0:T(1,128)S(1)} %all_to_all.17.m0), channel_id=1, source_target_pairs={{0,192},{64,0},{128,64},{192,128},{1,193},{65,1},{129,65},{193,129... | collective-permute-start | bytes 98312 | tf_op jit(solution)/shard_map/ppermute | solution.py:548
  143.2 4.3 %collective-permute-start.15 = (f32[64,1,128]{2,1,0:T(1,128)S(1)}, f32[64,1,128]{2,1,0:T(1,128)S(1)}, u32[]{:S(2)}, u32[]{:S(2)}) collective-permute-start(f32[64,1,128]{2,1,0:T(1,128)S(1)} %all_to_all.17.m0), channel_id=1, source_target_pairs={{0,128},{64,192},{128,0},{192,64},{1,129},{65,193},{129,1},{193,65... | collective-permute-start | bytes 98312 | tf_op jit(solution)/shard_map/ppermute | solution.py:548
  144.4 4.0 %collective-permute-start.14 = (f32[64,1,128]{2,1,0:T(1,128)S(1)}, f32[64,1,128]{2,1,0:T(1,128)S(1)}, u32[]{:S(2)}, u32[]{:S(2)}) collective-permute-start(f32[64,1,128]{2,1,0:T(1,128)S(1)} %all_to_all.17.m0), channel_id=1, source_target_pairs={{0,64},{64,128},{128,192},{192,0},{1,65},{65,129},{129,193},{193,1... | collective-permute-start | bytes 98312 | tf_op jit(solution)/shard_map/ppermute | solution.py:548

commit v4 on v3

--- a/solution.py
+++ b/solution.py
@@ -316,29 +316,32 @@
         packed[i] = tile
 
 
-def unpack(dst, row, lo, own, hi):
+def unpack(dst, row, lo, own, hi, scales):
     group = lax.broadcasted_iota(jnp.int32, (8, 128), 1) // 32
-    for part, src in enumerate((lo, own, hi)):
+    for part, (src, scale) in enumerate(zip((lo, own, hi), scales)):
         for bx in range(GX):
             for k in range(4):
-                halves = []
                 for h in range(2):
                     acc = None
                     for j in range(4):
-                        block = src[bx * GZ + 4 * h + j, row : row + 8, :]
-                        shift = (32 * (j - k)) % 128
-                        if shift:
-                            block = pltpu.roll(block, shift, 1)
+                        block = turn(src[bx * GZ + 4 * h + j, row : row + 8, :], 32 * (j - k))
                         acc = block if acc is None else jnp.where(group == j, block, acc)
-                    halves.append(acc)
-                dst[1 + 4 * bx + k, 8 * part : 8 * part + 8, :] = jnp.concatenate(halves, axis=1)
-
-
-def coarse(r2, d2, s0, s1, z2, gy):
+                    rows = slice(8 * part, 8 * part + 8)
+                    lanes = slice(128 * h, 128 * h + 128)
+                    dst[6 + 4 * bx + k, rows, lanes] = acc if scale is None else acc * scale
+    for p in (*range(6), *range(22, 28)):
+        dst[p] = jnp.zeros((24, 256), F32)
+
+
+def coarse(r2, d2, s0, s1, z2):
+    gx, gy, _ = places()
     shape = (24, 256)
     row = lax.broadcasted_iota(jnp.int32, shape, 0) + (gy * 8 - 8)
     mask = flag((row >= 0) & (row < 64))
+    low, high = mask * flag(gx > 0), mask * flag(gx < GX - 1)
+    inside = lambda i: low if i < 6 else mask if i < 10 else high
     lane = lax.broadcasted_iota(jnp.int32, shape, 1)
+    at = lambda ref, i: ref[4 * gx + i]
 
     def box(t):
         t = t + pltpu.roll(t, 1, 0) + pltpu.roll(t, 23, 0)
@@ -353,71 +356,53 @@
     rho = 1.0 / sigma
     rho1 = 1.0 / (2.0 * sigma - rho)
     rho2 = 1.0 / (2.0 * sigma - rho1)
-    zero = jnp.zeros(shape, F32)
-    for ref in (r2, s0, s1, z2):
-        ref[0] = zero
-        ref[17] = zero
-
-    def scale(p):
-        r2[p] = r2[p] * mask
-
-    loop(1, 17, scale)
-
-    def one(p):
-        r = r2[p]
+
+    for i in range(2, 14):
+        r = at(r2, i)
         step = r * (1.0 / theta)
-        remain = mask * (r - d2[p] * step + box(r2[p - 1] + r + r2[p + 1]) * (1.0 / theta))
-        s0[p] = remain
-        s1[p] = (rho1 * rho) * step + (2.0 * rho1 / delta) * remain
-
-    loop(1, 17, one)
-
-    def two(p):
-        step = s1[p]
-        remain = mask * (s0[p] - d2[p] * step + box(s1[p - 1] + step + s1[p + 1]))
+        total = box(at(r2, i - 1) + r + at(r2, i + 1)) * (1.0 / theta)
+        remain = inside(i) * (r - at(d2, i) * step + total)
+        s0[i] = remain
+        s1[i] = (rho1 * rho) * step + (2.0 * rho1 / delta) * remain
+    for i in range(3, 13):
+        step = s1[i]
+        remain = inside(i) * (s0[i] - at(d2, i) * step + box(s1[i - 1] + step + s1[i + 1]))
         last = (rho2 * rho1) * step + (2.0 * rho2 / delta) * remain
-        z2[p] = r2[p] * (1.0 / theta) + step + last
-
-    loop(1, 17, two)
-
-    def three(p):
-        y = z2[p]
-        left = r2[p] - d2[p] * y + box(z2[p - 1] + y + z2[p + 1])
+        z2[i] = at(r2, i) * (1.0 / theta) + step + last
+    for i in range(4, 12):
+        y, d = z2[i], at(d2, i)
+        left = at(r2, i) - d * y + box(z2[i - 1] + y + z2[i + 1])
         top = jnp.sum(left, axis=1, keepdims=True)
-        low = jnp.sum(d2[p] - 26.0, axis=1, keepdims=True)
-        s0[p] = mask * (y + top / low)
-
-    loop(1, 17, three)
+        bottom = jnp.sum(d - 26.0, axis=1, keepdims=True)
+        s0[i] = inside(i) * (y + top / bottom)
 
 
 def post_kernel(first, *refs):
+    lo, own, hi, zs, rs, z1, left1, d0, d1 = refs[:9]
     if first:
-        (lo, own, hi, zs, rs, z1, left1, d0, d1,
-         d2, z_core, q_core, q_down, q_up, q_halo,
-         r2, s0, s1, z2, wide, rows1, u, rem, zf1, rowsv, v, sv, rem0, zf0) = refs
+        d2, z_core, q_core, q_down, q_up, q_halo = refs[9:15]
     else:
-        (lo, own, hi, zs, rs, z1, left1, d0, d1, d2,
-         z_core, q_core,
-         r2, s0, s1, z2, wide, rows1, u, rem, zf1, rowsv, v, sv, rem0, zf0) = refs
+        d2, r_old, z_old, q_old, z_core, q_core, dots = refs[9:16]
+    r2, s0, s1, z2, wide, rows1, u, rem, zf1, rowsv, v, sv, rem0, zf0 = refs[-14:]
     gx, gy, gz = places()
-    unpack(r2, 0, lo, own, hi)
+    scales = (flag(gy > 0), None, flag(gy < GY - 1))
+    unpack(r2, 0, lo, own, hi, scales)
     if first:
-        unpack(d2, 8, lo, own, hi)
-    coarse(r2, d2, s0, s1, z2, gy)
+        unpack(d2, 8, lo, own, hi, (None, None, None))
+    coarse(r2, d2, s0, s1, z2)
 
     lane = lax.broadcasted_iota(jnp.int32, (16, 128), 1)
     z = jnp.where(lane < 48, lane, lane - 64) + 32 * gz
     in2 = flag((z >= 0) & (z < 256) & (lane < 64))
     turned = (256 - 32 * gz) % 256
-    for i in range(10):
-        p = 4 * gx - 3 + i
-        plane = pltpu.roll(s0[jnp.clip(p + 1, 0, 17)], turned, 1)[5:21]
+    for i in range(8):
+        plane = pltpu.roll(s0[i + 4], turned, 1)[5:21]
         plane = jnp.where(lane < 48, plane[:, :128], turn(plane[:, 128:], 64))
-        wide[16 * i : 16 * i + 16, :] = plane * (in2 * flag((p >= 0) & (p < 16)))
+        wide[16 * i : 16 * i + 16, :] = plane * in2
     up = dot(wide[...], doubling(128, 128))
-    rows1[pl.ds(0, 160, stride=2), :] = up
-    rows1[pl.ds(1, 160, stride=2), :] = up
-    u[...] = rows1[...].reshape(10, 32, 128)
+    rows1[pl.ds(0, 128, stride=2), :] = up
+    rows1[pl.ds(1, 128, stride=2), :] = up
+    u[1:9] = rows1[...].reshape(8, 32, 128)
 
     mask1 = plane_mask(1, (MY, MZ), -HY // 2)
     keep1, mask1 = x_masks(mask1, 1), x_masks(mask1, 1, CA)
@@ -463,13 +448,18 @@
     loop(1, 19, final)
 
     group = lax.broadcasted_iota(jnp.int32, (BY, BZ), 1) // 32
+    acc = [None] * 9
 
     def apply(i):
         c = zf0[i + 2]
         q = d0[i + HX, 8:48, :] * c - spread(zf0[i + 1] + c + zf0[i + 3])
-        q_own = q[4:36, :BZ]
-        z_core[i] = c[4:36, :BZ]
+        q_own, z_own = q[4:36, :BZ], c[4:36, :BZ]
+        z_core[i] = z_own
         q_core[i] = q_own
+        if not first:
+            for k, term in enumerate(products(r_old[i], z_old[i], q_old[i], z_own, q_own)):
+                term = term[:8] + term[8:16] + (term[16:24] + term[24:])
+                acc[k] = term if i == 0 else acc[k] + term
         if first:
             if i < 12:
                 q_down[i] = q_own
@@ -486,29 +476,24 @@
                 q_up[11 + g] = halo
 
     loop(0, BX, apply)
-
-
-def dots_kernel(r, z, q, p, w, dots):
-    acc = [None] * 9
-    for i in range(BX):
-        ri, zi, qi, pi, wi = r[i], z[i], q[i], p[i], w[i]
-        r1, z1, w1 = ri - qi, zi - pi, qi - wi
-        terms = (
-            ri * zi, zi * qi, r1 * z1, r1 * pi + qi * z1, qi * pi,
-            z1 * w1, z1 * wi + pi * w1, pi * wi, z1 * qi,
-        )
-        for k, term in enumerate(terms):
-            acc[k] = term if i == 0 else acc[k] + term
-    lane = lax.broadcasted_iota(jnp.int32, (1, 128), 1)
-    row = jnp.zeros((1, 128), F32)
-    for k, part in enumerate(acc):
-        total = jnp.sum(jnp.sum(part, axis=0, keepdims=True), axis=1, keepdims=True)
-        row = jnp.where(lane == k, total, row)
-    dots[...] = jnp.broadcast_to(row[None], (GY * GZ, 1, 128))
-
-
-def end_kernel(r, z, q, p, w, m0, m1, m2, m3, solution_field, residual):
-    last = jnp.sum(m0[...] + m1[...] + m2[...] + m3[...], axis=0)
+    if not first:
+        lane = lax.broadcasted_iota(jnp.int32, (1, 128), 1)
+        row = jnp.zeros((1, 128), F32)
+        for k, part in enumerate(acc):
+            total = jnp.sum(jnp.sum(part, axis=0, keepdims=True), axis=1, keepdims=True)
+            row = jnp.where(lane == k, total, row)
+        dots[...] = jnp.broadcast_to(row[None], dots.shape)
+
+
+def products(r, z, q, p, w):
+    r1, z1, w1 = r - q, z - p, q - w
+    return (
+        r * z, z * q, r1 * z1, r1 * p + q * z1, q * p, z1 * w1, z1 * w + p * w1, p * w, z1 * q,
+    )
+
+
+def end_kernel(r, z, q, p, w, sums, solution_field, residual):
+    last = jnp.sum(sums[...], axis=0)
     lane = lax.broadcasted_iota(jnp.int32, (1, 128), 1)
     at = lambda i: jnp.sum(jnp.where(lane == i, last, 0.0), axis=1, keepdims=True)
     rz, curve = at(0), at(1)
@@ -563,19 +548,20 @@
     return call(kernel, kept, scratch, *args)
 
 
-def post_call(parts, kept, d0, d1, d2=None):
-    first = d2 is None
-    scratch = [(18, 24, 256)] * 4 + [
-        (160, 128), (320, 128), (10, 32, 128), (MX, MY, MZ), (240, 128),
+def post_call(parts, kept, d0, d1, *old):
+    first = not old
+    scratch = [(28, 24, 256)] + [(16, 24, 256)] * 3 + [
+        (128, 128), (256, 128), (10, 32, 128), (MX, MY, MZ), (240, 128),
         (480, 128), (12, PY, EZ), (12, PY, EZ), (20, PY, EZ), (20, PY, EZ),
     ]
     core = shape(BX, BY, BZ)
     kernel = functools.partial(post_kernel, first)
     if first:
         slab = shape(15, BY, BZ)
-        outs = (shape(18, 24, 256), core, core, slab, slab, shape(4, BY, BZ))
+        outs = (shape(28, 24, 256), core, core, slab, slab, shape(4, BY, BZ))
         return call(kernel, outs, scratch, *parts, *kept, d0, d1)
-    return call(kernel, (core, core), scratch, *parts, *kept, d0, d1, d2)
+    outs = (core, core, shape(GX * GY * GZ, 1, 128))
+    return call(kernel, outs, scratch, *parts, *kept, d0, d1, *old)
 
 
 def first_exchange(right_side, diagonal):
@@ -606,13 +592,12 @@
     d0, d1, *kept = pre_call(True, *first_exchange(right_side, diagonal))
     d2, z, q, *edges = post_call(spread_coarse(kept[-1]), kept[:-1], d0, d1)
     kept = pre_call(False, *later_exchange(q, *edges), d0, d1)
-    p, w = post_call(spread_coarse(kept[-1]), kept[:-1], d0, d1, d2=d2)
-    fields = (right_side, z, q, p, w)
-    more = call(dots_kernel, shape(GY * GZ, 1, 128), [], *fields)
-    more = lax.all_to_all(more, ("gy", "gz"), 0, 0)
-    others = [shift(more, "gx", GX, i) for i in (1, 2, 3)]
+    p, w, dots = post_call(
+        spread_coarse(kept[-1]), kept[:-1], d0, d1, d2, right_side, z, q
+    )
+    sums = lax.all_to_all(dots, ("gx", "gy", "gz"), 0, 0)
     core = shape(BX, BY, BZ)
-    return call(end_kernel, (core, core), [], *fields, more, *others)
+    return call(end_kernel, (core, core), [], right_side, z, q, p, w, sums)
 
 
 def solution(mesh):

time: 150 us -> 147 us (0.980)
  blocking collectives: 51.4 us -> 56.7 us
  waiting for transfers between devices: 42 us -> 38 us
  starting transfers between devices: 30.7 us -> 28.5 us
  Pallas kernels: 23.4 us -> 21.5 us
    all_to_all x1, blocking collectives: 17.3 us -> 22.6 us  [local(): sums = lax.all_to_all(dots, ('gx', 'gy', 'gz'), 0, 0)]
    ppermute x17 -> x14, waiting for transfers between devices: 42 us -> 38 us  [shift(): lax.ppermute(value, axis, [(i, (i + by) % count) for i in range(count)])]
    ppermute x17 -> x14, starting transfers between devices: 30.7 us -> 28.5 us  [shift(): lax.ppermute(value, axis, [(i, (i + by) % count) for i in range(count)])]
    pallas_call x9 -> x8, Pallas kernels: 23.4 us -> 21.5 us  [call(): pl.pallas_call(kernel, out_shape=outs, in_specs=[whole] * len(args), out_...]
  transfers between devices with their start and end apart: 17 -> 14, of which waited for: 14 -> 11; matrix products, arithmetic and copies ran while one was open for 0% -> 0% of each run, Pallas kernels for 0% -> 0%
where the time goes in v4:
time: 147 us
  blocking collectives  56.7 us (39%)
  waiting for transfers between devices  38 us (26%)
  starting transfers between devices  28.5 us (19%)
  Pallas kernels  21.5 us (15%)
    ppermute x14, waiting for transfers between devices, shift(): lax.ppermute(value, axis, [(i, (i + by) % count) for i in range(count)])  38 us
    all_to_all x2, blocking collectives, spread_coarse(): own = lax.all_to_all(packed, ('gx', 'gz'), 0, 0)  34 us
    ppermute x14, starting transfers between devices, shift(): lax.ppermute(value, axis, [(i, (i + by) % count) for i in range(count)])  28.5 us
    all_to_all x1, blocking collectives, local(): sums = lax.all_to_all(dots, ('gx', 'gy', 'gz'), 0, 0)  22.6 us
    pallas_call x8, Pallas kernels, call(): pl.pallas_call(kernel, out_shape=outs, in_specs=[whole] * len(args), out_...  21.5 us
  transfers between devices with their start and end apart: 14, of which 11 were waited for; matrix products, arithmetic and copies ran while one was open for 0% of the time, Pallas kernels for 0%

profile of v4, /device:TPU:1, one launch (start us, length us, event | category | flops | bytes accessed | tf_op | source)
XLA Modules:
  0.0 146.8 jit_solution(2025017313968087043)
XLA Ops:
  0.6 0.0 copy-start
  0.6 0.0 copy-start.1
  0.6 1.3 slice_bitcast_fusion
  2.0 2.1 %collective-permute-start = (f32[2,12,32,128]{3,2,1,0:T(8,128)S(1)}, f32[2,12,32,128]{3,2,1,0:T(8,128)S(1)}, u32[]{:S(2)}, u32[]{:S(2)}) collective-permute-start(f32[2,12,32,128]{3,2,1,0:T(8,128)S(1)} %pad_maximum_fusion), channel_id=1, source_target_pairs={{0,64},{64,128},{128,192},{192,0},{1,65},{65,129},{129,193},{193,1... | collective-permute-start | bytes 1179656 | tf_op jit(solution)/shard_map/ppermute | solution.py:533
  4.2 1.4 collective-permute-start.1
  5.5 6.4 %collective-permute-done.xlo.refs_2_ = f32[2,12,32,128]{3,2,1,0:T(8,128)S(1)} collective-permute-done((f32[2,12,32,128]{3,2,1,0:T(8,128)S(1)}, f32[2,12,32,128]{3,2,1,0:T(8,128)S(1)}, u32[]{:S(2)}, u32[]{:S(2)}) %collective-permute-start) | collective-permute-done | bytes 393248 | tf_op jit(solution)/shard_map/ppermute | solution.py:533
  11.9 1.7 %collective-permute-done.1.xhi.refs_3_ = f32[2,12,32,128]{3,2,1,0:T(8,128)S(1)} collective-permute-done((f32[2,12,32,128]{3,2,1,0:T(8,128)S(1)}, f32[2,12,32,128]{3,2,1,0:T(8,128)S(1)}, u32[]{:S(2)}, u32[]{:S(2)}) %collective-permute-start.1) | collective-permute-done | bytes 393248 | tf_op jit(solution)/shard_map/ppermute | solution.py:533
  13.6 0.0 copy-done
  13.6 0.0 copy-done.1
  13.6 0.7 shard_map.41
  14.3 2.2 %collective-permute-start.2 = (f32[2,8,32,128]{3,2,1,0:T(8,128)S(1)}, f32[2,8,32,128]{3,2,1,0:T(8,128)S(1)}, u32[]{:S(2)}, u32[]{:S(2)}) collective-permute-start(f32[2,8,32,128]{3,2,1,0:T(8,128)S(1)} %get-tuple-element.29), channel_id=1, source_target_pairs={{0,1},{1,2},{2,3},{3,4},{4,5},{5,6},{6,7},{7,0},{8,9},{9,10},{10,1... | collective-permute-start | bytes 786440 | tf_op jit(solution)/shard_map/ppermute | solution.py:533
  16.5 4.0 %collective-permute-start.3 = (f32[2,8,32,128]{3,2,1,0:T(8,128)S(1)}, f32[2,8,32,128]{3,2,1,0:T(8,128)S(1)}, u32[]{:S(2)}, u32[]{:S(2)}) collective-permute-start(f32[2,8,32,128]{3,2,1,0:T(8,128)S(1)} %get-tuple-element.30), channel_id=1, source_target_pairs={{0,7},{1,0},{2,1},{3,2},{4,3},{5,4},{6,5},{7,6},{8,15},{9,8},{10,9... | collective-permute-start | bytes 786440 | tf_op jit(solution)/shard_map/ppermute | solution.py:533
  20.5 4.9 %collective-permute-done.2.zl.refs_4_ = f32[2,8,32,128]{3,2,1,0:T(8,128)S(1)} collective-permute-done((f32[2,8,32,128]{3,2,1,0:T(8,128)S(1)}, f32[2,8,32,128]{3,2,1,0:T(8,128)S(1)}, u32[]{:S(2)}, u32[]{:S(2)}) %collective-permute-start.2) | collective-permute-done | bytes 262176 | tf_op jit(solution)/shard_map/ppermute | solution.py:533
  25.4 0.0 collective-permute-done.3.zr.refs_5_
  25.4 0.1 shard_map.42
  25.5 3.5 %collective-permute-start.4 = (f32[168,8,128]{2,1,0:T(8,128)S(1)}, f32[168,8,128]{2,1,0:T(8,128)S(1)}, u32[]{:S(2)}, u32[]{:S(2)}) collective-permute-start(f32[168,8,128]{2,1,0:T(8,128)S(1)} %get-tuple-element.31), channel_id=1, source_target_pairs={{0,8},{8,16},{16,24},{24,32},{32,40},{40,48},{48,56},{56,0},{1,9},... | collective-permute-start | bytes 2064392 | tf_op jit(solution)/shard_map/ppermute | solution.py:533
  29.0 0.0 collective-permute-start.5
  29.0 7.9 %collective-permute-done.4.refs_6_ = f32[168,8,128]{2,1,0:T(8,128)S(1)} collective-permute-done((f32[168,8,128]{2,1,0:T(8,128)S(1)}, f32[168,8,128]{2,1,0:T(8,128)S(1)}, u32[]{:S(2)}, u32[]{:S(2)}) %collective-permute-start.4) | collective-permute-done | bytes 688160 | tf_op jit(solution)/shard_map/ppermute | solution.py:533
  36.9 2.5 %collective-permute-done.5.refs_7_ = f32[168,8,128]{2,1,0:T(8,128)S(1)} collective-permute-done((f32[168,8,128]{2,1,0:T(8,128)S(1)}, f32[168,8,128]{2,1,0:T(8,128)S(1)}, u32[]{:S(2)}, u32[]{:S(2)}) %collective-permute-start.5) | collective-permute-done | bytes 688160 | tf_op jit(solution)/shard_map/ppermute | solution.py:533
  39.4 5.4 %shard_map.43 = (f32[40,56,256]{2,1,0:T(8,128)S(1)}, f32[20,32,128]{2,1,0:T(8,128)S(1)}, f32[20,40,256]{2,1,0:T(8,128)S(1)}, f32[20,40,256]{2,1,0:T(8,128)S(1)},...) custom-call(f32[16,32,128]{2,1,0:T(8,128)S(1)} %copy-done, ...), custom_call_target="tpu_custom_call" | custom-call | tf_op jit(solution)/shard_map/pallas_call | solution.py:522
  44.8 18.2 %all_to_all.15.refs_1_ = f32[32,16,128]{2,1,0:T(8,128)S(1)} all-to-all(f32[32,16,128]{2,1,0:T(8,128)S(1)} %get-tuple-element.33), channel_id=1, replica_groups=mesh['gx'=4,'gy'=8,'gz'=8] {'gx','gz'}, dimensions={0} | all-to-all | bytes 524288 | tf_op jit(solution)/shard_map/all_to_all | solution.py:537
  63.0 2.4 %collective-permute-start.7 = (f32[32,16,128]{2,1,0:T(8,128)S(1)}, f32[32,16,128]{2,1,0:T(8,128)S(1)}, u32[]{:S(2)}, u32[]{:S(2)}) collective-permute-start(f32[32,16,128]{2,1,0:T(8,128)S(1)} %all_to_all.15.refs_1_), channel_id=1, source_target_pairs={{0,56},{8,0},{16,8},{24,16},{32,24},{40,32},{48,40},{56,48},{1,57}... | collective-permute-start | bytes 786440 | tf_op jit(solution)/shard_map/ppermute | solution.py:533
  65.4 0.0 collective-permute-start.6
  65.4 3.4 %collective-permute-done.7.refs_2_ = f32[32,16,128]{2,1,0:T(8,128)S(1)} collective-permute-done((f32[32,16,128]{2,1,0:T(8,128)S(1)}, f32[32,16,128]{2,1,0:T(8,128)S(1)}, u32[]{:S(2)}, u32[]{:S(2)}) %collective-permute-start.7) | collective-permute-done | bytes 262176 | tf_op jit(solution)/shard_map/ppermute | solution.py:533
  68.8 0.0 collective-permute-done.6.refs_0_
  68.8 5.3 %shard_map.44 = (f32[28,24,256]{2,1,0:T(8,128)S(1)}, f32[16,32,128]{2,1,0:T(8,128)S(1)}, f32[16,32,128]{2,1,0:T(8,128)S(1)}, f32[15,32,128]{2,1,0:T(8,128)S(1)},...) custom-call(f32[32,16,128]{2,1,0:T(8,128)S(1)} %collective-permute-done.6.refs_0_, ...), custom_call_target="tpu_custom_call" | custom-call | tf_op jit(solution)/shard_map/pallas_call | solution.py:522
  74.1 0.8 collective-permute-start.8
  74.9 2.0 %collective-permute-start.9 = (f32[15,32,128]{2,1,0:T(8,128)S(1)}, f32[15,32,128]{2,1,0:T(8,128)S(1)}, u32[]{:S(2)}, u32[]{:S(2)}) collective-permute-start(f32[15,32,128]{2,1,0:T(8,128)S(1)} %get-tuple-element.44), channel_id=1, source_target_pairs={{0,192},{64,0},{128,64},{192,128},{1,193},{65,1},{129,65},{193,129... | collective-permute-start | bytes 737288 | tf_op jit(solution)/shard_map/ppermute | solution.py:533
  76.8 3.6 %collective-permute-done.8.xlo.refs_2_ = f32[15,32,128]{2,1,0:T(8,128)S(1)} collective-permute-done((f32[15,32,128]{2,1,0:T(8,128)S(1)}, f32[15,32,128]{2,1,0:T(8,128)S(1)}, u32[]{:S(2)}, u32[]{:S(2)}) %collective-permute-start.8) | collective-permute-done | bytes 245792 | tf_op jit(solution)/shard_map/ppermute | solution.py:533
  80.4 0.0 collective-permute-done.9.xhi.refs_3_
  80.4 0.1 shard_map.45
  80.5 5.5 %collective-permute-start.10 = (f32[75,8,128]{2,1,0:T(8,128)S(1)}, f32[75,8,128]{2,1,0:T(8,128)S(1)}, u32[]{:S(2)}, u32[]{:S(2)}) collective-permute-start(f32[75,8,128]{2,1,0:T(8,128)S(1)} %get-tuple-element.45), channel_id=1, source_target_pairs={{0,8},{8,16},{16,24},{24,32},{32,40},{40,48},{48,56},{56,0},{1,9},... | collective-permute-start | bytes 921608 | tf_op jit(solution)/shard_map/ppermute | solution.py:533
  86.0 1.1 collective-permute-start.11
  87.0 2.7 %collective-permute-done.10.refs_4_ = f32[75,8,128]{2,1,0:T(8,128)S(1)} collective-permute-done((f32[75,8,128]{2,1,0:T(8,128)S(1)}, f32[75,8,128]{2,1,0:T(8,128)S(1)}, u32[]{:S(2)}, u32[]{:S(2)}) %collective-permute-start.10) | collective-permute-done | bytes 307232 | tf_op jit(solution)/shard_map/ppermute | solution.py:533
  89.8 2.8 %collective-permute-done.11.refs_5_ = f32[75,8,128]{2,1,0:T(8,128)S(1)} collective-permute-done((f32[75,8,128]{2,1,0:T(8,128)S(1)}, f32[75,8,128]{2,1,0:T(8,128)S(1)}, u32[]{:S(2)}, u32[]{:S(2)}) %collective-permute-start.11) | collective-permute-done | bytes 307232 | tf_op jit(solution)/shard_map/ppermute | solution.py:533
  92.5 4.2 %shard_map.46 = (f32[20,40,256]{2,1,0:T(8,128)S(1)}, f32[20,40,256]{2,1,0:T(8,128)S(1)}, f32[20,32,128]{2,1,0:T(8,128)S(1)}, f32[20,32,128]{2,1,0:T(8,128)S(1)}, f32[32,8,128]{2,1,0:T(8,128)S(1)}) custom-call(f32[16,32,128]{2,1,0:T(8,128)S(1)} %get-tuple-element.41.own.refs_0_.refs_12_.q, f32[4,32,128]{2,1,0:T(8,128)S(1)} %get-tuple-element.42.halo.refs_1_, ...), custom_call_target="tpu_custom_call" | custom-call | tf_op jit(solution)/shard_map/pallas_call | solution.py:522
  96.7 15.8 %all_to_all.16.refs_1_ = f32[32,8,128]{2,1,0:T(8,128)S(1)} all-to-all(f32[32,8,128]{2,1,0:T(8,128)S(1)} %get-tuple-element.47), channel_id=1, replica_groups=mesh['gx'=4,'gy'=8,'gz'=8] {'gx','gz'}, dimensions={0} | all-to-all | bytes 262144 | tf_op jit(solution)/shard_map/all_to_all | solution.py:537
  112.5 3.6 %collective-permute-start.13 = (f32[32,8,128]{2,1,0:T(8,128)S(1)}, f32[32,8,128]{2,1,0:T(8,128)S(1)}, u32[]{:S(2)}, u32[]{:S(2)}) collective-permute-start(f32[32,8,128]{2,1,0:T(8,128)S(1)} %all_to_all.16.refs_1_), channel_id=1, source_target_pairs={{0,56},{8,0},{16,8},{24,16},{32,24},{40,32},{48,40},{56,48},{1,57}... | collective-permute-start | bytes 393224 | tf_op jit(solution)/shard_map/ppermute | solution.py:533
  116.1 0.0 collective-permute-start.12
  116.1 1.0 collective-permute-done.13.refs_2_
  117.1 1.2 collective-permute-done.12.refs_0_
  118.4 4.5 %shard_map.47 = (f32[16,32,128]{2,1,0:T(8,128)S(1)}, f32[16,32,128]{2,1,0:T(8,128)S(1)}, f32[256,1,128]{2,1,0:T(1,128)S(1)}) custom-call(f32[32,8,128]{2,1,0:T(8,128)S(1)} %collective-permute-done.12.refs_0_, f32[32,8,128]{2,1,0:T(8,128)S(1)} %all_to_all.16.refs_1_, f32[32,8,128]{2,1,0:T(8,128)S(1)} %collective-permute-done.13.refs_2_, ...), custom_call_target="tpu_custom_call" | custom-call | tf_op jit(solution)/shard_map/pallas_call | solution.py:522
  122.9 22.6 %all_to_all.17.sums = f32[256,1,128]{2,1,0:T(1,128)S(1)} all-to-all(f32[256,1,128]{2,1,0:T(1,128)S(1)} %get-tuple-element.55), channel_id=1, replica_groups=mesh['gx'=4,'gy'=8,'gz'=8] {'gx','gy','gz'}, dimensions={0} | all-to-all | bytes 262144 | tf_op jit(solution)/shard_map/all_to_all | solution.py:598
  145.5 1.3 shard_map.48
  (2 shorter events, 0.1 us)
Async XLA Ops:
  0.6 13.0 %copy-start = (f32[16,32,128]{2,1,0:T(8,128)S(1)}, f32[16,32,128]{2,1,0:T(8,128)}, u32[]{:S(2)}) copy-start(f32[16,32,128]{2,1,0:T(8,128)} %r.1) | copy-start | bytes 786436
  0.6 13.0 %copy-start.1 = (f32[16,32,128]{2,1,0:T(8,128)S(1)}, f32[16,32,128]{2,1,0:T(8,128)}, u32[]{:S(2)}) copy-start(f32[16,32,128]{2,1,0:T(8,128)} %refs_1_.1) | copy-start | bytes 786436
  2.0 9.9 %collective-permute-start = (f32[2,12,32,128]{3,2,1,0:T(8,128)S(1)}, f32[2,12,32,128]{3,2,1,0:T(8,128)S(1)}, u32[]{:S(2)}, u32[]{:S(2)}) collective-permute-start(f32[2,12,32,128]{3,2,1,0:T(8,128)S(1)} %pad_maximum_fusion), channel_id=1, source_target_pairs={{0,64},{64,128},{128,192},{192,0},{1,65},{65,129},{129,193},{193,1... | collective-permute-start | bytes 1179656 | tf_op jit(solution)/shard_map/ppermute | solution.py:533
  4.2 9.5 %collective-permute-start.1 = (f32[2,12,32,128]{3,2,1,0:T(8,128)S(1)}, f32[2,12,32,128]{3,2,1,0:T(8,128)S(1)}, u32[]{:S(2)}, u32[]{:S(2)}) collective-permute-start(f32[2,12,32,128]{3,2,1,0:T(8,128)S(1)} %pad_maximum_fusion.1), channel_id=1, source_target_pairs={{0,192},{64,0},{128,64},{192,128},{1,193},{65,1},{129,65},{193,129... | collective-permute-start | bytes 1179656 | tf_op jit(solution)/shard_map/ppermute | solution.py:533
  14.3 11.1 %collective-permute-start.2 = (f32[2,8,32,128]{3,2,1,0:T(8,128)S(1)}, f32[2,8,32,128]{3,2,1,0:T(8,128)S(1)}, u32[]{:S(2)}, u32[]{:S(2)}) collective-permute-start(f32[2,8,32,128]{3,2,1,0:T(8,128)S(1)} %get-tuple-element.29), channel_id=1, source_target_pairs={{0,1},{1,2},{2,3},{3,4},{4,5},{5,6},{6,7},{7,0},{8,9},{9,10},{10,1... | collective-permute-start | bytes 786440 | tf_op jit(solution)/shard_map/ppermute | solution.py:533
  16.5 8.9 %collective-permute-start.3 = (f32[2,8,32,128]{3,2,1,0:T(8,128)S(1)}, f32[2,8,32,128]{3,2,1,0:T(8,128)S(1)}, u32[]{:S(2)}, u32[]{:S(2)}) collective-permute-start(f32[2,8,32,128]{3,2,1,0:T(8,128)S(1)} %get-tuple-element.30), channel_id=1, source_target_pairs={{0,7},{1,0},{2,1},{3,2},{4,3},{5,4},{6,5},{7,6},{8,15},{9,8},{10,9... | collective-permute-start | bytes 786440 | tf_op jit(solution)/shard_map/ppermute | solution.py:533
  25.5 11.4 %collective-permute-start.4 = (f32[168,8,128]{2,1,0:T(8,128)S(1)}, f32[168,8,128]{2,1,0:T(8,128)S(1)}, u32[]{:S(2)}, u32[]{:S(2)}) collective-permute-start(f32[168,8,128]{2,1,0:T(8,128)S(1)} %get-tuple-element.31), channel_id=1, source_target_pairs={{0,8},{8,16},{16,24},{24,32},{32,40},{40,48},{48,56},{56,0},{1,9},... | collective-permute-start | bytes 2064392 | tf_op jit(solution)/shard_map/ppermute | solution.py:533
  29.0 10.4 %collective-permute-start.5 = (f32[168,8,128]{2,1,0:T(8,128)S(1)}, f32[168,8,128]{2,1,0:T(8,128)S(1)}, u32[]{:S(2)}, u32[]{:S(2)}) collective-permute-start(f32[168,8,128]{2,1,0:T(8,128)S(1)} %get-tuple-element.32), channel_id=1, source_target_pairs={{0,56},{8,0},{16,8},{24,16},{32,24},{40,32},{48,40},{56,48},{1,57}... | collective-permute-start | bytes 2064392 | tf_op jit(solution)/shard_map/ppermute | solution.py:533
  63.0 5.8 %collective-permute-start.7 = (f32[32,16,128]{2,1,0:T(8,128)S(1)}, f32[32,16,128]{2,1,0:T(8,128)S(1)}, u32[]{:S(2)}, u32[]{:S(2)}) collective-permute-start(f32[32,16,128]{2,1,0:T(8,128)S(1)} %all_to_all.15.refs_1_), channel_id=1, source_target_pairs={{0,56},{8,0},{16,8},{24,16},{32,24},{40,32},{48,40},{56,48},{1,57}... | collective-permute-start | bytes 786440 | tf_op jit(solution)/shard_map/ppermute | solution.py:533
  65.4 3.4 %collective-permute-start.6 = (f32[32,16,128]{2,1,0:T(8,128)S(1)}, f32[32,16,128]{2,1,0:T(8,128)S(1)}, u32[]{:S(2)}, u32[]{:S(2)}) collective-permute-start(f32[32,16,128]{2,1,0:T(8,128)S(1)} %all_to_all.15.refs_1_), channel_id=1, source_target_pairs={{0,8},{8,16},{16,24},{24,32},{32,40},{40,48},{48,56},{56,0},{1,9},... | collective-permute-start | bytes 786440 | tf_op jit(solution)/shard_map/ppermute | solution.py:533
  74.1 6.3 %collective-permute-start.8 = (f32[15,32,128]{2,1,0:T(8,128)S(1)}, f32[15,32,128]{2,1,0:T(8,128)S(1)}, u32[]{:S(2)}, u32[]{:S(2)}) collective-permute-start(f32[15,32,128]{2,1,0:T(8,128)S(1)} %get-tuple-element.43), channel_id=1, source_target_pairs={{0,64},{64,128},{128,192},{192,0},{1,65},{65,129},{129,193},{193,1... | collective-permute-start | bytes 737288 | tf_op jit(solution)/shard_map/ppermute | solution.py:533
  74.9 5.5 %collective-permute-start.9 = (f32[15,32,128]{2,1,0:T(8,128)S(1)}, f32[15,32,128]{2,1,0:T(8,128)S(1)}, u32[]{:S(2)}, u32[]{:S(2)}) collective-permute-start(f32[15,32,128]{2,1,0:T(8,128)S(1)} %get-tuple-element.44), channel_id=1, source_target_pairs={{0,192},{64,0},{128,64},{192,128},{1,193},{65,1},{129,65},{193,129... | collective-permute-start | bytes 737288 | tf_op jit(solution)/shard_map/ppermute | solution.py:533
  80.5 9.3 %collective-permute-start.10 = (f32[75,8,128]{2,1,0:T(8,128)S(1)}, f32[75,8,128]{2,1,0:T(8,128)S(1)}, u32[]{:S(2)}, u32[]{:S(2)}) collective-permute-start(f32[75,8,128]{2,1,0:T(8,128)S(1)} %get-tuple-element.45), channel_id=1, source_target_pairs={{0,8},{8,16},{16,24},{24,32},{32,40},{40,48},{48,56},{56,0},{1,9},... | collective-permute-start | bytes 921608 | tf_op jit(solution)/shard_map/ppermute | solution.py:533
  86.0 6.6 %collective-permute-start.11 = (f32[75,8,128]{2,1,0:T(8,128)S(1)}, f32[75,8,128]{2,1,0:T(8,128)S(1)}, u32[]{:S(2)}, u32[]{:S(2)}) collective-permute-start(f32[75,8,128]{2,1,0:T(8,128)S(1)} %get-tuple-element.46), channel_id=1, source_target_pairs={{0,56},{8,0},{16,8},{24,16},{32,24},{40,32},{48,40},{56,48},{1,57}... | collective-permute-start | bytes 921608 | tf_op jit(solution)/shard_map/ppermute | solution.py:533
  112.5 4.6 %collective-permute-start.13 = (f32[32,8,128]{2,1,0:T(8,128)S(1)}, f32[32,8,128]{2,1,0:T(8,128)S(1)}, u32[]{:S(2)}, u32[]{:S(2)}) collective-permute-start(f32[32,8,128]{2,1,0:T(8,128)S(1)} %all_to_all.16.refs_1_), channel_id=1, source_target_pairs={{0,56},{8,0},{16,8},{24,16},{32,24},{40,32},{48,40},{56,48},{1,57}... | collective-permute-start | bytes 393224 | tf_op jit(solution)/shard_map/ppermute | solution.py:533
  116.1 2.2 %collective-permute-start.12 = (f32[32,8,128]{2,1,0:T(8,128)S(1)}, f32[32,8,128]{2,1,0:T(8,128)S(1)}, u32[]{:S(2)}, u32[]{:S(2)}) collective-permute-start(f32[32,8,128]{2,1,0:T(8,128)S(1)} %all_to_all.16.refs_1_), channel_id=1, source_target_pairs={{0,8},{8,16},{16,24},{24,32},{32,40},{40,48},{48,56},{56,0},{1,9},... | collective-permute-start | bytes 393224 | tf_op jit(solution)/shard_map/ppermute | solution.py:533

commit v5 on v4

--- a/solution.py
+++ b/solution.py
@@ -28,9 +28,16 @@
 CR, CA = cheb_two(7.0)
 
 
+def spread_y(t):
+    return t + pltpu.roll(t, 1, 0) + pltpu.roll(t, t.shape[0] - 1, 0)
+
+
+def spread_z(t):
+    return t + pltpu.roll(t, 1, 1) + pltpu.roll(t, t.shape[1] - 1, 1)
+
+
 def spread(t):
-    t = t + pltpu.roll(t, 1, 0) + pltpu.roll(t, t.shape[0] - 1, 0)
-    return t + pltpu.roll(t, 1, 1) + pltpu.roll(t, t.shape[1] - 1, 1)
+    return spread_z(spread_y(t))
 
 
 def flag(condition):
@@ -114,8 +121,9 @@
         whole = lambda y: pair(y[base + p], y[base + 40 + g], y[base + 48 + g])
         half = lambda y: pair(*(half_tile(y, base + 56, m) for m in (p, 40 + g, 48 + g)))
         center = x_plane(lambda i: own[i], lambda i: xlo[a, i], lambda i: xhi[a, i], p)
-        middle = pair(center, zl[a, g], zr[a, g])
-        return whole(ylo), half(ylo), middle, half(yhi), whole(yhi)
+        if ylo is None:
+            return [((12, 44), None, pair(center, zl[a, g], zr[a, g]))]
+        return list(zip(ROWS, SIDES, (whole(ylo), half(ylo), half(yhi), whole(yhi))))
 
     return parts
 
@@ -130,12 +138,14 @@
         side = x_plane(
             lambda i: halo[i // 4], lambda i: xlo[12 + i // 4], lambda i: xhi[12 + i // 4], p
         )
-        return whole(ylo), half(ylo), pair(center, side), half(yhi), whole(yhi)
+        if ylo is None:
+            return [((12, 44), None, pair(center, side))]
+        return list(zip(ROWS, SIDES, (whole(ylo), half(ylo), half(yhi), whole(yhi))))
 
     return parts
 
 
-ROWS = ((0, 8), (8, 12), (12, 44), (44, 48), (48, 56))
+ROWS, SIDES = ((0, 8), (8, 12), (44, 48), (48, 56)), (0, 0, 1, 1)
 
 
 def assemble_field(dst, parts):
@@ -143,12 +153,11 @@
     lane = lax.broadcasted_iota(jnp.int32, (1, BZ), 1)
     side = jnp.where(lane < 64, flag(gz < GZ - 1), flag(gz > 0))
     x_low, x_high = flag(gx > 0), flag(gx < GX - 1)
-    y_low, y_high = flag(gy > 0), flag(gy < GY - 1)
+    y_sides = flag(gy > 0), flag(gy < GY - 1)
     for p in range(EX):
         x = x_low if p < HX else None if p < HX + BX else x_high
-        for (lo, hi), y, (center, halo) in zip(
-            ROWS, (y_low, y_low, None, y_high, y_high), parts(p)
-        ):
+        for (lo, hi), y, (center, halo) in parts(p):
+            y = None if y is None else y_sides[y]
             scale = x if y is None else y if x is None else x * y
             dst[p, lo:hi, :BZ] = center if scale is None else center * scale
             dst[p, lo:hi, BZ:] = halo * (side if scale is None else side * scale)
@@ -156,7 +165,7 @@
 
 def assemble_diagonal(dst, parts):
     for p in range(EX):
-        for (lo, hi), (center, halo) in zip(ROWS, parts(p)):
+        for (lo, hi), _, (center, halo) in parts(p):
             dst[p, lo:hi, :BZ] = center + 27.0
             dst[p, lo:hi, BZ:] = halo + 27.0
 
@@ -232,16 +241,31 @@
         dst[p, MR:] = jnp.zeros((MY - MR, MZ), F32)
 
 
+def early_kernel(first, *refs):
+    if first:
+        right_side, diagonal, xlo, xhi, zl, zr, field, zfull, d0 = refs
+        assemble_field(field, first_parts(0, right_side, xlo, xhi, zl, zr, None, None))
+        assemble_diagonal(d0, first_parts(1, diagonal, xlo, xhi, zl, zr, None, None))
+    else:
+        own, halo, xlo, xhi, d0, field, zfull = refs
+        assemble_field(field, later_parts(own, halo, xlo, xhi, None, None))
+    mask = x_masks(plane_mask(0, (24, EZ), 16 - HY), 0, CA)
+    for p in range(1, EX - 1):
+        total = field[p - 1, 8:48] + field[p, 8:48] + field[p + 1, 8:48]
+        box = spread_z(spread_y(total)[8:32])
+        zfull[p, 16:40] = (CR + CA * d0[p, 16:40]) * field[p, 16:40] - mask(p) * box
+
+
 def pre_kernel(first, *refs):
     if first:
         right_side, diagonal, xlo, xhi, zl, zr, ylo, yhi = refs[:8]
-        refs = refs[8:]
-        assemble_field(refs[7], first_parts(0, right_side, xlo, xhi, zl, zr, ylo, yhi))
+        field, zfull, d0, d1, zs, rs, z1, left1, packed, pairs, rows, r1, small = refs[11:]
+        assemble_field(field, first_parts(0, right_side, xlo, xhi, zl, zr, ylo, yhi))
     else:
         own, halo, xlo, xhi, ylo, yhi = refs[:6]
-        refs = refs[6:]
-        assemble_field(refs[7], later_parts(own, halo, xlo, xhi, ylo, yhi))
-    d0, d1, zs, rs, z1, left1, packed, field, zfull, pairs, rows, r1, small = refs
+        d0, d1 = refs[8:10]
+        field, zfull, zs, rs, z1, left1, packed, pairs, rows, r1, small = refs[10:]
+        assemble_field(field, later_parts(own, halo, xlo, xhi, ylo, yhi))
     z_map = halving(EZ, MZ)
     if first:
         assemble_diagonal(d0, first_parts(1, diagonal, xlo, xhi, zl, zr, ylo, yhi))
@@ -250,15 +274,18 @@
         halve(pairs, rows, z_map, d1, 0.125)
     pairs[0:EY, :] = jnp.zeros((EY, EZ), F32)
     pairs[(MX - 1) * EY :, :] = jnp.zeros((EY, EZ), F32)
-    mask = x_masks(plane_mask(0, (EY, EZ), -HY), 0, CA)
+    low = x_masks(plane_mask(0, (16, EZ), -HY), 0, CA)
+    high = x_masks(plane_mask(0, (16, EZ), 40 - HY), 0, CA)
 
     def smooth(p):
-        r = field[p]
-        box = spread(field[p - 1] + r + field[p + 1])
-        z = (CR + CA * d0[p]) * r - mask(p) * box
-        zfull[p] = z
+        total = field[p - 1, 0:24] + field[p, 0:24] + field[p + 1, 0:24]
+        box = spread_z(spread_y(total)[0:16])
+        zfull[p, 0:16] = (CR + CA * d0[p, 0:16]) * field[p, 0:16] - low(p) * box
+        total = field[p - 1, 32:56] + field[p, 32:56] + field[p + 1, 32:56]
+        box = spread_z(spread_y(total)[8:24])
+        zfull[p, 40:56] = (CR + CA * d0[p, 40:56]) * field[p, 40:56] - high(p) * box
         if 10 <= p < 30:
-            zs[p - 10] = z[8:48]
+            zs[p - 10] = zfull[p, 8:48]
 
     def rest(p):
         z = zfull[p]
@@ -517,7 +544,7 @@
     return jax.ShapeDtypeStruct(dims, F32)
 
 
-def call(kernel, outs, scratch, *args):
+def call(kernel, outs, scratch, *args, aliases=None):
     whole = pl.BlockSpec(memory_space=pltpu.VMEM)
     return pl.pallas_call(
         kernel,
@@ -525,6 +552,7 @@
         in_specs=[whole] * len(args),
         out_specs=jax.tree.map(lambda _: whole, outs),
         scratch_shapes=[pltpu.VMEM(s, F32) for s in scratch],
+        input_output_aliases=aliases or {},
         compiler_params=pltpu.CompilerParams(vmem_limit_bytes=24 * 1024 * 1024),
     )(*args)
 
@@ -538,14 +566,20 @@
     return shift(own, "gy", GY, 1), own, shift(own, "gy", GY, -1)
 
 
-def pre_call(first, *args):
+def early_call(first, *args):
+    big = shape(EX, EY, EZ)
+    return call(functools.partial(early_kernel, first), (big,) * (3 if first else 2), [], *args)
+
+
+def pre_call(first, pieces, early, given=()):
+    big = shape(EX, EY, EZ)
     kept = (shape(20, PY, EZ), shape(20, PY, EZ), shape(MX, MY, MZ), shape(MX, MY, MZ),
             shape(GX * GZ, 16 if first else 8, 128))
-    scratch = [(EX, EY, EZ), (EX, EY, EZ), (MX * EY, EZ), (MX * EY, MZ), (MX, MY, MZ), (16, 128)]
+    scratch = [(MX * EY, EZ), (MX * EY, MZ), (MX, MY, MZ), (16, 128)]
+    outs = (big,) * len(early) + ((shape(MX, MY, MZ),) if first else ()) + kept
+    aliases = {len(pieces) + i: i for i in range(len(early))}
     kernel = functools.partial(pre_kernel, first)
-    if first:
-        kept = (shape(EX, EY, EZ), shape(MX, MY, MZ)) + kept
-    return call(kernel, kept, scratch, *args)
+    return call(kernel, outs, scratch, *pieces, *early, *given, aliases=aliases)[2:]
 
 
 def post_call(parts, kept, d0, d1, *old):
@@ -577,21 +611,23 @@
     edge = shape(168, 8, BZ)
     pieces = (right_side, diagonal, xlo, xhi, zl, zr)
     down, up = call(y_pack_kernel, (edge, edge), [], *pieces)
-    return *pieces, shift(up, "gy", GY, 1), shift(down, "gy", GY, -1)
-
-
-def later_exchange(q, q_down, q_up, q_halo):
+    early = early_call(True, *pieces)
+    return (*pieces, shift(up, "gy", GY, 1), shift(down, "gy", GY, -1)), early
+
+
+def later_exchange(d0, q, q_down, q_up, q_halo):
     xlo = shift(q_up, "gx", GX, 1)
     xhi = shift(q_down, "gx", GX, -1)
     edge = shape(75, 8, BZ)
     down, up = call(y_pack_later_kernel, (edge, edge), [], q, q_halo, xlo, xhi)
-    return q, q_halo, xlo, xhi, shift(up, "gy", GY, 1), shift(down, "gy", GY, -1)
+    early = early_call(False, q, q_halo, xlo, xhi, d0)
+    return (q, q_halo, xlo, xhi, shift(up, "gy", GY, 1), shift(down, "gy", GY, -1)), early
 
 
 def local(right_side, diagonal):
     d0, d1, *kept = pre_call(True, *first_exchange(right_side, diagonal))
     d2, z, q, *edges = post_call(spread_coarse(kept[-1]), kept[:-1], d0, d1)
-    kept = pre_call(False, *later_exchange(q, *edges), d0, d1)
+    kept = pre_call(False, *later_exchange(d0, q, *edges), (d0, d1))
     p, w, dots = post_call(
         spread_coarse(kept[-1]), kept[:-1], d0, d1, d2, right_side, z, q
     )

time: 147 us -> 145 us (0.986)
  waiting for transfers between devices: 38 us -> 35.9 us
    ppermute x14, waiting for transfers between devices: 38 us -> 35.9 us  [shift(): lax.ppermute(value, axis, [(i, (i + by) % count) for i in range(count)])]
    pallas_call x8 -> x10, Pallas kernels: 21.5 us -> 21.8 us  [call(): pl.pallas_call(kernel, out_shape=outs, in_specs=[whole] * len(args), out_...]
  transfers between devices with their start and end apart: 14 -> 14, of which waited for: 11 -> 11; matrix products, arithmetic and copies ran while one was open for 0% -> 0% of each run, Pallas kernels for 0% -> 1%
where the time goes in v5:
time: 145 us
  blocking collectives  56.7 us (39%)
  waiting for transfers between devices  35.9 us (25%)
  starting transfers between devices  28.5 us (20%)
  Pallas kernels  21.8 us (15%)
    ppermute x14, waiting for transfers between devices, shift(): lax.ppermute(value, axis, [(i, (i + by) % count) for i in range(count)])  35.9 us
    all_to_all x2, blocking collectives, spread_coarse(): own = lax.all_to_all(packed, ('gx', 'gz'), 0, 0)  34 us
    ppermute x14, starting transfers between devices, shift(): lax.ppermute(value, axis, [(i, (i + by) % count) for i in range(count)])  28.5 us
    all_to_all x1, blocking collectives, local(): sums = lax.all_to_all(dots, ('gx', 'gy', 'gz'), 0, 0)  22.7 us
    pallas_call x10, Pallas kernels, call(): pl.pallas_call(kernel, out_shape=outs, in_specs=[whole] * len(args), out_...  21.8 us
  transfers between devices with their start and end apart: 14, of which 11 were waited for; matrix products, arithmetic and copies ran while one was open for 0% of the time, Pallas kernels for 1%

profile of v5, /device:TPU:1, one launch (start us, length us, event | category | flops | bytes accessed | tf_op | source)
XLA Modules:
  0.0 145.0 jit_solution(6537558649591604612)
XLA Ops:
  0.6 0.0 copy-start
  0.6 0.0 copy-start.1
  0.6 1.3 slice_bitcast_fusion
  2.0 2.1 %collective-permute-start = (f32[2,12,32,128]{3,2,1,0:T(8,128)S(1)}, f32[2,12,32,128]{3,2,1,0:T(8,128)S(1)}, u32[]{:S(2)}, u32[]{:S(2)}) collective-permute-start(f32[2,12,32,128]{3,2,1,0:T(8,128)S(1)} %pad_maximum_fusion), channel_id=1, source_target_pairs={{0,64},{64,128},{128,192},{192,0},{1,65},{65,129},{129,193},{193,1... | collective-permute-start | bytes 1179656 | tf_op jit(solution)/shard_map/ppermute | solution.py:561
  4.2 1.4 collective-permute-start.1
  5.5 6.4 %collective-permute-done.xlo.refs_2_ = f32[2,12,32,128]{3,2,1,0:T(8,128)S(1)} collective-permute-done((f32[2,12,32,128]{3,2,1,0:T(8,128)S(1)}, f32[2,12,32,128]{3,2,1,0:T(8,128)S(1)}, u32[]{:S(2)}, u32[]{:S(2)}) %collective-permute-start) | collective-permute-done | bytes 393248 | tf_op jit(solution)/shard_map/ppermute | solution.py:561
  11.9 1.7 %collective-permute-done.1.xhi.refs_3_ = f32[2,12,32,128]{3,2,1,0:T(8,128)S(1)} collective-permute-done((f32[2,12,32,128]{3,2,1,0:T(8,128)S(1)}, f32[2,12,32,128]{3,2,1,0:T(8,128)S(1)}, u32[]{:S(2)}, u32[]{:S(2)}) %collective-permute-start.1) | collective-permute-done | bytes 393248 | tf_op jit(solution)/shard_map/ppermute | solution.py:561
  13.6 0.0 copy-done
  13.6 0.0 copy-done.1
  13.6 0.7 shard_map.41
  14.3 2.2 %collective-permute-start.2 = (f32[2,8,32,128]{3,2,1,0:T(8,128)S(1)}, f32[2,8,32,128]{3,2,1,0:T(8,128)S(1)}, u32[]{:S(2)}, u32[]{:S(2)}) collective-permute-start(f32[2,8,32,128]{3,2,1,0:T(8,128)S(1)} %get-tuple-element.34), channel_id=1, source_target_pairs={{0,1},{1,2},{2,3},{3,4},{4,5},{5,6},{6,7},{7,0},{8,9},{9,10},{10,1... | collective-permute-start | bytes 786440 | tf_op jit(solution)/shard_map/ppermute | solution.py:561
  16.5 4.0 %collective-permute-start.3 = (f32[2,8,32,128]{3,2,1,0:T(8,128)S(1)}, f32[2,8,32,128]{3,2,1,0:T(8,128)S(1)}, u32[]{:S(2)}, u32[]{:S(2)}) collective-permute-start(f32[2,8,32,128]{3,2,1,0:T(8,128)S(1)} %get-tuple-element.35), channel_id=1, source_target_pairs={{0,7},{1,0},{2,1},{3,2},{4,3},{5,4},{6,5},{7,6},{8,15},{9,8},{10,9... | collective-permute-start | bytes 786440 | tf_op jit(solution)/shard_map/ppermute | solution.py:561
  20.5 4.9 %collective-permute-done.2.zl.refs_4_ = f32[2,8,32,128]{3,2,1,0:T(8,128)S(1)} collective-permute-done((f32[2,8,32,128]{3,2,1,0:T(8,128)S(1)}, f32[2,8,32,128]{3,2,1,0:T(8,128)S(1)}, u32[]{:S(2)}, u32[]{:S(2)}) %collective-permute-start.2) | collective-permute-done | bytes 262176 | tf_op jit(solution)/shard_map/ppermute | solution.py:561
  25.4 0.0 collective-permute-done.3.zr.refs_5_
  25.4 0.1 shard_map.42
  25.5 3.5 %collective-permute-start.4 = (f32[168,8,128]{2,1,0:T(8,128)S(1)}, f32[168,8,128]{2,1,0:T(8,128)S(1)}, u32[]{:S(2)}, u32[]{:S(2)}) collective-permute-start(f32[168,8,128]{2,1,0:T(8,128)S(1)} %get-tuple-element.36), channel_id=1, source_target_pairs={{0,8},{8,16},{16,24},{24,32},{32,40},{40,48},{48,56},{56,0},{1,9},... | collective-permute-start | bytes 2064392 | tf_op jit(solution)/shard_map/ppermute | solution.py:561
  29.0 0.0 collective-permute-start.5
  29.0 1.2 shard_map.43
  30.2 6.7 %collective-permute-done.4.refs_6_ = f32[168,8,128]{2,1,0:T(8,128)S(1)} collective-permute-done((f32[168,8,128]{2,1,0:T(8,128)S(1)}, f32[168,8,128]{2,1,0:T(8,128)S(1)}, u32[]{:S(2)}, u32[]{:S(2)}) %collective-permute-start.4) | collective-permute-done | bytes 688160 | tf_op jit(solution)/shard_map/ppermute | solution.py:561
  36.9 2.5 %collective-permute-done.5.refs_7_ = f32[168,8,128]{2,1,0:T(8,128)S(1)} collective-permute-done((f32[168,8,128]{2,1,0:T(8,128)S(1)}, f32[168,8,128]{2,1,0:T(8,128)S(1)}, u32[]{:S(2)}, u32[]{:S(2)}) %collective-permute-start.5) | collective-permute-done | bytes 688160 | tf_op jit(solution)/shard_map/ppermute | solution.py:561
  39.4 4.2 %shard_map.44 = (f32[40,56,256]{2,1,0:T(8,128)S(1)}, f32[40,56,256]{2,1,0:T(8,128)S(1)}, f32[40,56,256]{2,1,0:T(8,128)S(1)}, f32[20,32,128]{2,1,0:T(8,128)S(1)},...) custom-call(f32[16,32,128]{2,1,0:T(8,128)S(1)} %copy-done, ...), custom_call_target="tpu_custom_call", output_to_operand_aliasing={{0}: (8, {}), {1}: (9, {}), {2}: (10, {})} | custom-call | tf_op jit(solution)/shard_map/pallas_call | solution.py:549
  43.6 18.2 %all_to_all.15.refs_1_ = f32[32,16,128]{2,1,0:T(8,128)S(1)} all-to-all(f32[32,16,128]{2,1,0:T(8,128)S(1)} %get-tuple-element.41), channel_id=1, replica_groups=mesh['gx'=4,'gy'=8,'gz'=8] {'gx','gz'}, dimensions={0} | all-to-all | bytes 524288 | tf_op jit(solution)/shard_map/all_to_all | solution.py:565
  61.9 2.4 %collective-permute-start.7 = (f32[32,16,128]{2,1,0:T(8,128)S(1)}, f32[32,16,128]{2,1,0:T(8,128)S(1)}, u32[]{:S(2)}, u32[]{:S(2)}) collective-permute-start(f32[32,16,128]{2,1,0:T(8,128)S(1)} %all_to_all.15.refs_1_), channel_id=1, source_target_pairs={{0,56},{8,0},{16,8},{24,16},{32,24},{40,32},{48,40},{56,48},{1,57}... | collective-permute-start | bytes 786440 | tf_op jit(solution)/shard_map/ppermute | solution.py:561
  64.3 0.0 collective-permute-start.6
  64.3 3.4 %collective-permute-done.7.refs_2_ = f32[32,16,128]{2,1,0:T(8,128)S(1)} collective-permute-done((f32[32,16,128]{2,1,0:T(8,128)S(1)}, f32[32,16,128]{2,1,0:T(8,128)S(1)}, u32[]{:S(2)}, u32[]{:S(2)}) %collective-permute-start.7) | collective-permute-done | bytes 262176 | tf_op jit(solution)/shard_map/ppermute | solution.py:561
  67.7 0.0 collective-permute-done.6.refs_0_
  67.7 5.3 %shard_map.45 = (f32[28,24,256]{2,1,0:T(8,128)S(1)}, f32[16,32,128]{2,1,0:T(8,128)S(1)}, f32[16,32,128]{2,1,0:T(8,128)S(1)}, f32[15,32,128]{2,1,0:T(8,128)S(1)},...) custom-call(f32[32,16,128]{2,1,0:T(8,128)S(1)} %collective-permute-done.6.refs_0_, ...), custom_call_target="tpu_custom_call" | custom-call | tf_op jit(solution)/shard_map/pallas_call | solution.py:549
  73.0 0.8 collective-permute-start.8
  73.7 2.0 %collective-permute-start.9 = (f32[15,32,128]{2,1,0:T(8,128)S(1)}, f32[15,32,128]{2,1,0:T(8,128)S(1)}, u32[]{:S(2)}, u32[]{:S(2)}) collective-permute-start(f32[15,32,128]{2,1,0:T(8,128)S(1)} %get-tuple-element.52), channel_id=1, source_target_pairs={{0,192},{64,0},{128,64},{192,128},{1,193},{65,1},{129,65},{193,129... | collective-permute-start | bytes 737288 | tf_op jit(solution)/shard_map/ppermute | solution.py:561
  75.7 3.6 %collective-permute-done.8.xlo.refs_2_ = f32[15,32,128]{2,1,0:T(8,128)S(1)} collective-permute-done((f32[15,32,128]{2,1,0:T(8,128)S(1)}, f32[15,32,128]{2,1,0:T(8,128)S(1)}, u32[]{:S(2)}, u32[]{:S(2)}) %collective-permute-start.8) | collective-permute-done | bytes 245792 | tf_op jit(solution)/shard_map/ppermute | solution.py:561
  79.3 0.0 collective-permute-done.9.xhi.refs_3_
  79.3 0.1 shard_map.46
  79.4 5.5 %collective-permute-start.10 = (f32[75,8,128]{2,1,0:T(8,128)S(1)}, f32[75,8,128]{2,1,0:T(8,128)S(1)}, u32[]{:S(2)}, u32[]{:S(2)}) collective-permute-start(f32[75,8,128]{2,1,0:T(8,128)S(1)} %get-tuple-element.53), channel_id=1, source_target_pairs={{0,8},{8,16},{16,24},{24,32},{32,40},{40,48},{48,56},{56,0},{1,9},... | collective-permute-start | bytes 921608 | tf_op jit(solution)/shard_map/ppermute | solution.py:561
  84.9 1.1 collective-permute-start.11
  85.9 0.9 shard_map.47
  86.9 1.8 %collective-permute-done.10.refs_4_ = f32[75,8,128]{2,1,0:T(8,128)S(1)} collective-permute-done((f32[75,8,128]{2,1,0:T(8,128)S(1)}, f32[75,8,128]{2,1,0:T(8,128)S(1)}, u32[]{:S(2)}, u32[]{:S(2)}) %collective-permute-start.10) | collective-permute-done | bytes 307232 | tf_op jit(solution)/shard_map/ppermute | solution.py:561
  88.7 2.8 %collective-permute-done.11.refs_5_ = f32[75,8,128]{2,1,0:T(8,128)S(1)} collective-permute-done((f32[75,8,128]{2,1,0:T(8,128)S(1)}, f32[75,8,128]{2,1,0:T(8,128)S(1)}, u32[]{:S(2)}, u32[]{:S(2)}) %collective-permute-start.11) | collective-permute-done | bytes 307232 | tf_op jit(solution)/shard_map/ppermute | solution.py:561
  91.4 3.4 %shard_map.48 = (f32[40,56,256]{2,1,0:T(8,128)S(1)}, f32[40,56,256]{2,1,0:T(8,128)S(1)}, f32[20,40,256]{2,1,0:T(8,128)S(1)}, f32[20,40,256]{2,1,0:T(8,128)S(1)},...) custom-call(f32[16,32,128]{2,1,0:T(8,128)S(1)} %get-tuple-element.49, ...), custom_call_target="tpu_custom_call", output_to_operand_aliasing={{0}: (6, {}), {1}: (7, {})} | custom-call | tf_op jit(solution)/shard_map/pallas_call | solution.py:549
  94.9 15.8 %all_to_all.16.refs_1_ = f32[32,8,128]{2,1,0:T(8,128)S(1)} all-to-all(f32[32,8,128]{2,1,0:T(8,128)S(1)} %get-tuple-element.57), channel_id=1, replica_groups=mesh['gx'=4,'gy'=8,'gz'=8] {'gx','gz'}, dimensions={0} | all-to-all | bytes 262144 | tf_op jit(solution)/shard_map/all_to_all | solution.py:565
  110.7 3.6 %collective-permute-start.13 = (f32[32,8,128]{2,1,0:T(8,128)S(1)}, f32[32,8,128]{2,1,0:T(8,128)S(1)}, u32[]{:S(2)}, u32[]{:S(2)}) collective-permute-start(f32[32,8,128]{2,1,0:T(8,128)S(1)} %all_to_all.16.refs_1_), channel_id=1, source_target_pairs={{0,56},{8,0},{16,8},{24,16},{32,24},{40,32},{48,40},{56,48},{1,57}... | collective-permute-start | bytes 393224 | tf_op jit(solution)/shard_map/ppermute | solution.py:561
  114.3 0.0 collective-permute-start.12
  114.3 1.0 collective-permute-done.13.refs_2_
  115.3 1.2 collective-permute-done.12.refs_0_
  116.5 4.6 %shard_map.49 = (f32[16,32,128]{2,1,0:T(8,128)S(1)}, f32[16,32,128]{2,1,0:T(8,128)S(1)}, f32[256,1,128]{2,1,0:T(1,128)S(1)}) custom-call(f32[32,8,128]{2,1,0:T(8,128)S(1)} %collective-permute-done.12.refs_0_, f32[32,8,128]{2,1,0:T(8,128)S(1)} %all_to_all.16.refs_1_, f32[32,8,128]{2,1,0:T(8,128)S(1)} %collective-permute-done.13.refs_2_, ...), custom_call_target="tpu_custom_call" | custom-call | tf_op jit(solution)/shard_map/pallas_call | solution.py:549
  121.1 22.7 %all_to_all.17.sums = f32[256,1,128]{2,1,0:T(1,128)S(1)} all-to-all(f32[256,1,128]{2,1,0:T(1,128)S(1)} %get-tuple-element.65), channel_id=1, replica_groups=mesh['gx'=4,'gy'=8,'gz'=8] {'gx','gy','gz'}, dimensions={0} | all-to-all | bytes 262144 | tf_op jit(solution)/shard_map/all_to_all | solution.py:634
  143.8 1.3 shard_map.50
  (2 shorter events, 0.1 us)
Async XLA Ops:
  0.6 13.0 %copy-start = (f32[16,32,128]{2,1,0:T(8,128)S(1)}, f32[16,32,128]{2,1,0:T(8,128)}, u32[]{:S(2)}) copy-start(f32[16,32,128]{2,1,0:T(8,128)} %r.1) | copy-start | bytes 786436
  0.6 13.0 %copy-start.1 = (f32[16,32,128]{2,1,0:T(8,128)S(1)}, f32[16,32,128]{2,1,0:T(8,128)}, u32[]{:S(2)}) copy-start(f32[16,32,128]{2,1,0:T(8,128)} %refs_1_.3) | copy-start | bytes 786436
  2.0 9.9 %collective-permute-start = (f32[2,12,32,128]{3,2,1,0:T(8,128)S(1)}, f32[2,12,32,128]{3,2,1,0:T(8,128)S(1)}, u32[]{:S(2)}, u32[]{:S(2)}) collective-permute-start(f32[2,12,32,128]{3,2,1,0:T(8,128)S(1)} %pad_maximum_fusion), channel_id=1, source_target_pairs={{0,64},{64,128},{128,192},{192,0},{1,65},{65,129},{129,193},{193,1... | collective-permute-start | bytes 1179656 | tf_op jit(solution)/shard_map/ppermute | solution.py:561
  4.2 9.5 %collective-permute-start.1 = (f32[2,12,32,128]{3,2,1,0:T(8,128)S(1)}, f32[2,12,32,128]{3,2,1,0:T(8,128)S(1)}, u32[]{:S(2)}, u32[]{:S(2)}) collective-permute-start(f32[2,12,32,128]{3,2,1,0:T(8,128)S(1)} %pad_maximum_fusion.1), channel_id=1, source_target_pairs={{0,192},{64,0},{128,64},{192,128},{1,193},{65,1},{129,65},{193,129... | collective-permute-start | bytes 1179656 | tf_op jit(solution)/shard_map/ppermute | solution.py:561
  14.3 11.1 %collective-permute-start.2 = (f32[2,8,32,128]{3,2,1,0:T(8,128)S(1)}, f32[2,8,32,128]{3,2,1,0:T(8,128)S(1)}, u32[]{:S(2)}, u32[]{:S(2)}) collective-permute-start(f32[2,8,32,128]{3,2,1,0:T(8,128)S(1)} %get-tuple-element.34), channel_id=1, source_target_pairs={{0,1},{1,2},{2,3},{3,4},{4,5},{5,6},{6,7},{7,0},{8,9},{9,10},{10,1... | collective-permute-start | bytes 786440 | tf_op jit(solution)/shard_map/ppermute | solution.py:561
  16.5 8.9 %collective-permute-start.3 = (f32[2,8,32,128]{3,2,1,0:T(8,128)S(1)}, f32[2,8,32,128]{3,2,1,0:T(8,128)S(1)}, u32[]{:S(2)}, u32[]{:S(2)}) collective-permute-start(f32[2,8,32,128]{3,2,1,0:T(8,128)S(1)} %get-tuple-element.35), channel_id=1, source_target_pairs={{0,7},{1,0},{2,1},{3,2},{4,3},{5,4},{6,5},{7,6},{8,15},{9,8},{10,9... | collective-permute-start | bytes 786440 | tf_op jit(solution)/shard_map/ppermute | solution.py:561
  25.5 11.4 %collective-permute-start.4 = (f32[168,8,128]{2,1,0:T(8,128)S(1)}, f32[168,8,128]{2,1,0:T(8,128)S(1)}, u32[]{:S(2)}, u32[]{:S(2)}) collective-permute-start(f32[168,8,128]{2,1,0:T(8,128)S(1)} %get-tuple-element.36), channel_id=1, source_target_pairs={{0,8},{8,16},{16,24},{24,32},{32,40},{40,48},{48,56},{56,0},{1,9},... | collective-permute-start | bytes 2064392 | tf_op jit(solution)/shard_map/ppermute | solution.py:561
  29.0 10.4 %collective-permute-start.5 = (f32[168,8,128]{2,1,0:T(8,128)S(1)}, f32[168,8,128]{2,1,0:T(8,128)S(1)}, u32[]{:S(2)}, u32[]{:S(2)}) collective-permute-start(f32[168,8,128]{2,1,0:T(8,128)S(1)} %get-tuple-element.37), channel_id=1, source_target_pairs={{0,56},{8,0},{16,8},{24,16},{32,24},{40,32},{48,40},{56,48},{1,57}... | collective-permute-start | bytes 2064392 | tf_op jit(solution)/shard_map/ppermute | solution.py:561
  61.9 5.8 %collective-permute-start.7 = (f32[32,16,128]{2,1,0:T(8,128)S(1)}, f32[32,16,128]{2,1,0:T(8,128)S(1)}, u32[]{:S(2)}, u32[]{:S(2)}) collective-permute-start(f32[32,16,128]{2,1,0:T(8,128)S(1)} %all_to_all.15.refs_1_), channel_id=1, source_target_pairs={{0,56},{8,0},{16,8},{24,16},{32,24},{40,32},{48,40},{56,48},{1,57}... | collective-permute-start | bytes 786440 | tf_op jit(solution)/shard_map/ppermute | solution.py:561
  64.3 3.4 %collective-permute-start.6 = (f32[32,16,128]{2,1,0:T(8,128)S(1)}, f32[32,16,128]{2,1,0:T(8,128)S(1)}, u32[]{:S(2)}, u32[]{:S(2)}) collective-permute-start(f32[32,16,128]{2,1,0:T(8,128)S(1)} %all_to_all.15.refs_1_), channel_id=1, source_target_pairs={{0,8},{8,16},{16,24},{24,32},{32,40},{40,48},{48,56},{56,0},{1,9},... | collective-permute-start | bytes 786440 | tf_op jit(solution)/shard_map/ppermute | solution.py:561
  73.0 6.3 %collective-permute-start.8 = (f32[15,32,128]{2,1,0:T(8,128)S(1)}, f32[15,32,128]{2,1,0:T(8,128)S(1)}, u32[]{:S(2)}, u32[]{:S(2)}) collective-permute-start(f32[15,32,128]{2,1,0:T(8,128)S(1)} %get-tuple-element.51), channel_id=1, source_target_pairs={{0,64},{64,128},{128,192},{192,0},{1,65},{65,129},{129,193},{193,1... | collective-permute-start | bytes 737288 | tf_op jit(solution)/shard_map/ppermute | solution.py:561
  73.7 5.5 %collective-permute-start.9 = (f32[15,32,128]{2,1,0:T(8,128)S(1)}, f32[15,32,128]{2,1,0:T(8,128)S(1)}, u32[]{:S(2)}, u32[]{:S(2)}) collective-permute-start(f32[15,32,128]{2,1,0:T(8,128)S(1)} %get-tuple-element.52), channel_id=1, source_target_pairs={{0,192},{64,0},{128,64},{192,128},{1,193},{65,1},{129,65},{193,129... | collective-permute-start | bytes 737288 | tf_op jit(solution)/shard_map/ppermute | solution.py:561
  79.4 9.3 %collective-permute-start.10 = (f32[75,8,128]{2,1,0:T(8,128)S(1)}, f32[75,8,128]{2,1,0:T(8,128)S(1)}, u32[]{:S(2)}, u32[]{:S(2)}) collective-permute-start(f32[75,8,128]{2,1,0:T(8,128)S(1)} %get-tuple-element.53), channel_id=1, source_target_pairs={{0,8},{8,16},{16,24},{24,32},{32,40},{40,48},{48,56},{56,0},{1,9},... | collective-permute-start | bytes 921608 | tf_op jit(solution)/shard_map/ppermute | solution.py:561
  84.9 6.6 %collective-permute-start.11 = (f32[75,8,128]{2,1,0:T(8,128)S(1)}, f32[75,8,128]{2,1,0:T(8,128)S(1)}, u32[]{:S(2)}, u32[]{:S(2)}) collective-permute-start(f32[75,8,128]{2,1,0:T(8,128)S(1)} %get-tuple-element.54), channel_id=1, source_target_pairs={{0,56},{8,0},{16,8},{24,16},{32,24},{40,32},{48,40},{56,48},{1,57}... | collective-permute-start | bytes 921608 | tf_op jit(solution)/shard_map/ppermute | solution.py:561
  110.7 4.6 %collective-permute-start.13 = (f32[32,8,128]{2,1,0:T(8,128)S(1)}, f32[32,8,128]{2,1,0:T(8,128)S(1)}, u32[]{:S(2)}, u32[]{:S(2)}) collective-permute-start(f32[32,8,128]{2,1,0:T(8,128)S(1)} %all_to_all.16.refs_1_), channel_id=1, source_target_pairs={{0,56},{8,0},{16,8},{24,16},{32,24},{40,32},{48,40},{56,48},{1,57}... | collective-permute-start | bytes 393224 | tf_op jit(solution)/shard_map/ppermute | solution.py:561
  114.3 2.2 %collective-permute-start.12 = (f32[32,8,128]{2,1,0:T(8,128)S(1)}, f32[32,8,128]{2,1,0:T(8,128)S(1)}, u32[]{:S(2)}, u32[]{:S(2)}) collective-permute-start(f32[32,8,128]{2,1,0:T(8,128)S(1)} %all_to_all.16.refs_1_), channel_id=1, source_target_pairs={{0,8},{8,16},{16,24},{24,32},{32,40},{40,48},{48,56},{56,0},{1,9},... | collective-permute-start | bytes 393224 | tf_op jit(solution)/shard_map/ppermute | solution.py:561

commit v6 on v5

--- a/solution.py
+++ b/solution.py
@@ -232,8 +232,17 @@
     y_rows(planes, 0, down, up)
 
 
-def halve(pairs, rows, z_map, dst, scale):
-    rows[...] = dot(pairs[...], z_map)
+def z_halve(rows, pairs, chunks):
+    size = sum(hi - lo for lo, hi in chunks)
+    narrow = dot(pairs[...], halving(EZ, MZ))
+    for i in range(MX):
+        at = i * size
+        for lo, hi in chunks:
+            rows[i * EY + lo : i * EY + hi] = narrow[at : at + hi - lo]
+            at += hi - lo
+
+
+def y_halve(rows, dst, scale):
     for p in range(MX):
         at = p * EY
         total = rows[pl.ds(at, MR, stride=2), :] + rows[pl.ds(at + 1, MR, stride=2), :]
@@ -241,65 +250,106 @@
         dst[p, MR:] = jnp.zeros((MY - MR, MZ), F32)
 
 
+def clear_ends(pairs):
+    size = pairs.shape[0] // MX
+    pairs[0:size] = jnp.zeros((size, EZ), F32)
+    pairs[(MX - 1) * size :] = jnp.zeros((size, EZ), F32)
+
+
+MIDDLE, OUTER = ((16, 40),), ((0, 16), (40, 56))
+
+
 def early_kernel(first, *refs):
     if first:
-        right_side, diagonal, xlo, xhi, zl, zr, field, zfull, d0 = refs
+        right_side, diagonal, xlo, xhi, zl, zr = refs[:6]
+        field, zfull, zs, rs, rows, d0, d_rows, pairs = refs[6:]
         assemble_field(field, first_parts(0, right_side, xlo, xhi, zl, zr, None, None))
         assemble_diagonal(d0, first_parts(1, diagonal, xlo, xhi, zl, zr, None, None))
+        for i in range(MX):
+            pairs[24 * i : 24 * i + 24] = d0[2 * i, 16:40] + d0[2 * i + 1, 16:40]
+        z_halve(d_rows, pairs, MIDDLE)
     else:
-        own, halo, xlo, xhi, d0, field, zfull = refs
+        own, halo, xlo, xhi, d0 = refs[:5]
+        field, zfull, zs, rs, rows, pairs = refs[5:]
         assemble_field(field, later_parts(own, halo, xlo, xhi, None, None))
-    mask = x_masks(plane_mask(0, (24, EZ), 16 - HY), 0, CA)
+    mask = x_masks(plane_mask(0, (PY, EZ), 8 - HY), 0, CA)
     for p in range(1, EX - 1):
-        total = field[p - 1, 8:48] + field[p, 8:48] + field[p + 1, 8:48]
+        r = field[p, 8:48]
+        box = spread(field[p - 1, 8:48] + r + field[p + 1, 8:48])
+        z = (CR + CA * d0[p, 8:48]) * r - mask(p) * box
+        zfull[p, 8:48] = z
+        if 10 <= p < 30:
+            zs[p - 10, 8:32] = z[8:32]
+
+    def rest(p):
+        total = zfull[p - 1, 8:48] + zfull[p, 8:48] + zfull[p + 1, 8:48]
         box = spread_z(spread_y(total)[8:32])
-        zfull[p, 16:40] = (CR + CA * d0[p, 16:40]) * field[p, 16:40] - mask(p) * box
+        left = field[p, 16:40] - d0[p, 16:40] * zfull[p, 16:40] + box
+        if 10 <= p < 30:
+            rs[p - 10, 8:32] = left
+        return left
+
+    clear_ends(pairs)
+    for i in range(1, MX - 1):
+        pairs[24 * i : 24 * i + 24] = rest(2 * i) + rest(2 * i + 1)
+    z_halve(rows, pairs, MIDDLE)
 
 
 def pre_kernel(first, *refs):
     if first:
         right_side, diagonal, xlo, xhi, zl, zr, ylo, yhi = refs[:8]
-        field, zfull, d0, d1, zs, rs, z1, left1, packed, pairs, rows, r1, small = refs[11:]
+        field, zfull, zs, rs, rows, d0, d_rows, d1 = refs[15:23]
+        z1, left1, packed, pairs, r1, small = refs[23:]
         assemble_field(field, first_parts(0, right_side, xlo, xhi, zl, zr, ylo, yhi))
+        assemble_diagonal(d0, first_parts(1, diagonal, xlo, xhi, zl, zr, ylo, yhi))
+        for i in range(MX):
+            at = 32 * i
+            pairs[at : at + 16] = d0[2 * i, 0:16] + d0[2 * i + 1, 0:16]
+            pairs[at + 16 : at + 32] = d0[2 * i, 40:56] + d0[2 * i + 1, 40:56]
+        z_halve(d_rows, pairs, OUTER)
+        y_halve(d_rows, d1, 0.125)
     else:
         own, halo, xlo, xhi, ylo, yhi = refs[:6]
-        d0, d1 = refs[8:10]
-        field, zfull, zs, rs, z1, left1, packed, pairs, rows, r1, small = refs[10:]
+        d0, d1 = refs[11:13]
+        field, zfull, zs, rs, rows = refs[13:18]
+        z1, left1, packed, pairs, r1, small = refs[18:]
         assemble_field(field, later_parts(own, halo, xlo, xhi, ylo, yhi))
-    z_map = halving(EZ, MZ)
-    if first:
-        assemble_diagonal(d0, first_parts(1, diagonal, xlo, xhi, zl, zr, ylo, yhi))
-        for i in range(MX):
-            pairs[i * EY : (i + 1) * EY, :] = d0[2 * i] + d0[2 * i + 1]
-        halve(pairs, rows, z_map, d1, 0.125)
-    pairs[0:EY, :] = jnp.zeros((EY, EZ), F32)
-    pairs[(MX - 1) * EY :, :] = jnp.zeros((EY, EZ), F32)
     low = x_masks(plane_mask(0, (16, EZ), -HY), 0, CA)
     high = x_masks(plane_mask(0, (16, EZ), 40 - HY), 0, CA)
 
     def smooth(p):
         total = field[p - 1, 0:24] + field[p, 0:24] + field[p + 1, 0:24]
         box = spread_z(spread_y(total)[0:16])
-        zfull[p, 0:16] = (CR + CA * d0[p, 0:16]) * field[p, 0:16] - low(p) * box
+        z = (CR + CA * d0[p, 0:16]) * field[p, 0:16] - low(p) * box
+        zfull[p, 0:16] = z
         total = field[p - 1, 32:56] + field[p, 32:56] + field[p + 1, 32:56]
         box = spread_z(spread_y(total)[8:24])
-        zfull[p, 40:56] = (CR + CA * d0[p, 40:56]) * field[p, 40:56] - high(p) * box
+        y = (CR + CA * d0[p, 40:56]) * field[p, 40:56] - high(p) * box
+        zfull[p, 40:56] = y
         if 10 <= p < 30:
-            zs[p - 10] = zfull[p, 8:48]
+            zs[p - 10, 0:8] = z[8:16]
+            zs[p - 10, 32:40] = y[0:8]
 
     def rest(p):
-        z = zfull[p]
-        left = field[p] - d0[p] * z + spread(zfull[p - 1] + z + zfull[p + 1])
+        total = zfull[p - 1, 0:24] + zfull[p, 0:24] + zfull[p + 1, 0:24]
+        box = spread_z(spread_y(total)[0:16])
+        a = field[p, 0:16] - d0[p, 0:16] * zfull[p, 0:16] + box
+        total = zfull[p - 1, 32:56] + zfull[p, 32:56] + zfull[p + 1, 32:56]
+        box = spread_z(spread_y(total)[8:24])
+        b = field[p, 40:56] - d0[p, 40:56] * zfull[p, 40:56] + box
         if 10 <= p < 30:
-            rs[p - 10] = left[8:48]
-        return left
-
-    def rest_pair(i):
-        pairs[i * EY : (i + 1) * EY, :] = rest(2 * i) + rest(2 * i + 1)
-
+            rs[p - 10, 0:8] = a[8:16]
+            rs[p - 10, 32:40] = b[0:8]
+        return a, b
+
+    clear_ends(pairs)
     loop(1, EX - 1, smooth)
-    loop(1, MX - 1, rest_pair)
-    halve(pairs, rows, z_map, r1, 0.5)
+    for i in range(1, MX - 1):
+        (a, b), (c, d) = rest(2 * i), rest(2 * i + 1)
+        pairs[32 * i : 32 * i + 16] = a + c
+        pairs[32 * i + 16 : 32 * i + 32] = b + d
+    z_halve(rows, pairs, OUTER)
+    y_halve(rows, r1, 0.5)
     mask1 = plane_mask(1, (MY, MZ), -HY // 2)
     keep1, mask1 = x_masks(mask1, 1), x_masks(mask1, 1, CA)
 
@@ -332,7 +382,8 @@
         total = jnp.zeros((16, 128), F32)
         for k in range(4):
             s = src[6 + 2 * k, 6:22, :] + src[7 + 2 * k, 6:22, :]
-            total = total + dot(s, flag((lane // 2 + 32 * k == col) & (lane < 64)))
+            at = 32 * ((k + places()[2]) % 4)
+            total = total + dot(s, flag((lane // 2 + at == col) & (lane < 64)))
         small[...] = total
         return (small[pl.ds(0, 8, stride=2), :] + small[pl.ds(1, 8, stride=2), :]) * scale
 
@@ -351,8 +402,10 @@
                 for h in range(2):
                     acc = None
                     for j in range(4):
-                        block = turn(src[bx * GZ + 4 * h + j, row : row + 8, :], 32 * (j - k))
-                        acc = block if acc is None else jnp.where(group == j, block, acc)
+                        block = src[bx * GZ + 4 * h + j, row : row + 8, :]
+                        here = group == (j + k) % 4
+                        acc = block if acc is None else jnp.where(here, block, acc)
+                    acc = turn(acc, -32 * k)
                     rows = slice(8 * part, 8 * part + 8)
                     lanes = slice(128 * h, 128 * h + 128)
                     dst[6 + 4 * bx + k, rows, lanes] = acc if scale is None else acc * scale
@@ -567,19 +620,21 @@
 
 
 def early_call(first, *args):
-    big = shape(EX, EY, EZ)
-    return call(functools.partial(early_kernel, first), (big,) * (3 if first else 2), [], *args)
+    big, half, rows = shape(EX, EY, EZ), shape(20, PY, EZ), shape(MX * EY, MZ)
+    outs = (big, big, half, half, rows) + ((big, rows) if first else ())
+    return call(functools.partial(early_kernel, first), outs, [(MX * 24, EZ)], *args)
 
 
 def pre_call(first, pieces, early, given=()):
-    big = shape(EX, EY, EZ)
-    kept = (shape(20, PY, EZ), shape(20, PY, EZ), shape(MX, MY, MZ), shape(MX, MY, MZ),
-            shape(GX * GZ, 16 if first else 8, 128))
-    scratch = [(MX * EY, EZ), (MX * EY, MZ), (MX, MY, MZ), (16, 128)]
-    outs = (big,) * len(early) + ((shape(MX, MY, MZ),) if first else ()) + kept
+    level1 = shape(MX, MY, MZ)
+    new = (level1,) * (3 if first else 2) + (shape(GX * GZ, 16 if first else 8, 128),)
+    outs = tuple(shape(*a.shape) for a in early) + new
+    scratch = [(MX * 32, EZ), (MX, MY, MZ), (16, 128)]
     aliases = {len(pieces) + i: i for i in range(len(early))}
     kernel = functools.partial(pre_kernel, first)
-    return call(kernel, outs, scratch, *pieces, *early, *given, aliases=aliases)[2:]
+    outs = call(kernel, outs, scratch, *pieces, *early, *given, aliases=aliases)
+    kept = (*outs[2:4], *outs[-3:])
+    return (outs[5], outs[7], *kept) if first else kept
 
 
 def post_call(parts, kept, d0, d1, *old):

time: 145 us -> 143 us (0.986)
  waiting for transfers between devices: 35.9 us -> 33.3 us
    ppermute x14, waiting for transfers between devices: 35.9 us -> 33.3 us  [shift(): lax.ppermute(value, axis, [(i, (i + by) % count) for i in range(count)])]
  transfers between devices with their start and end apart: 14 -> 14, of which waited for: 11 -> 11; matrix products, arithmetic and copies ran while one was open for 0% -> 0% of each run, Pallas kernels for 1% -> 3%
where the time goes in v6:
time: 143 us
  blocking collectives  56.7 us (40%)
  waiting for transfers between devices  33.3 us (23%)
  starting transfers between devices  28.5 us (20%)
  Pallas kernels  22.1 us (15%)
    all_to_all x2, blocking collectives, spread_coarse(): own = lax.all_to_all(packed, ('gx', 'gz'), 0, 0)  34 us
    ppermute x14, waiting for transfers between devices, shift(): lax.ppermute(value, axis, [(i, (i + by) % count) for i in range(count)])  33.3 us
    ppermute x14, starting transfers between devices, shift(): lax.ppermute(value, axis, [(i, (i + by) % count) for i in range(count)])  28.5 us
    all_to_all x1, blocking collectives, local(): sums = lax.all_to_all(dots, ('gx', 'gy', 'gz'), 0, 0)  22.6 us
    pallas_call x10, Pallas kernels, call(): pl.pallas_call(kernel, out_shape=outs, in_specs=[whole] * len(args), out_...  22.1 us
  transfers between devices with their start and end apart: 14, of which 11 were waited for; matrix products, arithmetic and copies ran while one was open for 0% of the time, Pallas kernels for 3%

profile of v6, /device:TPU:1, one launch (start us, length us, event | category | flops | bytes accessed | tf_op | source)
XLA Modules:
  0.0 142.7 jit_solution(17828758481350178592)
XLA Ops:
  0.6 0.0 copy-start
  0.6 0.0 copy-start.1
  0.6 1.3 slice_bitcast_fusion
  2.0 2.1 %collective-permute-start = (f32[2,12,32,128]{3,2,1,0:T(8,128)S(1)}, f32[2,12,32,128]{3,2,1,0:T(8,128)S(1)}, u32[]{:S(2)}, u32[]{:S(2)}) collective-permute-start(f32[2,12,32,128]{3,2,1,0:T(8,128)S(1)} %pad_maximum_fusion), channel_id=1, source_target_pairs={{0,64},{64,128},{128,192},{192,0},{1,65},{65,129},{129,193},{193,1... | collective-permute-start | bytes 1179656 | tf_op jit(solution)/shard_map/ppermute | solution.py:614
  4.2 1.4 collective-permute-start.1
  5.5 6.4 %collective-permute-done.xlo.refs_2_ = f32[2,12,32,128]{3,2,1,0:T(8,128)S(1)} collective-permute-done((f32[2,12,32,128]{3,2,1,0:T(8,128)S(1)}, f32[2,12,32,128]{3,2,1,0:T(8,128)S(1)}, u32[]{:S(2)}, u32[]{:S(2)}) %collective-permute-start) | collective-permute-done | bytes 393248 | tf_op jit(solution)/shard_map/ppermute | solution.py:614
  11.9 1.7 %collective-permute-done.1.xhi.refs_3_ = f32[2,12,32,128]{3,2,1,0:T(8,128)S(1)} collective-permute-done((f32[2,12,32,128]{3,2,1,0:T(8,128)S(1)}, f32[2,12,32,128]{3,2,1,0:T(8,128)S(1)}, u32[]{:S(2)}, u32[]{:S(2)}) %collective-permute-start.1) | collective-permute-done | bytes 393248 | tf_op jit(solution)/shard_map/ppermute | solution.py:614
  13.6 0.0 copy-done
  13.6 0.0 copy-done.1
  13.6 0.7 shard_map.41
  14.3 2.2 %collective-permute-start.2 = (f32[2,8,32,128]{3,2,1,0:T(8,128)S(1)}, f32[2,8,32,128]{3,2,1,0:T(8,128)S(1)}, u32[]{:S(2)}, u32[]{:S(2)}) collective-permute-start(f32[2,8,32,128]{3,2,1,0:T(8,128)S(1)} %get-tuple-element.41), channel_id=1, source_target_pairs={{0,1},{1,2},{2,3},{3,4},{4,5},{5,6},{6,7},{7,0},{8,9},{9,10},{10,1... | collective-permute-start | bytes 786440 | tf_op jit(solution)/shard_map/ppermute | solution.py:614
  16.5 4.0 %collective-permute-start.3 = (f32[2,8,32,128]{3,2,1,0:T(8,128)S(1)}, f32[2,8,32,128]{3,2,1,0:T(8,128)S(1)}, u32[]{:S(2)}, u32[]{:S(2)}) collective-permute-start(f32[2,8,32,128]{3,2,1,0:T(8,128)S(1)} %get-tuple-element.42), channel_id=1, source_target_pairs={{0,7},{1,0},{2,1},{3,2},{4,3},{5,4},{6,5},{7,6},{8,15},{9,8},{10,9... | collective-permute-start | bytes 786440 | tf_op jit(solution)/shard_map/ppermute | solution.py:614
  20.5 4.9 %collective-permute-done.2.zl.refs_4_ = f32[2,8,32,128]{3,2,1,0:T(8,128)S(1)} collective-permute-done((f32[2,8,32,128]{3,2,1,0:T(8,128)S(1)}, f32[2,8,32,128]{3,2,1,0:T(8,128)S(1)}, u32[]{:S(2)}, u32[]{:S(2)}) %collective-permute-start.2) | collective-permute-done | bytes 262176 | tf_op jit(solution)/shard_map/ppermute | solution.py:614
  25.4 0.0 collective-permute-done.3.zr.refs_5_
  25.4 0.1 shard_map.42
  25.5 3.5 %collective-permute-start.4 = (f32[168,8,128]{2,1,0:T(8,128)S(1)}, f32[168,8,128]{2,1,0:T(8,128)S(1)}, u32[]{:S(2)}, u32[]{:S(2)}) collective-permute-start(f32[168,8,128]{2,1,0:T(8,128)S(1)} %get-tuple-element.43), channel_id=1, source_target_pairs={{0,8},{8,16},{16,24},{24,32},{32,40},{40,48},{48,56},{56,0},{1,9},... | collective-permute-start | bytes 2064392 | tf_op jit(solution)/shard_map/ppermute | solution.py:614
  29.0 0.0 collective-permute-start.5
  29.0 2.6 %shard_map.43 = (f32[40,56,256]{2,1,0:T(8,128)S(1)}, f32[40,56,256]{2,1,0:T(8,128)S(1)}, f32[20,40,256]{2,1,0:T(8,128)S(1)}, f32[20,40,256]{2,1,0:T(8,128)S(1)},...) custom-call(f32[16,32,128]{2,1,0:T(8,128)S(1)} %copy-done, ...), custom_call_target="tpu_custom_call" | custom-call | tf_op jit(solution)/shard_map/pallas_call | solution.py:602
  31.7 5.2 %collective-permute-done.4.refs_6_ = f32[168,8,128]{2,1,0:T(8,128)S(1)} collective-permute-done((f32[168,8,128]{2,1,0:T(8,128)S(1)}, f32[168,8,128]{2,1,0:T(8,128)S(1)}, u32[]{:S(2)}, u32[]{:S(2)}) %collective-permute-start.4) | collective-permute-done | bytes 688160 | tf_op jit(solution)/shard_map/ppermute | solution.py:614
  36.9 2.5 %collective-permute-done.5.refs_7_ = f32[168,8,128]{2,1,0:T(8,128)S(1)} collective-permute-done((f32[168,8,128]{2,1,0:T(8,128)S(1)}, f32[168,8,128]{2,1,0:T(8,128)S(1)}, u32[]{:S(2)}, u32[]{:S(2)}) %collective-permute-start.5) | collective-permute-done | bytes 688160 | tf_op jit(solution)/shard_map/ppermute | solution.py:614
  39.4 3.3 %shard_map.44 = (f32[40,56,256]{2,1,0:T(8,128)S(1)}, f32[40,56,256]{2,1,0:T(8,128)S(1)}, f32[20,40,256]{2,1,0:T(8,128)S(1)}, f32[20,40,256]{2,1,0:T(8,128)S(1)},...) custom-call(f32[16,32,128]{2,1,0:T(8,128)S(1)} %copy-done, ...), custom_call_target="tpu_custom_call", output_to_operand_aliasing={{0}: (8, {}), {1}: (9, {}), {2}: (10, {}), {3}: (11, {}), {... | custom-call | tf_op jit(solution)/shard_map/pallas_call | solution.py:602
  42.7 18.2 %all_to_all.15.refs_1_ = f32[32,16,128]{2,1,0:T(8,128)S(1)} all-to-all(f32[32,16,128]{2,1,0:T(8,128)S(1)} %get-tuple-element.52), channel_id=1, replica_groups=mesh['gx'=4,'gy'=8,'gz'=8] {'gx','gz'}, dimensions={0} | all-to-all | bytes 524288 | tf_op jit(solution)/shard_map/all_to_all | solution.py:618
  60.9 2.4 %collective-permute-start.7 = (f32[32,16,128]{2,1,0:T(8,128)S(1)}, f32[32,16,128]{2,1,0:T(8,128)S(1)}, u32[]{:S(2)}, u32[]{:S(2)}) collective-permute-start(f32[32,16,128]{2,1,0:T(8,128)S(1)} %all_to_all.15.refs_1_), channel_id=1, source_target_pairs={{0,56},{8,0},{16,8},{24,16},{32,24},{40,32},{48,40},{56,48},{1,57}... | collective-permute-start | bytes 786440 | tf_op jit(solution)/shard_map/ppermute | solution.py:614
  63.3 0.0 collective-permute-start.6
  63.3 3.4 %collective-permute-done.7.refs_2_ = f32[32,16,128]{2,1,0:T(8,128)S(1)} collective-permute-done((f32[32,16,128]{2,1,0:T(8,128)S(1)}, f32[32,16,128]{2,1,0:T(8,128)S(1)}, u32[]{:S(2)}, u32[]{:S(2)}) %collective-permute-start.7) | collective-permute-done | bytes 262176 | tf_op jit(solution)/shard_map/ppermute | solution.py:614
  66.7 0.0 collective-permute-done.6.refs_0_
  66.7 5.0 %shard_map.45 = (f32[28,24,256]{2,1,0:T(8,128)S(1)}, f32[16,32,128]{2,1,0:T(8,128)S(1)}, f32[16,32,128]{2,1,0:T(8,128)S(1)}, f32[15,32,128]{2,1,0:T(8,128)S(1)},...) custom-call(f32[32,16,128]{2,1,0:T(8,128)S(1)} %collective-permute-done.6.refs_0_, ...), custom_call_target="tpu_custom_call" | custom-call | tf_op jit(solution)/shard_map/pallas_call | solution.py:602
  71.7 0.8 collective-permute-start.8
  72.4 2.0 %collective-permute-start.9 = (f32[15,32,128]{2,1,0:T(8,128)S(1)}, f32[15,32,128]{2,1,0:T(8,128)S(1)}, u32[]{:S(2)}, u32[]{:S(2)}) collective-permute-start(f32[15,32,128]{2,1,0:T(8,128)S(1)} %get-tuple-element.63), channel_id=1, source_target_pairs={{0,192},{64,0},{128,64},{192,128},{1,193},{65,1},{129,65},{193,129... | collective-permute-start | bytes 737288 | tf_op jit(solution)/shard_map/ppermute | solution.py:614
  74.4 3.6 %collective-permute-done.8.xlo.refs_2_ = f32[15,32,128]{2,1,0:T(8,128)S(1)} collective-permute-done((f32[15,32,128]{2,1,0:T(8,128)S(1)}, f32[15,32,128]{2,1,0:T(8,128)S(1)}, u32[]{:S(2)}, u32[]{:S(2)}) %collective-permute-start.8) | collective-permute-done | bytes 245792 | tf_op jit(solution)/shard_map/ppermute | solution.py:614
  78.0 0.0 collective-permute-done.9.xhi.refs_3_
  78.0 0.1 shard_map.46
  78.0 5.5 %collective-permute-start.10 = (f32[75,8,128]{2,1,0:T(8,128)S(1)}, f32[75,8,128]{2,1,0:T(8,128)S(1)}, u32[]{:S(2)}, u32[]{:S(2)}) collective-permute-start(f32[75,8,128]{2,1,0:T(8,128)S(1)} %get-tuple-element.64), channel_id=1, source_target_pairs={{0,8},{8,16},{16,24},{24,32},{32,40},{40,48},{48,56},{56,0},{1,9},... | collective-permute-start | bytes 921608 | tf_op jit(solution)/shard_map/ppermute | solution.py:614
  83.5 1.1 collective-permute-start.11
  84.6 2.1 %shard_map.47 = (f32[40,56,256]{2,1,0:T(8,128)S(1)}, f32[40,56,256]{2,1,0:T(8,128)S(1)}, f32[20,40,256]{2,1,0:T(8,128)S(1)}, f32[20,40,256]{2,1,0:T(8,128)S(1)}, f32[1120,128]{1,0:T(8,128)S(1)}) custom-call(f32[16,32,128]{2,1,0:T(8,128)S(1)} %get-tuple-element.60.own.refs_0_.refs_12_.q, f32[4,32,128]{2,1,0:T(8,128)S(1)} %get-tuple-element.61.halo.refs_1_, ...), custom_call_target="tpu_custom_call" | custom-call | tf_op jit(solution)/shard_map/pallas_call | solution.py:602
  86.7 0.6 collective-permute-done.10.refs_4_
  87.3 2.8 %collective-permute-done.11.refs_5_ = f32[75,8,128]{2,1,0:T(8,128)S(1)} collective-permute-done((f32[75,8,128]{2,1,0:T(8,128)S(1)}, f32[75,8,128]{2,1,0:T(8,128)S(1)}, u32[]{:S(2)}, u32[]{:S(2)}) %collective-permute-start.11) | collective-permute-done | bytes 307232 | tf_op jit(solution)/shard_map/ppermute | solution.py:614
  90.1 2.6 %shard_map.48 = (f32[40,56,256]{2,1,0:T(8,128)S(1)}, f32[40,56,256]{2,1,0:T(8,128)S(1)}, f32[20,40,256]{2,1,0:T(8,128)S(1)}, f32[20,40,256]{2,1,0:T(8,128)S(1)},...) custom-call(f32[16,32,128]{2,1,0:T(8,128)S(1)} %get-tuple-element.60, ...), custom_call_target="tpu_custom_call", output_to_operand_aliasing={{0}: (6, {}), {1}: (7, {}), {2}: (8, {}), {3}: (9, {}), {4}... | custom-call | tf_op jit(solution)/shard_map/pallas_call | solution.py:602
  92.8 15.8 %all_to_all.16.refs_1_ = f32[32,8,128]{2,1,0:T(8,128)S(1)} all-to-all(f32[32,8,128]{2,1,0:T(8,128)S(1)} %get-tuple-element.71), channel_id=1, replica_groups=mesh['gx'=4,'gy'=8,'gz'=8] {'gx','gz'}, dimensions={0} | all-to-all | bytes 262144 | tf_op jit(solution)/shard_map/all_to_all | solution.py:618
  108.6 3.6 %collective-permute-start.13 = (f32[32,8,128]{2,1,0:T(8,128)S(1)}, f32[32,8,128]{2,1,0:T(8,128)S(1)}, u32[]{:S(2)}, u32[]{:S(2)}) collective-permute-start(f32[32,8,128]{2,1,0:T(8,128)S(1)} %all_to_all.16.refs_1_), channel_id=1, source_target_pairs={{0,56},{8,0},{16,8},{24,16},{32,24},{40,32},{48,40},{56,48},{1,57}... | collective-permute-start | bytes 393224 | tf_op jit(solution)/shard_map/ppermute | solution.py:614
  112.2 0.0 collective-permute-start.12
  112.2 1.0 collective-permute-done.13.refs_2_
  113.1 1.2 collective-permute-done.12.refs_0_
  114.4 4.3 %shard_map.49 = (f32[16,32,128]{2,1,0:T(8,128)S(1)}, f32[16,32,128]{2,1,0:T(8,128)S(1)}, f32[256,1,128]{2,1,0:T(1,128)S(1)}) custom-call(f32[32,8,128]{2,1,0:T(8,128)S(1)} %collective-permute-done.12.refs_0_, f32[32,8,128]{2,1,0:T(8,128)S(1)} %all_to_all.16.refs_1_, f32[32,8,128]{2,1,0:T(8,128)S(1)} %collective-permute-done.13.refs_2_, ...), custom_call_target="tpu_custom_call" | custom-call | tf_op jit(solution)/shard_map/pallas_call | solution.py:602
  118.7 22.6 %all_to_all.17.sums = f32[256,1,128]{2,1,0:T(1,128)S(1)} all-to-all(f32[256,1,128]{2,1,0:T(1,128)S(1)} %get-tuple-element.79), channel_id=1, replica_groups=mesh['gx'=4,'gy'=8,'gz'=8] {'gx','gy','gz'}, dimensions={0} | all-to-all | bytes 262144 | tf_op jit(solution)/shard_map/all_to_all | solution.py:689
  141.4 1.3 shard_map.50
  (2 shorter events, 0.1 us)
Async XLA Ops:
  0.6 13.0 %copy-start = (f32[16,32,128]{2,1,0:T(8,128)S(1)}, f32[16,32,128]{2,1,0:T(8,128)}, u32[]{:S(2)}) copy-start(f32[16,32,128]{2,1,0:T(8,128)} %r.1) | copy-start | bytes 786436
  0.6 13.0 %copy-start.1 = (f32[16,32,128]{2,1,0:T(8,128)S(1)}, f32[16,32,128]{2,1,0:T(8,128)}, u32[]{:S(2)}) copy-start(f32[16,32,128]{2,1,0:T(8,128)} %refs_1_.3) | copy-start | bytes 786436
  2.0 9.9 %collective-permute-start = (f32[2,12,32,128]{3,2,1,0:T(8,128)S(1)}, f32[2,12,32,128]{3,2,1,0:T(8,128)S(1)}, u32[]{:S(2)}, u32[]{:S(2)}) collective-permute-start(f32[2,12,32,128]{3,2,1,0:T(8,128)S(1)} %pad_maximum_fusion), channel_id=1, source_target_pairs={{0,64},{64,128},{128,192},{192,0},{1,65},{65,129},{129,193},{193,1... | collective-permute-start | bytes 1179656 | tf_op jit(solution)/shard_map/ppermute | solution.py:614
  4.2 9.5 %collective-permute-start.1 = (f32[2,12,32,128]{3,2,1,0:T(8,128)S(1)}, f32[2,12,32,128]{3,2,1,0:T(8,128)S(1)}, u32[]{:S(2)}, u32[]{:S(2)}) collective-permute-start(f32[2,12,32,128]{3,2,1,0:T(8,128)S(1)} %pad_maximum_fusion.1), channel_id=1, source_target_pairs={{0,192},{64,0},{128,64},{192,128},{1,193},{65,1},{129,65},{193,129... | collective-permute-start | bytes 1179656 | tf_op jit(solution)/shard_map/ppermute | solution.py:614
  14.3 11.1 %collective-permute-start.2 = (f32[2,8,32,128]{3,2,1,0:T(8,128)S(1)}, f32[2,8,32,128]{3,2,1,0:T(8,128)S(1)}, u32[]{:S(2)}, u32[]{:S(2)}) collective-permute-start(f32[2,8,32,128]{3,2,1,0:T(8,128)S(1)} %get-tuple-element.41), channel_id=1, source_target_pairs={{0,1},{1,2},{2,3},{3,4},{4,5},{5,6},{6,7},{7,0},{8,9},{9,10},{10,1... | collective-permute-start | bytes 786440 | tf_op jit(solution)/shard_map/ppermute | solution.py:614
  16.5 8.9 %collective-permute-start.3 = (f32[2,8,32,128]{3,2,1,0:T(8,128)S(1)}, f32[2,8,32,128]{3,2,1,0:T(8,128)S(1)}, u32[]{:S(2)}, u32[]{:S(2)}) collective-permute-start(f32[2,8,32,128]{3,2,1,0:T(8,128)S(1)} %get-tuple-element.42), channel_id=1, source_target_pairs={{0,7},{1,0},{2,1},{3,2},{4,3},{5,4},{6,5},{7,6},{8,15},{9,8},{10,9... | collective-permute-start | bytes 786440 | tf_op jit(solution)/shard_map/ppermute | solution.py:614
  25.5 11.4 %collective-permute-start.4 = (f32[168,8,128]{2,1,0:T(8,128)S(1)}, f32[168,8,128]{2,1,0:T(8,128)S(1)}, u32[]{:S(2)}, u32[]{:S(2)}) collective-permute-start(f32[168,8,128]{2,1,0:T(8,128)S(1)} %get-tuple-element.43), channel_id=1, source_target_pairs={{0,8},{8,16},{16,24},{24,32},{32,40},{40,48},{48,56},{56,0},{1,9},... | collective-permute-start | bytes 2064392 | tf_op jit(solution)/shard_map/ppermute | solution.py:614
  29.0 10.4 %collective-permute-start.5 = (f32[168,8,128]{2,1,0:T(8,128)S(1)}, f32[168,8,128]{2,1,0:T(8,128)S(1)}, u32[]{:S(2)}, u32[]{:S(2)}) collective-permute-start(f32[168,8,128]{2,1,0:T(8,128)S(1)} %get-tuple-element.44), channel_id=1, source_target_pairs={{0,56},{8,0},{16,8},{24,16},{32,24},{40,32},{48,40},{56,48},{1,57}... | collective-permute-start | bytes 2064392 | tf_op jit(solution)/shard_map/ppermute | solution.py:614
  60.9 5.8 %collective-permute-start.7 = (f32[32,16,128]{2,1,0:T(8,128)S(1)}, f32[32,16,128]{2,1,0:T(8,128)S(1)}, u32[]{:S(2)}, u32[]{:S(2)}) collective-permute-start(f32[32,16,128]{2,1,0:T(8,128)S(1)} %all_to_all.15.refs_1_), channel_id=1, source_target_pairs={{0,56},{8,0},{16,8},{24,16},{32,24},{40,32},{48,40},{56,48},{1,57}... | collective-permute-start | bytes 786440 | tf_op jit(solution)/shard_map/ppermute | solution.py:614
  63.3 3.4 %collective-permute-start.6 = (f32[32,16,128]{2,1,0:T(8,128)S(1)}, f32[32,16,128]{2,1,0:T(8,128)S(1)}, u32[]{:S(2)}, u32[]{:S(2)}) collective-permute-start(f32[32,16,128]{2,1,0:T(8,128)S(1)} %all_to_all.15.refs_1_), channel_id=1, source_target_pairs={{0,8},{8,16},{16,24},{24,32},{32,40},{40,48},{48,56},{56,0},{1,9},... | collective-permute-start | bytes 786440 | tf_op jit(solution)/shard_map/ppermute | solution.py:614
  71.7 6.3 %collective-permute-start.8 = (f32[15,32,128]{2,1,0:T(8,128)S(1)}, f32[15,32,128]{2,1,0:T(8,128)S(1)}, u32[]{:S(2)}, u32[]{:S(2)}) collective-permute-start(f32[15,32,128]{2,1,0:T(8,128)S(1)} %get-tuple-element.62), channel_id=1, source_target_pairs={{0,64},{64,128},{128,192},{192,0},{1,65},{65,129},{129,193},{193,1... | collective-permute-start | bytes 737288 | tf_op jit(solution)/shard_map/ppermute | solution.py:614
  72.4 5.5 %collective-permute-start.9 = (f32[15,32,128]{2,1,0:T(8,128)S(1)}, f32[15,32,128]{2,1,0:T(8,128)S(1)}, u32[]{:S(2)}, u32[]{:S(2)}) collective-permute-start(f32[15,32,128]{2,1,0:T(8,128)S(1)} %get-tuple-element.63), channel_id=1, source_target_pairs={{0,192},{64,0},{128,64},{192,128},{1,193},{65,1},{129,65},{193,129... | collective-permute-start | bytes 737288 | tf_op jit(solution)/shard_map/ppermute | solution.py:614
  78.0 9.3 %collective-permute-start.10 = (f32[75,8,128]{2,1,0:T(8,128)S(1)}, f32[75,8,128]{2,1,0:T(8,128)S(1)}, u32[]{:S(2)}, u32[]{:S(2)}) collective-permute-start(f32[75,8,128]{2,1,0:T(8,128)S(1)} %get-tuple-element.64), channel_id=1, source_target_pairs={{0,8},{8,16},{16,24},{24,32},{32,40},{40,48},{48,56},{56,0},{1,9},... | collective-permute-start | bytes 921608 | tf_op jit(solution)/shard_map/ppermute | solution.py:614
  83.5 6.6 %collective-permute-start.11 = (f32[75,8,128]{2,1,0:T(8,128)S(1)}, f32[75,8,128]{2,1,0:T(8,128)S(1)}, u32[]{:S(2)}, u32[]{:S(2)}) collective-permute-start(f32[75,8,128]{2,1,0:T(8,128)S(1)} %get-tuple-element.65), channel_id=1, source_target_pairs={{0,56},{8,0},{16,8},{24,16},{32,24},{40,32},{48,40},{56,48},{1,57}... | collective-permute-start | bytes 921608 | tf_op jit(solution)/shard_map/ppermute | solution.py:614
  108.6 4.6 %collective-permute-start.13 = (f32[32,8,128]{2,1,0:T(8,128)S(1)}, f32[32,8,128]{2,1,0:T(8,128)S(1)}, u32[]{:S(2)}, u32[]{:S(2)}) collective-permute-start(f32[32,8,128]{2,1,0:T(8,128)S(1)} %all_to_all.16.refs_1_), channel_id=1, source_target_pairs={{0,56},{8,0},{16,8},{24,16},{32,24},{40,32},{48,40},{56,48},{1,57}... | collective-permute-start | bytes 393224 | tf_op jit(solution)/shard_map/ppermute | solution.py:614
  112.2 2.2 %collective-permute-start.12 = (f32[32,8,128]{2,1,0:T(8,128)S(1)}, f32[32,8,128]{2,1,0:T(8,128)S(1)}, u32[]{:S(2)}, u32[]{:S(2)}) collective-permute-start(f32[32,8,128]{2,1,0:T(8,128)S(1)} %all_to_all.16.refs_1_), channel_id=1, source_target_pairs={{0,8},{8,16},{16,24},{24,32},{32,40},{40,48},{48,56},{56,0},{1,9},... | collective-permute-start | bytes 393224 | tf_op jit(solution)/shard_map/ppermute | solution.py:614

commit v7 on v6

--- a/solution.py
+++ b/solution.py
@@ -108,21 +108,36 @@
     return src[base + plane // 2, at : at + 4]
 
 
+def z_place(p):
+    if HX <= p < HX + BX:
+        return (p - HX) // 5, (p - HX) % 5
+    other = p if p < HX else p - BX
+    return 4 + other // 5, other % 5
+
+
+def z_tile(halves, t):
+    return (halves[0], t) if t < 4 else (halves[1], t - 4)
+
+
 def first_parts(a, own, xlo, xhi, zl, zr, ylo, yhi):
-    base = a * 84
+    base = a * 87
+
+    def load(halves, t):
+        ref, at = z_tile(halves, t)
+        return ref[a, at]
 
     def parts(p):
-        g, k = p // 5, p % 5
+        g, k = z_place(p)
 
         def pair(center, left, right):
             lane = lax.broadcasted_iota(jnp.int32, left.shape, 1)
             return center, jnp.where(lane < 64, turn(right, -24 * k), turn(left, 104 - 24 * k))
 
-        whole = lambda y: pair(y[base + p], y[base + 40 + g], y[base + 48 + g])
-        half = lambda y: pair(*(half_tile(y, base + 56, m) for m in (p, 40 + g, 48 + g)))
+        whole = lambda y: pair(y[base + p], y[base + 40 + g], y[base + 49 + g])
+        half = lambda y: pair(*(half_tile(y, base + 58, m) for m in (p, 40 + g, 49 + g)))
         center = x_plane(lambda i: own[i], lambda i: xlo[a, i], lambda i: xhi[a, i], p)
         if ylo is None:
-            return [((12, 44), None, pair(center, zl[a, g], zr[a, g]))]
+            return [((12, 44), None, pair(center, load(zl, g), load(zr, g)))]
         return list(zip(ROWS, SIDES, (whole(ylo), half(ylo), half(yhi), whole(yhi))))
 
     return parts
@@ -170,20 +185,28 @@
             dst[p, lo:hi, BZ:] = halo + 27.0
 
 
-def z_pack_kernel(right_side, diagonal, xlo, xhi, down, up):
+def z_pack(planes, a, down, up):
     group = lax.broadcasted_iota(jnp.int32, (BY, BZ), 1) // 24
+    for at in range(0, len(planes), 5):
+        low = high = None
+        for k, plane in enumerate(planes[at : at + 5]):
+            src = plane()
+            first, last = turn(src, 24 * k), turn(src, 24 * k - 104)
+            low = first if k == 0 else jnp.where(group == k, first, low)
+            high = last if k == 0 else jnp.where(group == k, last, high)
+        down[a, at // 5] = low
+        up[a, at // 5] = high
+
+
+def z_pack_own_kernel(right_side, diagonal, down, up):
     for a, own in enumerate((right_side, diagonal)):
-        for g in range(EX // 5):
-            low = high = None
-            for k in range(5):
-                src = x_plane(
-                    lambda i: own[i], lambda i: xlo[a, i], lambda i: xhi[a, i], 5 * g + k
-                )
-                first, last = turn(src, 24 * k), turn(src, 24 * k - 104)
-                low = first if k == 0 else jnp.where(group == k, first, low)
-                high = last if k == 0 else jnp.where(group == k, last, high)
-            down[a, g] = low
-            up[a, g] = high
+        z_pack([lambda i=i, own=own: own[i] for i in range(BX)], a, down, up)
+
+
+def z_pack_halo_kernel(xlo, xhi, down, up):
+    for a in range(2):
+        planes = [lambda i=i, x=x, a=a: x[a, i] for x in (xlo, xhi) for i in range(HX)]
+        z_pack(planes, a, down, up)
 
 
 def y_rows(planes, base, down, up):
@@ -197,7 +220,9 @@
         up[at, row : row + 4] = plane(28, 32)
 
 
-def y_pack_kernel(right_side, diagonal, xlo, xhi, zl, zr, down, up):
+def y_pack_kernel(right_side, diagonal, xlo, xhi, *refs):
+    zl, zr, (down, up) = refs[0:2], refs[2:4], refs[4:]
+
     def rows(ref, *index):
         return lambda lo, hi: ref[(*index, slice(lo, hi))]
 
@@ -208,8 +233,11 @@
             )
             for p in range(EX)
         ]
-        planes += [rows(zl, a, g) for g in range(8)] + [rows(zr, a, g) for g in range(8)]
-        y_rows(planes, 84 * a, down, up)
+        for halves in (zl, zr):
+            for t in range(9):
+                ref, at = z_tile(halves, t)
+                planes.append(rows(ref, a, at))
+        y_rows(planes, 87 * a, down, up)
 
 
 def y_pack_later_kernel(own, halo, xlo, xhi, down, up):
@@ -261,8 +289,9 @@
 
 def early_kernel(first, *refs):
     if first:
-        right_side, diagonal, xlo, xhi, zl, zr = refs[:6]
-        field, zfull, zs, rs, rows, d0, d_rows, pairs = refs[6:]
+        right_side, diagonal, xlo, xhi = refs[:4]
+        zl, zr = refs[4:6], refs[6:8]
+        field, zfull, zs, rs, rows, d0, d_rows, pairs = refs[8:]
         assemble_field(field, first_parts(0, right_side, xlo, xhi, zl, zr, None, None))
         assemble_diagonal(d0, first_parts(1, diagonal, xlo, xhi, zl, zr, None, None))
         for i in range(MX):
@@ -297,9 +326,10 @@
 
 def pre_kernel(first, *refs):
     if first:
-        right_side, diagonal, xlo, xhi, zl, zr, ylo, yhi = refs[:8]
-        field, zfull, zs, rs, rows, d0, d_rows, d1 = refs[15:23]
-        z1, left1, packed, pairs, r1, small = refs[23:]
+        right_side, diagonal, xlo, xhi = refs[:4]
+        zl, zr, (ylo, yhi) = refs[4:6], refs[6:8], refs[8:10]
+        field, zfull, zs, rs, rows, d0, d_rows, d1 = refs[17:25]
+        z1, left1, packed, pairs, r1, small = refs[25:]
         assemble_field(field, first_parts(0, right_side, xlo, xhi, zl, zr, ylo, yhi))
         assemble_diagonal(d0, first_parts(1, diagonal, xlo, xhi, zl, zr, ylo, yhi))
         for i in range(MX):
@@ -394,15 +424,19 @@
         packed[i] = tile
 
 
-def unpack(dst, row, lo, own, hi, scales):
+def unpack(dst, row, mate, own, across, scales):
+    odd = places()[1] % 2 == 1
+    pick_low = lambda at: jnp.where(odd, mate[at], across[at])
+    pick_own = lambda at: own[at]
+    pick_high = lambda at: jnp.where(odd, across[at], mate[at])
     group = lax.broadcasted_iota(jnp.int32, (8, 128), 1) // 32
-    for part, (src, scale) in enumerate(zip((lo, own, hi), scales)):
+    for part, (src, scale) in enumerate(zip((pick_low, pick_own, pick_high), scales)):
         for bx in range(GX):
             for k in range(4):
                 for h in range(2):
                     acc = None
                     for j in range(4):
-                        block = src[bx * GZ + 4 * h + j, row : row + 8, :]
+                        block = src((bx * GZ + 4 * h + j, slice(row, row + 8)))
                         here = group == (j + k) % 4
                         acc = block if acc is None else jnp.where(here, block, acc)
                     acc = turn(acc, -32 * k)
@@ -413,7 +447,7 @@
         dst[p] = jnp.zeros((24, 256), F32)
 
 
-def coarse(r2, d2, s0, s1, z2):
+def coarse(first, r2, d2, den, s0, s1, z2):
     gx, gy, _ = places()
     shape = (24, 256)
     row = lax.broadcasted_iota(jnp.int32, shape, 0) + (gy * 8 - 8)
@@ -453,23 +487,26 @@
         y, d = z2[i], at(d2, i)
         left = at(r2, i) - d * y + box(z2[i - 1] + y + z2[i + 1])
         top = jnp.sum(left, axis=1, keepdims=True)
-        bottom = jnp.sum(d - 26.0, axis=1, keepdims=True)
-        s0[i] = inside(i) * (y + top / bottom)
+        if first:
+            bottom = jnp.sum(d - 26.0, axis=1, keepdims=True)
+            den[i - 4] = jnp.broadcast_to(bottom, (24, 128))
+        shift_line = jnp.broadcast_to(top, (24, 128)) / den[i - 4]
+        s0[i] = inside(i) * (y + jnp.concatenate([shift_line, shift_line], axis=1))
 
 
 def post_kernel(first, *refs):
     lo, own, hi, zs, rs, z1, left1, d0, d1 = refs[:9]
     if first:
-        d2, z_core, q_core, q_down, q_up, q_halo = refs[9:15]
+        d2, den, z_core, q_core, q_down, q_up, q_halo = refs[9:16]
     else:
-        d2, r_old, z_old, q_old, z_core, q_core, dots = refs[9:16]
+        d2, den, r_old, z_old, q_old, z_core, q_core, dots = refs[9:17]
     r2, s0, s1, z2, wide, rows1, u, rem, zf1, rowsv, v, sv, rem0, zf0 = refs[-14:]
     gx, gy, gz = places()
     scales = (flag(gy > 0), None, flag(gy < GY - 1))
     unpack(r2, 0, lo, own, hi, scales)
     if first:
         unpack(d2, 8, lo, own, hi, (None, None, None))
-    coarse(r2, d2, s0, s1, z2)
+    coarse(first, r2, d2, den, s0, s1, z2)
 
     lane = lax.broadcasted_iota(jnp.int32, (16, 128), 1)
     z = jnp.where(lane < 48, lane, lane - 64) + 32 * gz
@@ -616,7 +653,9 @@
 
 def spread_coarse(packed):
     own = lax.all_to_all(packed, ("gx", "gz"), 0, 0)
-    return shift(own, "gy", GY, 1), own, shift(own, "gy", GY, -1)
+    mate = lax.ppermute(own, "gy", [(i, i ^ 1) for i in range(GY)])
+    across = lax.ppermute(own, "gy", [(i, (i + 2 * (i % 2) - 1) % GY) for i in range(GY)])
+    return mate, own, across
 
 
 def early_call(first, *args):
@@ -647,7 +686,7 @@
     kernel = functools.partial(post_kernel, first)
     if first:
         slab = shape(15, BY, BZ)
-        outs = (shape(28, 24, 256), core, core, slab, slab, shape(4, BY, BZ))
+        outs = (shape(28, 24, 256), shape(8, 24, 128), core, core, slab, slab, shape(4, BY, BZ))
         return call(kernel, outs, scratch, *parts, *kept, d0, d1)
     outs = (core, core, shape(GX * GY * GZ, 1, 128))
     return call(kernel, outs, scratch, *parts, *kept, d0, d1, *old)
@@ -659,12 +698,15 @@
 
     xlo = shift(slab(BX - HX, BX), "gx", GX, 1)
     xhi = shift(slab(0, HX), "gx", GX, -1)
-    edge = shape(2, EX // 5, BY, BZ)
-    down, up = call(z_pack_kernel, (edge, edge), [], right_side, diagonal, xlo, xhi)
-    zl = shift(up, "gz", GZ, 1)
-    zr = shift(down, "gz", GZ, -1)
-    edge = shape(168, 8, BZ)
-    pieces = (right_side, diagonal, xlo, xhi, zl, zr)
+    edge = shape(2, 4, BY, BZ)
+    down, up = call(z_pack_own_kernel, (edge, edge), [], right_side, diagonal)
+    zl, zr = shift(up, "gz", GZ, 1), shift(down, "gz", GZ, -1)
+    edge = shape(2, 5, BY, BZ)
+    xlo, xhi, zl, zr = lax.optimization_barrier((xlo, xhi, zl, zr))
+    down, up = call(z_pack_halo_kernel, (edge, edge), [], xlo, xhi)
+    zl, zr = (zl, shift(up, "gz", GZ, 1)), (zr, shift(down, "gz", GZ, -1))
+    edge = shape(174, 8, BZ)
+    pieces = (right_side, diagonal, xlo, xhi, *zl, *zr)
     down, up = call(y_pack_kernel, (edge, edge), [], *pieces)
     early = early_call(True, *pieces)
     return (*pieces, shift(up, "gy", GY, 1), shift(down, "gy", GY, -1)), early
@@ -681,10 +723,10 @@
 
 def local(right_side, diagonal):
     d0, d1, *kept = pre_call(True, *first_exchange(right_side, diagonal))
-    d2, z, q, *edges = post_call(spread_coarse(kept[-1]), kept[:-1], d0, d1)
+    d2, den, z, q, *edges = post_call(spread_coarse(kept[-1]), kept[:-1], d0, d1)
     kept = pre_call(False, *later_exchange(d0, q, *edges), (d0, d1))
     p, w, dots = post_call(
-        spread_coarse(kept[-1]), kept[:-1], d0, d1, d2, right_side, z, q
+        spread_coarse(kept[-1]), kept[:-1], d0, d1, d2, den, right_side, z, q
     )
     sums = lax.all_to_all(dots, ("gx", "gy", "gz"), 0, 0)
     core = shape(BX, BY, BZ)

time: 143 us -> 140 us (0.979)
  waiting for transfers between devices: 33.3 us -> 23.6 us
  starting transfers between devices: 28.5 us -> 35.3 us
    ppermute x14 -> x12, waiting for transfers between devices: 33.3 us -> 21 us  [shift(): lax.ppermute(value, axis, [(i, (i + by) % count) for i in range(count)])]
    ppermute x0 -> x4, starting transfers between devices: none -> 8.44 us  [the longest x2 5.61 us: spread_coarse(): mate = lax.ppermute(own, 'gy', [(i, i ^ 1) for i in range(GY)])]
    ppermute x0 -> x4, waiting for transfers between devices: none -> 2.6 us  [the longest x2 1.75 us: spread_coarse(): lax.ppermute(own, 'gy', [(i, (i + 2 * (i % 2) - 1) % GY) for i in range(G...]
    ppermute x14 -> x12, starting transfers between devices: 28.5 us -> 26.9 us  [shift(): lax.ppermute(value, axis, [(i, (i + by) % count) for i in range(count)])]
    pallas_call x10 -> x11, Pallas kernels: 22.1 us -> 22.2 us  [call(): pl.pallas_call(kernel, out_shape=outs, in_specs=[whole] * len(args), out_...]
  transfers between devices with their start and end apart: 14 -> 16, of which waited for: 11 -> 10; matrix products, arithmetic and copies ran while one was open for 0% -> 0% of each run, Pallas kernels for 3% -> 4%
where the time goes in v7:
time: 140 us
  blocking collectives  56.5 us (40%)
  starting transfers between devices  35.3 us (25%)
  waiting for transfers between devices  23.6 us (17%)
  Pallas kernels  22.2 us (16%)
    all_to_all x2, blocking collectives, spread_coarse(): own = lax.all_to_all(packed, ('gx', 'gz'), 0, 0)  34.9 us
    ppermute x12, starting transfers between devices, shift(): lax.ppermute(value, axis, [(i, (i + by) % count) for i in range(count)])  26.9 us
    pallas_call x11, Pallas kernels, call(): pl.pallas_call(kernel, out_shape=outs, in_specs=[whole] * len(args), out_...  22.2 us
    all_to_all x1, blocking collectives, local(): sums = lax.all_to_all(dots, ('gx', 'gy', 'gz'), 0, 0)  21.6 us
    ppermute x12, waiting for transfers between devices, shift(): lax.ppermute(value, axis, [(i, (i + by) % count) for i in range(count)])  21 us
    ppermute x2, starting transfers between devices, spread_coarse(): mate = lax.ppermute(own, 'gy', [(i, i ^ 1) for i in range(GY)])  5.61 us
    ppermute x2, starting transfers between devices, spread_coarse(): lax.ppermute(own, 'gy', [(i, (i + 2 * (i % 2) - 1) % GY) for i in range(G...  2.83 us
  transfers between devices with their start and end apart: 16, of which 10 were waited for; matrix products, arithmetic and copies ran while one was open for 0% of the time, Pallas kernels for 4%

profile of v7, /device:TPU:1, one launch (start us, length us, event | category | flops | bytes accessed | tf_op | source)
XLA Modules:
  0.0 139.8 jit_solution(10668866181050314880)
XLA Ops:
  0.6 0.0 copy-start
  0.6 1.3 slice_bitcast_fusion
  2.0 2.1 %collective-permute-start = (f32[2,12,32,128]{3,2,1,0:T(8,128)S(1)}, f32[2,12,32,128]{3,2,1,0:T(8,128)S(1)}, u32[]{:S(2)}, u32[]{:S(2)}) collective-permute-start(f32[2,12,32,128]{3,2,1,0:T(8,128)S(1)} %pad_maximum_fusion), channel_id=1, source_target_pairs={{0,64},{64,128},{128,192},{192,0},{1,65},{65,129},{129,193},{193,1... | collective-permute-start | bytes 1179656 | tf_op jit(solution)/shard_map/ppermute | solution.py:651
  4.2 1.4 collective-permute-start.1
  5.5 0.3 shard_map.41
  5.8 1.9 %collective-permute-start.2 = (f32[2,4,32,128]{3,2,1,0:T(8,128)S(1)}, f32[2,4,32,128]{3,2,1,0:T(8,128)S(1)}, u32[]{:S(2)}, u32[]{:S(2)}) collective-permute-start(f32[2,4,32,128]{3,2,1,0:T(8,128)S(1)} %get-tuple-element.48), channel_id=1, source_target_pairs={{0,1},{1,2},{2,3},{3,4},{4,5},{5,6},{6,7},{7,0},{8,9},{9,10},{10,1... | collective-permute-start | bytes 393224 | tf_op jit(solution)/shard_map/ppermute | solution.py:651
  7.7 4.0 %collective-permute-start.3 = (f32[2,4,32,128]{3,2,1,0:T(8,128)S(1)}, f32[2,4,32,128]{3,2,1,0:T(8,128)S(1)}, u32[]{:S(2)}, u32[]{:S(2)}) collective-permute-start(f32[2,4,32,128]{3,2,1,0:T(8,128)S(1)} %get-tuple-element.49), channel_id=1, source_target_pairs={{0,7},{1,0},{2,1},{3,2},{4,3},{5,4},{6,5},{7,6},{8,15},{9,8},{10,9... | collective-permute-start | bytes 393224 | tf_op jit(solution)/shard_map/ppermute | solution.py:651
  11.7 2.6 %collective-permute-done.2.refs_0_.refs_4_ = f32[2,4,32,128]{3,2,1,0:T(8,128)S(1)} collective-permute-done((f32[2,4,32,128]{3,2,1,0:T(8,128)S(1)}, f32[2,4,32,128]{3,2,1,0:T(8,128)S(1)}, u32[]{:S(2)}, u32[]{:S(2)}) %collective-permute-start.2) | collective-permute-done | bytes 131104 | tf_op jit(solution)/shard_map/ppermute | solution.py:651
  14.3 0.0 collective-permute-done.3.refs_2_.refs_6_
  14.3 0.0 collective-permute-done.xlo.refs_2_
  14.3 0.0 collective-permute-done.1.xhi.refs_3_
  14.3 0.4 shard_map.42
  14.8 1.5 %collective-permute-start.4 = (f32[2,5,32,128]{3,2,1,0:T(8,128)S(1)}, f32[2,5,32,128]{3,2,1,0:T(8,128)S(1)}, u32[]{:S(2)}, u32[]{:S(2)}) collective-permute-start(f32[2,5,32,128]{3,2,1,0:T(8,128)S(1)} %get-tuple-element.53), channel_id=1, source_target_pairs={{0,1},{1,2},{2,3},{3,4},{4,5},{5,6},{6,7},{7,0},{8,9},{9,10},{10,1... | collective-permute-start | bytes 491528 | tf_op jit(solution)/shard_map/ppermute | solution.py:651
  16.3 4.0 %collective-permute-start.5 = (f32[2,5,32,128]{3,2,1,0:T(8,128)S(1)}, f32[2,5,32,128]{3,2,1,0:T(8,128)S(1)}, u32[]{:S(2)}, u32[]{:S(2)}) collective-permute-start(f32[2,5,32,128]{3,2,1,0:T(8,128)S(1)} %get-tuple-element.55), channel_id=1, source_target_pairs={{0,7},{1,0},{2,1},{3,2},{4,3},{5,4},{6,5},{7,6},{8,15},{9,8},{10,9... | collective-permute-start | bytes 491528 | tf_op jit(solution)/shard_map/ppermute | solution.py:651
  20.3 2.6 %collective-permute-done.4.refs_1_.refs_5_ = f32[2,5,32,128]{3,2,1,0:T(8,128)S(1)} collective-permute-done((f32[2,5,32,128]{3,2,1,0:T(8,128)S(1)}, f32[2,5,32,128]{3,2,1,0:T(8,128)S(1)}, u32[]{:S(2)}, u32[]{:S(2)}) %collective-permute-start.4) | collective-permute-done | bytes 163872 | tf_op jit(solution)/shard_map/ppermute | solution.py:651
  22.9 0.0 collective-permute-done.5.refs_3_.refs_7_
  22.9 0.1 shard_map.43
  23.0 3.7 %collective-permute-start.6 = (f32[174,8,128]{2,1,0:T(8,128)S(1)}, f32[174,8,128]{2,1,0:T(8,128)S(1)}, u32[]{:S(2)}, u32[]{:S(2)}) collective-permute-start(f32[174,8,128]{2,1,0:T(8,128)S(1)} %get-tuple-element.56), channel_id=1, source_target_pairs={{0,8},{8,16},{16,24},{24,32},{32,40},{40,48},{48,56},{56,0},{1,9},... | collective-permute-start | bytes 2138120 | tf_op jit(solution)/shard_map/ppermute | solution.py:651
  26.7 0.0 collective-permute-start.7
  26.8 2.7 %shard_map.44 = (f32[40,56,256]{2,1,0:T(8,128)S(1)}, f32[40,56,256]{2,1,0:T(8,128)S(1)}, f32[20,40,256]{2,1,0:T(8,128)S(1)}, f32[20,40,256]{2,1,0:T(8,128)S(1)},...) custom-call(f32[16,32,128]{2,1,0:T(8,128)S(1)} %copy-done, ...), custom_call_target="tpu_custom_call" | custom-call | tf_op jit(solution)/shard_map/pallas_call | solution.py:639
  29.5 5.4 %collective-permute-done.6.refs_8_ = f32[174,8,128]{2,1,0:T(8,128)S(1)} collective-permute-done((f32[174,8,128]{2,1,0:T(8,128)S(1)}, f32[174,8,128]{2,1,0:T(8,128)S(1)}, u32[]{:S(2)}, u32[]{:S(2)}) %collective-permute-start.6) | collective-permute-done | bytes 712736 | tf_op jit(solution)/shard_map/ppermute | solution.py:651
  34.9 2.5 %collective-permute-done.7.refs_9_ = f32[174,8,128]{2,1,0:T(8,128)S(1)} collective-permute-done((f32[174,8,128]{2,1,0:T(8,128)S(1)}, f32[174,8,128]{2,1,0:T(8,128)S(1)}, u32[]{:S(2)}, u32[]{:S(2)}) %collective-permute-start.7) | collective-permute-done | bytes 712736 | tf_op jit(solution)/shard_map/ppermute | solution.py:651
  37.4 3.3 %shard_map.45 = (f32[40,56,256]{2,1,0:T(8,128)S(1)}, f32[40,56,256]{2,1,0:T(8,128)S(1)}, f32[20,40,256]{2,1,0:T(8,128)S(1)}, f32[20,40,256]{2,1,0:T(8,128)S(1)},...) custom-call(f32[16,32,128]{2,1,0:T(8,128)S(1)} %copy-done, ...), custom_call_target="tpu_custom_call", output_to_operand_aliasing={{0}: (10, {}), {1}: (11, {}), {2}: (12, {}), {3}: (13, {}),... | custom-call | tf_op jit(solution)/shard_map/pallas_call | solution.py:639
  40.7 19.0 %all_to_all.15.refs_1_ = f32[32,16,128]{2,1,0:T(8,128)S(1)} all-to-all(f32[32,16,128]{2,1,0:T(8,128)S(1)} %get-tuple-element.65), channel_id=1, replica_groups=mesh['gx'=4,'gy'=8,'gz'=8] {'gx','gz'}, dimensions={0} | all-to-all | bytes 524288 | tf_op jit(solution)/shard_map/all_to_all | solution.py:655
  59.7 1.7 %collective-permute-start.9 = (f32[32,16,128]{2,1,0:T(8,128)S(1)}, f32[32,16,128]{2,1,0:T(8,128)S(1)}, u32[]{:S(2)}, u32[]{:S(2)}) collective-permute-start(f32[32,16,128]{2,1,0:T(8,128)S(1)} %all_to_all.15.refs_1_), channel_id=1, source_target_pairs={{0,56},{8,16},{16,8},{24,32},{32,24},{40,48},{48,40},{56,0},{1,57}... | collective-permute-start | bytes 786440 | tf_op jit(solution)/shard_map/ppermute | solution.py:657
  61.4 2.5 %collective-permute-start.8 = (f32[32,16,128]{2,1,0:T(8,128)S(1)}, f32[32,16,128]{2,1,0:T(8,128)S(1)}, u32[]{:S(2)}, u32[]{:S(2)}) collective-permute-start(f32[32,16,128]{2,1,0:T(8,128)S(1)} %all_to_all.15.refs_1_), channel_id=1, source_target_pairs={{0,8},{8,0},{16,24},{24,16},{32,40},{40,32},{48,56},{56,48},{1,9},... | collective-permute-start | bytes 786440 | tf_op jit(solution)/shard_map/ppermute | solution.py:656
  63.8 1.6 %collective-permute-done.9.refs_2_ = f32[32,16,128]{2,1,0:T(8,128)S(1)} collective-permute-done((f32[32,16,128]{2,1,0:T(8,128)S(1)}, f32[32,16,128]{2,1,0:T(8,128)S(1)}, u32[]{:S(2)}, u32[]{:S(2)}) %collective-permute-start.9) | collective-permute-done | bytes 262176 | tf_op jit(solution)/shard_map/ppermute | solution.py:657
  65.5 0.0 collective-permute-done.8.refs_0_
  65.5 5.0 %shard_map.46 = (f32[28,24,256]{2,1,0:T(8,128)S(1)}, f32[8,24,128]{2,1,0:T(8,128)S(1)}, f32[16,32,128]{2,1,0:T(8,128)S(1)}, f32[16,32,128]{2,1,0:T(8,128)S(1)}, ...) custom-call(f32[32,16,128]{2,1,0:T(8,128)S(1)} %collective-permute-done.8.refs_0_, ...), custom_call_target="tpu_custom_call" | custom-call | tf_op jit(solution)/shard_map/pallas_call | solution.py:639
  70.5 0.5 collective-permute-start.10
  71.0 2.3 %collective-permute-start.11 = (f32[15,32,128]{2,1,0:T(8,128)S(1)}, f32[15,32,128]{2,1,0:T(8,128)S(1)}, u32[]{:S(2)}, u32[]{:S(2)}) collective-permute-start(f32[15,32,128]{2,1,0:T(8,128)S(1)} %get-tuple-element.76), channel_id=1, source_target_pairs={{0,192},{64,0},{128,64},{192,128},{1,193},{65,1},{129,65},{193,129... | collective-permute-start | bytes 737288 | tf_op jit(solution)/shard_map/ppermute | solution.py:651
  73.2 3.6 %collective-permute-done.10.xlo.refs_2_ = f32[15,32,128]{2,1,0:T(8,128)S(1)} collective-permute-done((f32[15,32,128]{2,1,0:T(8,128)S(1)}, f32[15,32,128]{2,1,0:T(8,128)S(1)}, u32[]{:S(2)}, u32[]{:S(2)}) %collective-permute-start.10) | collective-permute-done | bytes 245792 | tf_op jit(solution)/shard_map/ppermute | solution.py:651
  76.8 0.0 collective-permute-done.11.xhi.refs_3_
  76.8 0.1 shard_map.47
  76.9 5.5 %collective-permute-start.12 = (f32[75,8,128]{2,1,0:T(8,128)S(1)}, f32[75,8,128]{2,1,0:T(8,128)S(1)}, u32[]{:S(2)}, u32[]{:S(2)}) collective-permute-start(f32[75,8,128]{2,1,0:T(8,128)S(1)} %get-tuple-element.77), channel_id=1, source_target_pairs={{0,8},{8,16},{16,24},{24,32},{32,40},{40,48},{48,56},{56,0},{1,9},... | collective-permute-start | bytes 921608 | tf_op jit(solution)/shard_map/ppermute | solution.py:651
  82.3 0.0 collective-permute-start.13
  82.3 2.1 %shard_map.48 = (f32[40,56,256]{2,1,0:T(8,128)S(1)}, f32[40,56,256]{2,1,0:T(8,128)S(1)}, f32[20,40,256]{2,1,0:T(8,128)S(1)}, f32[20,40,256]{2,1,0:T(8,128)S(1)}, f32[1120,128]{1,0:T(8,128)S(1)}) custom-call(f32[16,32,128]{2,1,0:T(8,128)S(1)} %get-tuple-element.73.own.refs_0_.refs_13_.q, f32[4,32,128]{2,1,0:T(8,128)S(1)} %get-tuple-element.74.halo.refs_1_, ...), custom_call_target="tpu_custom_call" | custom-call | tf_op jit(solution)/shard_map/pallas_call | solution.py:639
  84.5 1.7 %collective-permute-done.12.refs_4_ = f32[75,8,128]{2,1,0:T(8,128)S(1)} collective-permute-done((f32[75,8,128]{2,1,0:T(8,128)S(1)}, f32[75,8,128]{2,1,0:T(8,128)S(1)}, u32[]{:S(2)}, u32[]{:S(2)}) %collective-permute-start.12) | collective-permute-done | bytes 307232 | tf_op jit(solution)/shard_map/ppermute | solution.py:651
  86.1 2.6 %collective-permute-done.13.refs_5_ = f32[75,8,128]{2,1,0:T(8,128)S(1)} collective-permute-done((f32[75,8,128]{2,1,0:T(8,128)S(1)}, f32[75,8,128]{2,1,0:T(8,128)S(1)}, u32[]{:S(2)}, u32[]{:S(2)}) %collective-permute-start.13) | collective-permute-done | bytes 307232 | tf_op jit(solution)/shard_map/ppermute | solution.py:651
  88.8 2.6 %shard_map.49 = (f32[40,56,256]{2,1,0:T(8,128)S(1)}, f32[40,56,256]{2,1,0:T(8,128)S(1)}, f32[20,40,256]{2,1,0:T(8,128)S(1)}, f32[20,40,256]{2,1,0:T(8,128)S(1)},...) custom-call(f32[16,32,128]{2,1,0:T(8,128)S(1)} %get-tuple-element.73, ...), custom_call_target="tpu_custom_call", output_to_operand_aliasing={{0}: (6, {}), {1}: (7, {}), {2}: (8, {}), {3}: (9, {}), {4}... | custom-call | tf_op jit(solution)/shard_map/pallas_call | solution.py:639
  91.4 15.9 %all_to_all.16.refs_1_ = f32[32,8,128]{2,1,0:T(8,128)S(1)} all-to-all(f32[32,8,128]{2,1,0:T(8,128)S(1)} %get-tuple-element.84), channel_id=1, replica_groups=mesh['gx'=4,'gy'=8,'gz'=8] {'gx','gz'}, dimensions={0} | all-to-all | bytes 262144 | tf_op jit(solution)/shard_map/all_to_all | solution.py:655
  107.3 1.1 collective-permute-start.15
  108.4 3.1 %collective-permute-start.14 = (f32[32,8,128]{2,1,0:T(8,128)S(1)}, f32[32,8,128]{2,1,0:T(8,128)S(1)}, u32[]{:S(2)}, u32[]{:S(2)}) collective-permute-start(f32[32,8,128]{2,1,0:T(8,128)S(1)} %all_to_all.16.refs_1_), channel_id=1, source_target_pairs={{0,8},{8,0},{16,24},{24,16},{32,40},{40,32},{48,56},{56,48},{1,9},... | collective-permute-start | bytes 393224 | tf_op jit(solution)/shard_map/ppermute | solution.py:656
  111.6 0.1 collective-permute-done.15.refs_2_
  111.7 0.9 collective-permute-done.14.refs_0_
  112.5 4.3 %shard_map.50 = (f32[16,32,128]{2,1,0:T(8,128)S(1)}, f32[16,32,128]{2,1,0:T(8,128)S(1)}, f32[256,1,128]{2,1,0:T(1,128)S(1)}) custom-call(f32[32,8,128]{2,1,0:T(8,128)S(1)} %collective-permute-done.14.refs_0_, f32[32,8,128]{2,1,0:T(8,128)S(1)} %all_to_all.16.refs_1_, f32[32,8,128]{2,1,0:T(8,128)S(1)} %collective-permute-done.15.refs_2_, ...), custom_call_target="tpu_custom_call" | custom-call | tf_op jit(solution)/shard_map/pallas_call | solution.py:639
  116.9 21.6 %all_to_all.17.sums = f32[256,1,128]{2,1,0:T(1,128)S(1)} all-to-all(f32[256,1,128]{2,1,0:T(1,128)S(1)} %get-tuple-element.93), channel_id=1, replica_groups=mesh['gx'=4,'gy'=8,'gz'=8] {'gx','gy','gz'}, dimensions={0} | all-to-all | bytes 262144 | tf_op jit(solution)/shard_map/all_to_all | solution.py:731
  138.5 1.3 shard_map.51
  (5 shorter events, 0.1 us)
Async XLA Ops:
  0.6 4.9 %copy-start = (f32[16,32,128]{2,1,0:T(8,128)S(1)}, f32[16,32,128]{2,1,0:T(8,128)}, u32[]{:S(2)}) copy-start(f32[16,32,128]{2,1,0:T(8,128)} %r.1) | copy-start | bytes 786436
  0.6 4.9 %copy-start.1 = (f32[16,32,128]{2,1,0:T(8,128)S(1)}, f32[16,32,128]{2,1,0:T(8,128)}, u32[]{:S(2)}) copy-start(f32[16,32,128]{2,1,0:T(8,128)} %refs_1_.3) | copy-start | bytes 786436
  2.0 12.3 %collective-permute-start = (f32[2,12,32,128]{3,2,1,0:T(8,128)S(1)}, f32[2,12,32,128]{3,2,1,0:T(8,128)S(1)}, u32[]{:S(2)}, u32[]{:S(2)}) collective-permute-start(f32[2,12,32,128]{3,2,1,0:T(8,128)S(1)} %pad_maximum_fusion), channel_id=1, source_target_pairs={{0,64},{64,128},{128,192},{192,0},{1,65},{65,129},{129,193},{193,1... | collective-permute-start | bytes 1179656 | tf_op jit(solution)/shard_map/ppermute | solution.py:651
  4.2 10.2 %collective-permute-start.1 = (f32[2,12,32,128]{3,2,1,0:T(8,128)S(1)}, f32[2,12,32,128]{3,2,1,0:T(8,128)S(1)}, u32[]{:S(2)}, u32[]{:S(2)}) collective-permute-start(f32[2,12,32,128]{3,2,1,0:T(8,128)S(1)} %pad_maximum_fusion.1), channel_id=1, source_target_pairs={{0,192},{64,0},{128,64},{192,128},{1,193},{65,1},{129,65},{193,129... | collective-permute-start | bytes 1179656 | tf_op jit(solution)/shard_map/ppermute | solution.py:651
  5.8 8.5 %collective-permute-start.2 = (f32[2,4,32,128]{3,2,1,0:T(8,128)S(1)}, f32[2,4,32,128]{3,2,1,0:T(8,128)S(1)}, u32[]{:S(2)}, u32[]{:S(2)}) collective-permute-start(f32[2,4,32,128]{3,2,1,0:T(8,128)S(1)} %get-tuple-element.48), channel_id=1, source_target_pairs={{0,1},{1,2},{2,3},{3,4},{4,5},{5,6},{6,7},{7,0},{8,9},{9,10},{10,1... | collective-permute-start | bytes 393224 | tf_op jit(solution)/shard_map/ppermute | solution.py:651
  7.7 6.6 %collective-permute-start.3 = (f32[2,4,32,128]{3,2,1,0:T(8,128)S(1)}, f32[2,4,32,128]{3,2,1,0:T(8,128)S(1)}, u32[]{:S(2)}, u32[]{:S(2)}) collective-permute-start(f32[2,4,32,128]{3,2,1,0:T(8,128)S(1)} %get-tuple-element.49), channel_id=1, source_target_pairs={{0,7},{1,0},{2,1},{3,2},{4,3},{5,4},{6,5},{7,6},{8,15},{9,8},{10,9... | collective-permute-start | bytes 393224 | tf_op jit(solution)/shard_map/ppermute | solution.py:651
  14.8 8.1 %collective-permute-start.4 = (f32[2,5,32,128]{3,2,1,0:T(8,128)S(1)}, f32[2,5,32,128]{3,2,1,0:T(8,128)S(1)}, u32[]{:S(2)}, u32[]{:S(2)}) collective-permute-start(f32[2,5,32,128]{3,2,1,0:T(8,128)S(1)} %get-tuple-element.53), channel_id=1, source_target_pairs={{0,1},{1,2},{2,3},{3,4},{4,5},{5,6},{6,7},{7,0},{8,9},{9,10},{10,1... | collective-permute-start | bytes 491528 | tf_op jit(solution)/shard_map/ppermute | solution.py:651
  16.3 6.7 %collective-permute-start.5 = (f32[2,5,32,128]{3,2,1,0:T(8,128)S(1)}, f32[2,5,32,128]{3,2,1,0:T(8,128)S(1)}, u32[]{:S(2)}, u32[]{:S(2)}) collective-permute-start(f32[2,5,32,128]{3,2,1,0:T(8,128)S(1)} %get-tuple-element.55), channel_id=1, source_target_pairs={{0,7},{1,0},{2,1},{3,2},{4,3},{5,4},{6,5},{7,6},{8,15},{9,8},{10,9... | collective-permute-start | bytes 491528 | tf_op jit(solution)/shard_map/ppermute | solution.py:651
  23.0 11.9 %collective-permute-start.6 = (f32[174,8,128]{2,1,0:T(8,128)S(1)}, f32[174,8,128]{2,1,0:T(8,128)S(1)}, u32[]{:S(2)}, u32[]{:S(2)}) collective-permute-start(f32[174,8,128]{2,1,0:T(8,128)S(1)} %get-tuple-element.56), channel_id=1, source_target_pairs={{0,8},{8,16},{16,24},{24,32},{32,40},{40,48},{48,56},{56,0},{1,9},... | collective-permute-start | bytes 2138120 | tf_op jit(solution)/shard_map/ppermute | solution.py:651
  26.7 10.6 %collective-permute-start.7 = (f32[174,8,128]{2,1,0:T(8,128)S(1)}, f32[174,8,128]{2,1,0:T(8,128)S(1)}, u32[]{:S(2)}, u32[]{:S(2)}) collective-permute-start(f32[174,8,128]{2,1,0:T(8,128)S(1)} %get-tuple-element.57), channel_id=1, source_target_pairs={{0,56},{8,0},{16,8},{24,16},{32,24},{40,32},{48,40},{56,48},{1,57}... | collective-permute-start | bytes 2138120 | tf_op jit(solution)/shard_map/ppermute | solution.py:651
  59.7 5.8 %collective-permute-start.9 = (f32[32,16,128]{2,1,0:T(8,128)S(1)}, f32[32,16,128]{2,1,0:T(8,128)S(1)}, u32[]{:S(2)}, u32[]{:S(2)}) collective-permute-start(f32[32,16,128]{2,1,0:T(8,128)S(1)} %all_to_all.15.refs_1_), channel_id=1, source_target_pairs={{0,56},{8,16},{16,8},{24,32},{32,24},{40,48},{48,40},{56,0},{1,57}... | collective-permute-start | bytes 786440 | tf_op jit(solution)/shard_map/ppermute | solution.py:657
  61.4 4.1 %collective-permute-start.8 = (f32[32,16,128]{2,1,0:T(8,128)S(1)}, f32[32,16,128]{2,1,0:T(8,128)S(1)}, u32[]{:S(2)}, u32[]{:S(2)}) collective-permute-start(f32[32,16,128]{2,1,0:T(8,128)S(1)} %all_to_all.15.refs_1_), channel_id=1, source_target_pairs={{0,8},{8,0},{16,24},{24,16},{32,40},{40,32},{48,56},{56,48},{1,9},... | collective-permute-start | bytes 786440 | tf_op jit(solution)/shard_map/ppermute | solution.py:656
  70.5 6.3 %collective-permute-start.10 = (f32[15,32,128]{2,1,0:T(8,128)S(1)}, f32[15,32,128]{2,1,0:T(8,128)S(1)}, u32[]{:S(2)}, u32[]{:S(2)}) collective-permute-start(f32[15,32,128]{2,1,0:T(8,128)S(1)} %get-tuple-element.75), channel_id=1, source_target_pairs={{0,64},{64,128},{128,192},{192,0},{1,65},{65,129},{129,193},{193,1... | collective-permute-start | bytes 737288 | tf_op jit(solution)/shard_map/ppermute | solution.py:651
  71.0 5.8 %collective-permute-start.11 = (f32[15,32,128]{2,1,0:T(8,128)S(1)}, f32[15,32,128]{2,1,0:T(8,128)S(1)}, u32[]{:S(2)}, u32[]{:S(2)}) collective-permute-start(f32[15,32,128]{2,1,0:T(8,128)S(1)} %get-tuple-element.76), channel_id=1, source_target_pairs={{0,192},{64,0},{128,64},{192,128},{1,193},{65,1},{129,65},{193,129... | collective-permute-start | bytes 737288 | tf_op jit(solution)/shard_map/ppermute | solution.py:651
  76.9 9.3 %collective-permute-start.12 = (f32[75,8,128]{2,1,0:T(8,128)S(1)}, f32[75,8,128]{2,1,0:T(8,128)S(1)}, u32[]{:S(2)}, u32[]{:S(2)}) collective-permute-start(f32[75,8,128]{2,1,0:T(8,128)S(1)} %get-tuple-element.77), channel_id=1, source_target_pairs={{0,8},{8,16},{16,24},{24,32},{32,40},{40,48},{48,56},{56,0},{1,9},... | collective-permute-start | bytes 921608 | tf_op jit(solution)/shard_map/ppermute | solution.py:651
  82.3 6.4 %collective-permute-start.13 = (f32[75,8,128]{2,1,0:T(8,128)S(1)}, f32[75,8,128]{2,1,0:T(8,128)S(1)}, u32[]{:S(2)}, u32[]{:S(2)}) collective-permute-start(f32[75,8,128]{2,1,0:T(8,128)S(1)} %get-tuple-element.78), channel_id=1, source_target_pairs={{0,56},{8,0},{16,8},{24,16},{32,24},{40,32},{48,40},{56,48},{1,57}... | collective-permute-start | bytes 921608 | tf_op jit(solution)/shard_map/ppermute | solution.py:651
  107.3 4.4 %collective-permute-start.15 = (f32[32,8,128]{2,1,0:T(8,128)S(1)}, f32[32,8,128]{2,1,0:T(8,128)S(1)}, u32[]{:S(2)}, u32[]{:S(2)}) collective-permute-start(f32[32,8,128]{2,1,0:T(8,128)S(1)} %all_to_all.16.refs_1_), channel_id=1, source_target_pairs={{0,56},{8,16},{16,8},{24,32},{32,24},{40,48},{48,40},{56,0},{1,57}... | collective-permute-start | bytes 393224 | tf_op jit(solution)/shard_map/ppermute | solution.py:657
  108.4 4.1 %collective-permute-start.14 = (f32[32,8,128]{2,1,0:T(8,128)S(1)}, f32[32,8,128]{2,1,0:T(8,128)S(1)}, u32[]{:S(2)}, u32[]{:S(2)}) collective-permute-start(f32[32,8,128]{2,1,0:T(8,128)S(1)} %all_to_all.16.refs_1_), channel_id=1, source_target_pairs={{0,8},{8,0},{16,24},{24,16},{32,40},{40,32},{48,56},{56,48},{1,9},... | collective-permute-start | bytes 393224 | tf_op jit(solution)/shard_map/ppermute | solution.py:656
